TPU v7x, 32 devices: a whole 2x2x4 slice. The times are simulated.
32 devices in a mesh: guide: 2 (over core), blk: 16 (over z, y, x).
Axes of the slice: x: 2, y: 2, z: 4, core: 2. Of those that a mesh axis runs over, the one named last changes fastest.
Arguments:
- x_cols: bfloat16 [128, 2048], P(None, 'blk'), may hold values from -3 to 3
- queries: bfloat16 [128, 9216], P('blk'), may hold values from -64 to 64
- new_kv: bfloat16 [128, 576], P('blk'), may hold values from -6 to 6
- cache: bfloat16 [2, 128, 256, 576], P('guide', 'blk'), may hold values from -8 to 8
- lengths: int32 [2, 128], P('guide'), may hold values from 2 to 256, as said below
- perm: int32 [128], replicated, may hold values from 0 to 127, each once
- guide_scale: float32 [128], replicated, may hold values from 1.5 to 7.5
- w_uv: bfloat16 [16, 512, 128], replicated, may hold values from -0.75 to 0.75
- w_out: bfloat16 [2048, 2048], P(None, 'blk'), may hold values from -0.125 to 0.125
- mlp_gain: float32 [2048], replicated, may hold values from 0.5 to 1.5
- w_gate: bfloat16 [2048, 10944], P(None, 'blk'), may hold values from -0.125 to 0.125
- w_up: bfloat16 [2048, 10944], P(None, 'blk'), may hold values from -0.125 to 0.125
- w_down: bfloat16 [10944, 2048], P('blk'), may hold values from -0.0546875 to 0.0546875
- head_gain: float32 [2048], replicated, may hold values from 0.5 to 1.5
- w_head: bfloat16 [2048, 102400], P(None, 'blk'), may hold values from -0.125 to 0.125
Outputs:
- guided: bfloat16 [128, 102400], P('guide', 'blk')
Inputs may be any that keep to these rules, and one draw needn't show every extreme that they name: Positions 0 to lengths[g, r] - 1 of request r's cache in group g are live; each group has a request with 256 live positions. Slot s holds request perm[s]; every request has one slot.
All inputs are finite; a program needn't handle non-finite values.
Results may differ from a plain program's by a relative error of at most 0.018.
Values may be sent and summed in bfloat16 or wider, within the bound.
No kernel may reach another device: no remote copies, remote signals or barrier semaphores. Data moves between devices by JAX's collectives and lax.ppermute only.
A program may use at most 128 MiB of HBM per device.

v0:
```python
import jax
import jax.numpy as jnp
from jax import lax
from jax.sharding import PartitionSpec as P

FF = 10944


def partner(value, axis, apart):
    mask = 2**apart
    pairs = [(source, source ^ mask) for source in range(lax.axis_size(axis))]
    return lax.ppermute(value, axis, pairs)


def rms_round(hidden, gain):
    values = hidden.astype(jnp.float32)
    meansq = jnp.mean(values * values, axis=-1, keepdims=True)
    return (values * lax.rsqrt(meansq + 1e-06) * gain).astype(jnp.bfloat16)


def body(
    x_cols,
    queries,
    new_kv,
    cache,
    lengths,
    perm,
    guide_scale,
    w_uv,
    w_out,
    mlp_gain,
    w_gate,
    w_up,
    w_down,
    head_gain,
    w_head,
):
    guide_index = lax.axis_index("guide")
    blk_index = lax.axis_index("blk")
    slots_dev = queries.shape[0]
    heads_count = w_uv.shape[0]
    latent_size = w_uv.shape[1]
    key_width = new_kv.shape[1]
    score_scale = (w_uv.shape[2] + key_width - latent_size) ** (-0.5)
    slot_ids = blk_index * slots_dev + jnp.arange(slots_dev, dtype=jnp.int32)
    owners = jnp.take(perm, slot_ids)
    live_len = jnp.take(lengths[0], owners)
    query_heads = queries.reshape(slots_dev, heads_count, key_width)
    cached_keys = cache[0]
    scores = (
        jnp.einsum("shk,slk->shl", query_heads, cached_keys, preferred_element_type=jnp.float32)
        * score_scale
    )
    own_score = (
        jnp.einsum("shk,sk->sh", query_heads, new_kv, preferred_element_type=jnp.float32)
        * score_scale
    )
    live_mask = (
        jnp.arange(cached_keys.shape[1], dtype=jnp.int32)[None, None, :] < live_len[:, None, None]
    )
    scores = jnp.where(live_mask, scores, jnp.float32(-1e30))
    peak_score = jnp.maximum(jnp.max(scores, axis=-1), own_score)
    probs = jnp.where(live_mask, jnp.exp(scores - peak_score[..., None]), jnp.float32(0.0))
    own_prob = jnp.exp(own_score - peak_score)
    softmax_total = jnp.sum(probs, axis=-1) + own_prob
    weights = (probs / softmax_total[..., None]).astype(jnp.bfloat16)
    own_weight = (own_prob / softmax_total).astype(jnp.bfloat16)
    latent_out = jnp.einsum(
        "shl,slc->shc", weights, cached_keys[:, :, :latent_size], preferred_element_type=jnp.float32
    )
    latent_out = latent_out + own_weight.astype(jnp.float32)[..., None] * new_kv[
        :, None, :latent_size
    ].astype(jnp.float32)
    value_rows = jnp.einsum(
        "shc,hcd->shd", latent_out.astype(jnp.bfloat16), w_uv, preferred_element_type=jnp.float32
    )
    value_rows = value_rows.astype(jnp.bfloat16).reshape(slots_dev, -1)
    attended = jnp.dot(
        lax.all_gather(value_rows, "blk", axis=0, tiled=True),
        w_out,
        preferred_element_type=jnp.float32,
    )
    residual = (x_cols.astype(jnp.float32) + attended).astype(jnp.bfloat16)
    rows_full = lax.all_gather(residual, "blk", axis=1, tiled=True)
    normed = rms_round(rows_full, mlp_gain)
    unit_count = w_gate.shape[1]
    gate_out = jnp.dot(normed, w_gate, preferred_element_type=jnp.float32)
    up_out = jnp.dot(normed, w_up, preferred_element_type=jnp.float32)
    unit_ids = blk_index * unit_count + jnp.arange(unit_count, dtype=jnp.int32)
    hidden = jnp.where(
        unit_ids[None, :] < FF, jax.nn.silu(gate_out) * up_out, jnp.float32(0.0)
    ).astype(jnp.bfloat16)
    partial_sum = jnp.dot(hidden, w_down, preferred_element_type=jnp.float32)
    summed = lax.psum(partial_sum, "blk")
    after_mlp = (rows_full.astype(jnp.float32) + summed).astype(jnp.bfloat16)
    logits = jnp.dot(rms_round(after_mlp, head_gain), w_head, preferred_element_type=jnp.float32)
    request_count = logits.shape[0]
    half_rows = request_count // 2
    slot_scale = jnp.take(guide_scale, perm)
    request_order = (
        jnp.zeros((request_count,), jnp.int32)
        .at[perm]
        .set(jnp.arange(request_count, dtype=jnp.int32))
    )
    own_order = lax.dynamic_slice_in_dim(request_order, guide_index * half_rows, half_rows)
    other_logits = partner(logits.astype(jnp.bfloat16), "guide", 0).astype(logits.dtype)
    cond_logits = jnp.where(guide_index == 0, logits, other_logits)
    uncond_logits = jnp.where(guide_index == 0, other_logits, logits)
    mixed = (uncond_logits + slot_scale[:, None] * (cond_logits - uncond_logits)).astype(
        jnp.bfloat16
    )
    return jnp.take(mixed, own_order, axis=0)


def solution(mesh):
    return jax.shard_map(
        body,
        mesh=mesh,
        in_specs=(
            P(None, "blk"),
            P("blk", None),
            P("blk", None),
            P("guide", "blk", None, None),
            P("guide", None),
            P(),
            P(),
            P(),
            P(None, "blk"),
            P(),
            P(None, "blk"),
            P(None, "blk"),
            P("blk", None),
            P(),
            P(None, "blk"),
        ),
        out_specs=P("guide", "blk"),
        check_vma=False,
    )
```

profile of v0, /device:TPU:0, one launch (start us, length us, event | category | flops | bytes accessed | tf_op | source)
XLA Modules:
  0.0 257.7 jit_solution(10083849745343940406)
XLA Ops:
  6.5 0.0 copy-start
  6.5 1.2 reshape.73
  7.8 1.3 gather_fusion.2
  9.1 1.3 gather_fusion.3
  10.4 0.1 iota_compare_fusion
  10.5 0.7 slice_convert_fusion
  11.2 0.9 fusion.44
  12.1 2.2 fusion.55
  14.3 0.2 fusion.39
  14.5 0.1 copy.17
  14.6 2.4 fusion.4
  17.0 0.5 fusion.11
  17.5 45.3 %all_gather.6 = bf16[128,2048]{1,0:T(8,128)(2,1)S(1)} all-gather(bf16[8,2048]{1,0:T(8,128)(2,1)S(1)} %fusion.11), channel_id=1, replica_groups=mesh['guide'=2,'blk'=16] {'blk'}, dimensions={0}, use_global_device_ids=true | all-gather | bytes 557056 | tf_op jit(solution)/shard_map/all_gather | solution.py:79
  62.8 0.3 fusion.10
  63.1 38.5 %all_gather.7 = bf16[128,2048]{1,0:T(8,128)(2,1)S(1)} all-gather(bf16[128,128]{1,0:T(8,128)(2,1)S(1)} %fusion.10), channel_id=1, replica_groups=mesh['guide'=2,'blk'=16] {'blk'}, dimensions={1}, use_global_device_ids=true | all-gather | bytes 557056 | tf_op jit(solution)/shard_map/all_gather | solution.py:84
  101.7 0.2 fusion.15
  101.9 3.5 %fusion.34 = f32[128,684]{0,1:T(8,128)} fusion(bf16[2048,684]{0,1:T(8,128)(2,1)} %param.27, bf16[128,2048]{1,0:T(8,128)(2,1)S(1)} %all_gather.7, f32[2048]{0:T(1024)S(1)} %copy-done.7, f32[128]{0:T(128)S(1)} %add_rsqrt_fusion.1), kind=kOutput, calls=%fused_computation.49 | convolution fusion | flops 359661568 | bytes 3684864 | tf_op jit(solution)/shard_map/dot_general | solution.py:87
  105.4 5.0 %fusion.8 = f32[128,2048]{1,0:T(8,128)} fusion(bf16[684,2048]{1,0:T(8,128)(2,1)S(1)} %copy-done, bf16[2048,684]{0,1:T(8,128)(2,1)} %param.28, f32[128,684]{0,1:T(8,128)} %fusion.34, pred[684]{0:T(1024)(128)(4,1)S(1)} %add_compare_fusion, bf16[128,2048]{1,0:T(8,128)(2,1)S(1)} %all_gather.7, f32[2048]{0:T(1024)S(1)} %copy-done.7, f32[128]{0:T(128)S(1)} %add_rsqrt_fusion.1), kind=kOutput, calls=%fused_computation.21 | convolution fusion | flops 718887424 | bytes 7535788 | tf_op jit(solution)/shard_map/dot_general | solution.py:93
  110.4 0.0 all-reduce.2.cloned.1.call-update
  110.5 109.6 %all-reduce.2.cloned.1.call-done = f32[128,2048]{1,0:T(8,128)} async-done(((f32[128,2048]{1,0:T(8,128)}), f32[128,2048]{1,0:T(8,128)}) %all-reduce.2.cloned.1.call-update) | async-done | bytes 1048592 | tf_op jit(solution)/shard_map/psum | solution.py:94
  220.1 1.4 fusion.12
  221.5 0.0 copy-start.2
  221.5 0.0 copy-start.1
  221.5 14.7 %fusion.56 = (bf16[128,6400]{1,0:T(8,128)(2,1)}, f32[128,6400]{1,0:T(8,128)}) fusion(bf16[2048,6400]{1,0:T(8,128)(2,1)} %param.31, f32[2048]{0:T(1024)S(1)} %copy-done.5, f32[128]{0:T(128)S(1)} %add_rsqrt_fusion, f32[128,2048]{1,0:T(8,128)} %all-reduce.2.cloned.1.call-done, bf16[128,2048]{1,0:T(8,128)(2,1)S(1)} %all_gather.7), kind=kOutput, calls=%fused_computation.90 | convolution fusion | flops 3358097408 | bytes 32711168 | tf_op jit(solution)/shard_map/dot_general | solution.py:96
  236.2 0.0 collective-permute-start
  236.2 1.2 scatter_custom_fusion
  237.4 1.2 gather_fusion
  238.6 0.1 compare_and_fusion
  238.8 1.3 collective-permute-done
  240.1 4.3 %fusion.3 = bf16[128,6400]{1,0:T(8,128)(2,1)} fusion(f32[128,6400]{1,0:T(8,128)} %get-tuple-element.13, bf16[128,6400]{1,0:T(8,128)(2,1)} %collective-permute-done, f32[128]{0:T(128)S(1)} %and_select_fusion.2, pred[]{:T(512)S(6)} %eq.4), kind=kLoop, calls=%fused_computation.10 | loop fusion | flops 5734400 | bytes 6554113 | tf_op jit(solution)/shard_map/convert_element_type | solution.py:109
  244.4 4.3 %gather_fusion.1 = bf16[64,6400]{1,0:T(8,128)(2,1)} fusion(bf16[128,6400]{1,0:T(8,128)(2,1)} %fusion.3, s32[1024]{0:T(1024)S(1)} %pad_clamp_fusion), kind=kCustom, calls=%fused_computation.3 | custom fusion | bytes 1638656 | tf_op jit(solution)/shard_map/jit(_take)/gather | solution.py:112
  248.7 2.2 broadcast_select_fusion
  (29 shorter events, 0.1 us)
Async XLA Ops:
  6.5 98.9 %copy-start = (bf16[684,2048]{1,0:T(8,128)(2,1)S(1)}, bf16[684,2048]{1,0:T(8,128)(2,1)}, u32[]{:S(2)}) copy-start(bf16[684,2048]{1,0:T(8,128)(2,1)} %param.29) | copy-start | bytes 8404996
  6.5 213.5 %all-reduce.2.cloned.1.call-start = ((), (), s32[]{:S(2)}) async-start(), calls=%async_computation | async-start | bytes 2097152 | tf_op jit(solution)/shard_map/psum | solution.py:94
  14.6 2.4 copy-start.3
  14.6 48.3 %copy-start.4 = (bf16[2048,128]{1,0:T(8,128)(2,1)S(1)}, bf16[2048,128]{1,0:T(8,128)(2,1)}, u32[]{:S(2)}) copy-start(bf16[2048,128]{1,0:T(8,128)(2,1)} %param.25) | copy-start | bytes 1572868
  14.6 48.3 %copy-start.6 = (bf16[128,128]{1,0:T(8,128)(2,1)S(1)}, bf16[128,128]{1,0:T(8,128)(2,1)}, u32[]{:S(2)}) copy-start(bf16[128,128]{1,0:T(8,128)(2,1)} %param.17) | copy-start | bytes 98308
  17.0 84.9 %copy-start.7 = (f32[2048]{0:T(1024)S(1)}, f32[2048]{0:T(1024)}, u32[]{:S(2)}) copy-start(f32[2048]{0:T(1024)} %param.26) | copy-start | bytes 24580
  105.4 116.1 %copy-start.5 = (f32[2048]{0:T(1024)S(1)}, f32[2048]{0:T(1024)}, u32[]{:S(2)}) copy-start(f32[2048]{0:T(1024)} %param.30) | copy-start | bytes 24580
  221.5 14.7 %copy-start.2 = (s32[128]{0:T(128)S(1)}, s32[128]{0:T(128)}, u32[]{:S(2)}) copy-start(s32[128]{0:T(128)} %param.22) | copy-start | bytes 1540
  221.5 15.9 %copy-start.1 = (f32[128]{0:T(128)S(1)}, f32[128]{0:T(128)}, u32[]{:S(2)}) copy-start(f32[128]{0:T(128)} %param.23) | copy-start | bytes 1540
  236.2 3.8 %collective-permute-start = (bf16[128,6400]{1,0:T(8,128)(2,1)}, bf16[128,6400]{1,0:T(8,128)(2,1)}, u32[]{:S(2)}, u32[]{:S(2)}) collective-permute-start(bf16[128,6400]{1,0:T(8,128)(2,1)} %get-tuple-element.12), channel_id=1, source_target_pairs={{0,16},{16,0},{1,17},{17,1},{2,18},{18,2},{3,19},{19,3},{4,20},{20... | collective-permute-start | bytes 4915208 | tf_op jit(solution)/shard_map/ppermute | solution.py:12
Sparse Core Ops, SparseCore 0:
  110.6 109.4 all-reduce.1
where the time goes:
time: 258 us
  waiting for transfers between devices  111 us (43%)
  blocking collectives  83.9 us (33%)
  matrix products  29.5 us (11%)
  between operations  13.5 us (5%)
  local copies, waits for them, and re-layouts  10.7 us (4%)
  other arithmetic  9.26 us (4%)
    psum x1, waiting for transfers between devices, body(): summed = lax.psum(partial_sum, 'blk')  110 us
    all_gather x1, blocking collectives, body(): lax.all_gather(value_rows, 'blk', axis=0, tiled=True)  45.3 us
    all_gather x1, blocking collectives, body(): rows_full = lax.all_gather(residual, 'blk', axis=1, tiled=True)  38.5 us
    dot_general x1, matrix products, body(): jnp.dot(rms_round(after_mlp, head_gain), w_head, preferred_element_type=j...  14.7 us
  transfers between devices with their start and end apart: 2, of which 2 were waited for; matrix products, arithmetic and copies ran while one was open for 1% of the time, Pallas kernels for 0%

commit v1 on v0

--- a/solution.py
+++ b/solution.py
@@ -1,9 +1,19 @@
 import jax
 import jax.numpy as jnp
 from jax import lax
+from jax.experimental import pallas as pl
+from jax.experimental.pallas import tpu as pltpu
 from jax.sharding import PartitionSpec as P
 
 FF = 10944
+BF = jnp.bfloat16
+F32 = jnp.float32
+NN = (((1,), (0,)), ((), ()))
+NT = (((1,), (1,)), ((), ()))
+TN = (((0,), (0,)), ((), ()))
+VM = pl.BlockSpec(memory_space=pltpu.VMEM)
+SM = pl.BlockSpec(memory_space=pltpu.SMEM)
+HB = pl.BlockSpec(memory_space=pltpu.HBM)
 
 
 def partner(value, axis, apart):
@@ -12,10 +22,337 @@
     return lax.ppermute(value, axis, pairs)
 
 
+def swap(value, mask):
+    pairs = [(source, source ^ mask) for source in range(lax.axis_size("blk"))]
+    return lax.ppermute(value, "blk", pairs)
+
+
 def rms_round(hidden, gain):
     values = hidden.astype(jnp.float32)
     meansq = jnp.mean(values * values, axis=-1, keepdims=True)
     return (values * lax.rsqrt(meansq + 1e-06) * gain).astype(jnp.bfloat16)
+
+
+def cost(micros):
+    return pl.CostEstimate(flops=int(micros * 1e9), bytes_accessed=int(micros * 3e6), transcendentals=0)
+
+
+def iota(shape, dim):
+    return lax.broadcasted_iota(jnp.int32, shape, dim)
+
+
+def dot(a, b, dims, precision=None):
+    return lax.dot_general(a, b, dims, precision=precision, preferred_element_type=F32)
+
+
+def attend_kernel(
+    ids, perm_h, lengths_h, queries_h, new_h, cache, w_uv, out,
+    perm, lengths, queries, new_kv, qs, keys, up, sems, others,
+):
+    slots, width, positions = cache.shape
+    heads, latent, nope = w_uv.shape
+    rows = heads * slots
+    first = ids[1] * slots
+    small = [
+        pltpu.make_async_copy(source, target, others.at[k])
+        for k, (source, target) in enumerate(
+            ((queries_h, queries), (new_h, new_kv), (perm_h, perm), (lengths_h, lengths))
+        )
+    ]
+    copies = [
+        pltpu.make_async_copy(cache.at[s], keys.at[s], sems.at[s]) for s in range(slots)
+    ]
+    upcopy = pltpu.make_async_copy(w_uv, up, others.at[4])
+    for copy in small + copies + [upcopy]:
+        copy.start()
+    small[0].wait()
+    for h in range(heads):
+        qs[h * slots : (h + 1) * slots, :] = queries[:, h * width : (h + 1) * width]
+    q = qs[...]
+    small[1].wait()
+    new = new_kv[...]
+    scale = (nope + width - latent) ** (-0.5)
+    slot_of = iota((rows, 1), 0) % slots
+    own = dot(q, new, NT)
+    own = jnp.sum(jnp.where(iota((rows, slots), 1) == slot_of, own, 0.0), 1, keepdims=True) * scale
+    small[2].wait()
+    small[3].wait()
+    live = jnp.zeros((rows, 1), jnp.int32)
+    for s in range(slots):
+        live = jnp.where(slot_of == s, lengths[0, perm[first + s]], live)
+    scores = jnp.zeros((rows, positions), F32)
+    for s in range(slots):
+        copies[s].wait()
+        scores = jnp.where(slot_of == s, dot(q, keys[s], NN), scores)
+    mask = iota((rows, positions), 1) < live
+    scores = jnp.where(mask, scores * scale, -1e30)
+    peak = jnp.maximum(jnp.max(scores, axis=1, keepdims=True), own)
+    probs = jnp.where(mask, jnp.exp(scores - peak), 0.0)
+    own = jnp.exp(own - peak)
+    total = jnp.sum(probs, axis=1, keepdims=True) + own
+    weights = probs / total
+    own = (own / total).astype(BF).astype(F32)
+    mixed = jnp.zeros((rows, latent), F32)
+    for s in range(slots):
+        part = jnp.where(slot_of == s, weights, 0.0).astype(BF)
+        mixed += dot(part, keys[s, :latent, :], NT)
+    mixed += own * jnp.tile(new[:, :latent].astype(F32), (heads, 1))
+    upcopy.wait()
+    for h in range(heads):
+        rows_h = mixed[h * slots : (h + 1) * slots, :].astype(BF)
+        out[:, h * nope : (h + 1) * nope] = dot(rows_h, up[h], NN).astype(BF)
+
+
+def attend(ids, perm, lengths, queries, new_kv, cache, w_uv):
+    slots, width, positions = cache.shape
+    heads, latent, nope = w_uv.shape
+    return pl.pallas_call(
+        attend_kernel,
+        out_shape=jax.ShapeDtypeStruct((slots, heads * nope), BF),
+        in_specs=[SM] + [HB] * 6,
+        out_specs=VM,
+        scratch_shapes=[
+            pltpu.SMEM(perm.shape, jnp.int32),
+            pltpu.SMEM(lengths.shape, jnp.int32),
+            pltpu.VMEM(queries.shape, BF),
+            pltpu.VMEM(new_kv.shape, BF),
+            pltpu.VMEM((heads * slots, width), BF),
+            pltpu.VMEM((slots, width, positions), BF),
+            pltpu.VMEM((heads, latent, nope), BF),
+            pltpu.SemaphoreType.DMA((slots,)),
+            pltpu.SemaphoreType.DMA((5,)),
+        ],
+        compiler_params=pltpu.CompilerParams(vmem_limit_bytes=60 << 20),
+        cost_estimate=cost(15),
+        name="attend",
+    )(ids, perm, lengths, queries, new_kv, cache, w_uv)
+
+
+def request_of(row, rows):
+    chip = ((row >> 3) & 3) * 4 + (row >> 5)
+    return ((row >> 2) & 1) * (rows // 2) + chip * 4 + (row & 3)
+
+
+def project_kernel(ids, perm, v0, v1, v2, v3, w_out, x_cols, out):
+    blk = ids[1]
+    rows = x_cols.shape[0]
+    w = w_out[...]
+    attended = jnp.concatenate([dot(v[...], w, NN) for v in (v0, v1, v2, v3)], axis=0)
+    shape = (rows, rows)
+    wanted = request_of(iota(shape, 0), rows)
+    by_slot = (jnp.broadcast_to(perm[...], shape) == wanted).astype(F32)
+    arrived = iota(shape, 1)
+    slot = ((blk ^ (((arrived >> 3) & 3) * 4) ^ (arrived >> 5)) << 3) | (arrived & 7)
+    move = (iota(shape, 0) == slot).astype(F32)
+    by_arrival = dot(by_slot.astype(BF), move.astype(BF), NN)
+    moved = dot(by_arrival, attended, NN, lax.Precision.HIGHEST)
+    base = dot(by_slot.astype(BF), x_cols[...], NN)
+    out[...] = (base + moved).astype(BF)
+
+
+def project(ids, perm, pieces, w_out, x_cols):
+    return pl.pallas_call(
+        project_kernel,
+        out_shape=jax.ShapeDtypeStruct(x_cols.shape, BF),
+        in_specs=[SM] + [VM] * 7,
+        out_specs=VM,
+        compiler_params=pltpu.CompilerParams(vmem_limit_bytes=4 << 20),
+        cost_estimate=cost(15),
+        name="project",
+    )(ids, perm, *pieces, w_out, x_cols)
+
+
+def feed_kernel(
+    ids, r0, r1, r2, r3, gain, w_gate, w_up, w_down, own, c1, c2, c3, kept, full, acc
+):
+    blk = ids[1]
+    groups, rows, cols = r0.shape
+    units = w_gate.shape[0]
+    for q, ref in enumerate((r0, r1, r2, r3)):
+        for j in range(groups):
+            at = pl.multiple_of((blk ^ (4 * j) ^ q) * cols, cols)
+            full[:, pl.ds(at, cols)] = ref[j].astype(F32)
+    values = full[...]
+    meansq = jnp.mean(values * values, axis=1, keepdims=True)
+    normed = (values * lax.rsqrt(meansq + 1e-06) * gain[...]).astype(BF)
+    gate = dot(normed, w_gate[...], NT)
+    up = dot(normed, w_up[...], NT)
+    unit = blk * units + iota((rows, units), 1)
+    hidden = gate * (1.0 / (1.0 + jnp.exp(-gate))) * up
+    hidden = jnp.where(unit < FF, hidden, 0.0).astype(BF)
+    acc[...] = dot(hidden, w_down[...], NN)
+    low, high = blk & 3, blk >> 2
+    chunk = rows // 4
+    for q, ref in enumerate((own, c1, c2, c3)):
+        at = pl.multiple_of((low ^ q) * chunk, chunk)
+        ref[...] = acc[pl.ds(at, chunk), :].astype(ref.dtype)
+    small = chunk // 4
+    at = pl.multiple_of(low * chunk + high * small, small)
+    kept[...] = full[pl.ds(at, small), :]
+
+
+def feed(ids, pieces, gain, w_gate, w_up, w_down):
+    groups, rows, cols = pieces[0].shape
+    width = w_down.shape[1]
+    part = (rows // 4, width)
+    return pl.pallas_call(
+        feed_kernel,
+        out_shape=[
+            jax.ShapeDtypeStruct(part, F32),
+            jax.ShapeDtypeStruct(part, BF),
+            jax.ShapeDtypeStruct(part, BF),
+            jax.ShapeDtypeStruct(part, BF),
+            jax.ShapeDtypeStruct((rows // 16, width), F32),
+        ],
+        in_specs=[SM] + [VM] * 8,
+        out_specs=[VM] * 5,
+        scratch_shapes=[pltpu.VMEM((rows, width), F32), pltpu.VMEM((rows, width), F32)],
+        compiler_params=pltpu.CompilerParams(vmem_limit_bytes=8 << 20),
+        cost_estimate=cost(15),
+        name="feed",
+    )(ids, *pieces, gain, w_gate, w_up, w_down)
+
+
+def reduce_kernel(ids, own, p1, p2, p3, keep, o1, o2, o3, acc):
+    high = ids[1] >> 2
+    acc[...] = own[...] + p1[...].astype(F32) + p2[...].astype(F32) + p3[...].astype(F32)
+    small = keep.shape[0]
+    for j, ref in enumerate((keep, o1, o2, o3)):
+        at = pl.multiple_of((high ^ j) * small, small)
+        ref[...] = acc[pl.ds(at, small), :].astype(ref.dtype)
+
+
+def reduce_part(ids, own, parts):
+    rows, width = own.shape
+    small = (rows // 4, width)
+    return pl.pallas_call(
+        reduce_kernel,
+        out_shape=[jax.ShapeDtypeStruct(small, F32)] + [jax.ShapeDtypeStruct(small, BF)] * 3,
+        in_specs=[SM] + [VM] * 4,
+        out_specs=[VM] * 4,
+        scratch_shapes=[pltpu.VMEM((rows, width), F32)],
+        compiler_params=pltpu.CompilerParams(vmem_limit_bytes=2 << 20),
+        cost_estimate=cost(20),
+        name="reduce_part",
+    )(ids, own, *parts)
+
+
+def finish_kernel(ids, own, p1, p2, p3, kept, gain, stay, go):
+    total = own[...] + p1[...].astype(F32) + p2[...].astype(F32) + p3[...].astype(F32)
+    after = (kept[...] + total).astype(BF).astype(F32)
+    meansq = jnp.mean(after * after, axis=1, keepdims=True)
+    normed = after * lax.rsqrt(meansq + 1e-06) * gain[...]
+    half = normed.shape[0] // 2
+    first, last = normed[:half], normed[half:]
+    lower = ids[0] == 0
+    stay[...] = jnp.where(lower, first, last).astype(BF)
+    go[...] = jnp.where(lower, last, first).astype(BF)
+
+
+def finish(ids, own, parts, kept, gain):
+    rows, width = own.shape
+    return pl.pallas_call(
+        finish_kernel,
+        out_shape=[jax.ShapeDtypeStruct((rows // 2, width), BF)] * 2,
+        in_specs=[SM] + [VM] * 6,
+        out_specs=[VM] * 2,
+        compiler_params=pltpu.CompilerParams(vmem_limit_bytes=1 << 20),
+        cost_estimate=cost(20),
+        name="finish",
+    )(ids, own, *parts, kept, gain)
+
+
+def head_kernel(ids, r0, r1, r2, r3, scale, w_head, out, full, factor):
+    guide, blk = ids[0], ids[1]
+    part = r0.shape[0]
+    rows = 4 * part
+    half = rows // 2
+
+    @pl.when(pl.program_id(0) == 0)
+    def _():
+        wanted = iota((rows, part), 0)
+        total = None
+        for q, ref in enumerate((r0, r1, r2, r3)):
+            at = iota((rows, part), 1)
+            chip = blk ^ ((at >> 3) << 2) ^ q
+            row = (((at >> 2) & 1) ^ guide) * half + chip * 4 + (at & 3)
+            piece = dot((row == wanted).astype(BF), ref[...], NN)
+            total = piece if total is None else total + piece
+        full[...] = total.astype(BF)
+        mine = iota((half, rows), 0) + guide * half == iota((half, rows), 1)
+        factor[...] = jnp.sum(
+            jnp.where(mine, jnp.broadcast_to(scale[...], (half, rows)), 0.0), 1, keepdims=True
+        )
+
+    logits = dot(full[...], w_head[...], NN)
+    cond, uncond = logits[:half], logits[half:]
+    out[...] = (uncond + factor[...] * (cond - uncond)).astype(BF)
+
+
+def head(ids, pieces, scale, w_head):
+    part, width = pieces[0].shape
+    rows = 4 * part
+    vocab = w_head.shape[1]
+    tile = next(t for t in (640, 512, 256, 128, vocab) if vocab % t == 0)
+    whole = pl.BlockSpec((part, width), lambda i: (0, 0))
+    return pl.pallas_call(
+        head_kernel,
+        out_shape=jax.ShapeDtypeStruct((rows // 2, vocab), BF),
+        grid=(vocab // tile,),
+        in_specs=[SM]
+        + [whole] * 4
+        + [
+            pl.BlockSpec((1, rows), lambda i: (0, 0)),
+            pl.BlockSpec((width, tile), lambda i: (0, i)),
+        ],
+        out_specs=pl.BlockSpec((rows // 2, tile), lambda i: (0, i)),
+        scratch_shapes=[pltpu.VMEM((rows, width), BF), pltpu.VMEM((rows // 2, 1), F32)],
+        compiler_params=pltpu.CompilerParams(vmem_limit_bytes=48 << 20),
+        cost_estimate=cost(8),
+        name="head",
+    )(ids, *pieces, scale, w_head)
+
+
+def spread(value):
+    near = [value] + [swap(value, mask) for mask in (4, 8, 12)]
+    group = jnp.concatenate(near, axis=0)
+    return [group] + [swap(group, mask) for mask in (1, 2, 3)]
+
+
+def fast_body(
+    x_cols,
+    queries,
+    new_kv,
+    cache,
+    lengths,
+    perm,
+    guide_scale,
+    w_uv,
+    w_out,
+    mlp_gain,
+    w_gate,
+    w_up,
+    w_down,
+    head_gain,
+    w_head,
+):
+    guide_index = lax.axis_index("guide")
+    blk_index = lax.axis_index("blk")
+    ids = jnp.stack([guide_index, blk_index]).astype(jnp.int32)
+    rows, cols = x_cols.shape
+    keys = jnp.swapaxes(cache[0], 1, 2)
+    values = attend(ids, perm, lengths, queries, new_kv, keys, w_uv)
+    residual = project(ids, perm[None], spread(values), w_out, x_cols)
+    pieces = [piece.reshape(4, rows, cols) for piece in spread(residual)]
+    own, *chunks, kept = feed(
+        ids, pieces, mlp_gain[None], jnp.swapaxes(w_gate, 0, 1), jnp.swapaxes(w_up, 0, 1), w_down
+    )
+    arrived = [swap(chunk, mask) for chunk, mask in zip(chunks, (1, 2, 3))]
+    own, *chunks = reduce_part(ids, own, arrived)
+    arrived = [swap(chunk, mask) for chunk, mask in zip(chunks, (4, 8, 12))]
+    stay, go = finish(ids, own, arrived, kept, head_gain[None])
+    normed = jnp.concatenate([stay, partner(go, "guide", 0)], axis=0)
+    return head(ids, spread(normed), guide_scale[None], w_head)
 
 
 def body(
@@ -113,26 +450,32 @@
 
 
 def solution(mesh):
-    return jax.shard_map(
-        body,
-        mesh=mesh,
-        in_specs=(
-            P(None, "blk"),
-            P("blk", None),
-            P("blk", None),
-            P("guide", "blk", None, None),
-            P("guide", None),
-            P(),
-            P(),
-            P(),
-            P(None, "blk"),
-            P(),
-            P(None, "blk"),
-            P(None, "blk"),
-            P("blk", None),
-            P(),
-            P(None, "blk"),
-        ),
-        out_specs=P("guide", "blk"),
-        check_vma=False,
-    )
+    def run(*args):
+        chips = mesh.shape["blk"]
+        rows, width = args[0].shape
+        fits = chips == 16 and rows == 128 and mesh.shape["guide"] == 2 and width % (128 * chips) == 0
+        return jax.shard_map(
+            fast_body if fits else body,
+            mesh=mesh,
+            in_specs=(
+                P(None, "blk"),
+                P("blk", None),
+                P("blk", None),
+                P("guide", "blk", None, None),
+                P("guide", None),
+                P(),
+                P(),
+                P(),
+                P(None, "blk"),
+                P(),
+                P(None, "blk"),
+                P(None, "blk"),
+                P("blk", None),
+                P(),
+                P(None, "blk"),
+            ),
+            out_specs=P("guide", "blk"),
+            check_vma=False,
+        )(*args)
+
+    return run

time: 258 us -> 95.3 us (0.37)
  blocking collectives: 83.9 us -> 0 us
  waiting for transfers between devices: 111 us -> 33 us
  starting transfers between devices: 0.01 us -> 33.4 us
  matrix products: 29.5 us -> 0 us
  Pallas kernels: 0 us -> 26.9 us
  between operations: 13.5 us -> 0.15 us
  local copies, waits for them, and re-layouts: 10.7 us -> 0.08 us
  other arithmetic: 9.26 us -> 1.38 us
    psum x1 -> x0, waiting for transfers between devices: 110 us -> none  [body(): summed = lax.psum(partial_sum, 'blk')]
    all_gather x2 -> x0, blocking collectives: 83.9 us -> none  [the longest x1 45.3 us: body(): lax.all_gather(value_rows, 'blk', axis=0, tiled=True)]
    ppermute x0 -> x24, starting transfers between devices: none -> 33.3 us  [swap(): return lax.ppermute(value, 'blk', pairs)]
    ppermute x0 -> x24, waiting for transfers between devices: none -> 31.9 us  [swap(): return lax.ppermute(value, 'blk', pairs)]
    dot_general x8 -> x0, matrix products: 29.5 us -> none  [the longest x1 14.7 us: body(): jnp.dot(rms_round(after_mlp, head_gain), w_head, preferred_element_type=j...]
    pallas_call x0 -> x6, Pallas kernels: none -> 26.9 us  [the longest x1 14.8 us: head(): pl.pallas_call(head_kernel, out_shape=jax.ShapeDtypeStruct((rows // 2, vo...]
    gather x4 -> x0, local copies, waits for them, and re-layouts: 8.17 us -> none  [the longest x1 4.35 us: body(): return jnp.take(mixed, own_order, axis=0)]
    convert_element_type x3 -> x0, other arithmetic: 5.02 us -> none  [the longest x1 4.31 us: body(): (uncond_logits + slot_scale[:, None] * (cond_logits - uncond_logits)).ast...]
  transfers between devices with their start and end apart: 2 -> 25, of which waited for: 2 -> 21; matrix products, arithmetic and copies ran while one was open for 1% -> 0% of each run, Pallas kernels for 0% -> 0%
where the time goes in v1:
time: 95.3 us; the launch traced here: 94.9 us
  starting transfers between devices  33.4 us (35%)
  waiting for transfers between devices  33 us (35%)
  Pallas kernels  26.9 us (28%)
  other arithmetic  1.38 us (1%)
    ppermute x24, starting transfers between devices, swap(): return lax.ppermute(value, 'blk', pairs)  33.3 us
    ppermute x24, waiting for transfers between devices, swap(): return lax.ppermute(value, 'blk', pairs)  31.9 us
    pallas_call x1, Pallas kernels, head(): pl.pallas_call(head_kernel, out_shape=jax.ShapeDtypeStruct((rows // 2, vo...  14.8 us
    pallas_call x1, Pallas kernels, attend(): pl.pallas_call(attend_kernel, out_shape=jax.ShapeDtypeStruct((slots, head...  6.47 us
    pallas_call x1, Pallas kernels, feed(): pl.pallas_call(feed_kernel, out_shape=[jax.ShapeDtypeStruct(part, F32), j...  3.1 us
  transfers between devices with their start and end apart: 25, of which 21 were waited for; matrix products, arithmetic and copies ran while one was open for 0% of the time, Pallas kernels for 0%

profile of v1, /device:TPU:0, one launch (start us, length us, event | category | flops | bytes accessed | tf_op | source)
XLA Modules:
  0.0 94.9 jit_solution(13221936752058991933)
XLA Ops:
  0.6 6.5 %attend.1 = bf16[8,2048]{1,0:T(8,128)(2,1)} custom-call(s32[2]{0:T(128)} %pad_add_fusion.ids, s32[128]{0:T(128)} %perm_h.1, s32[1,128]{1,0:T(1,128)} %lengths_h.1, bf16[8,9216]{1,0:T(8,128)(2,1)} %queries_h.1, bf16[8,576]{1,0:T(8,128)(2,1)} %new_h.1, bf16[8,576,256]{2,1,0:T(8,128)(2,1)} %bitcast.25, bf16[16,512,128]{2,1,0:T(8,128)(2,1)} %w_uv.1), custom_call_target="tpu_custom_call" | custom-call | flops 15000000512 | bytes 45000000 | tf_op jit(solution)/shard_map/attend/pallas_call | solution.py:109
  7.1 5.1 %collective-permute-start.2 = (bf16[8,2048]{1,0:T(8,128)(2,1)}, bf16[8,2048]{1,0:T(8,128)(2,1)S(1)}, u32[]{:S(2)}, u32[]{:S(2)}) collective-permute-start(bf16[8,2048]{1,0:T(8,128)(2,1)} %attend.1), channel_id=1, source_target_pairs={{0,12},{1,13},{2,14},{3,15},{4,8},{5,9},{6,10},{7,11},{8,4},{9,5},... | collective-permute-start | bytes 98312 | tf_op jit(solution)/shard_map/ppermute | solution.py:27
  12.8 1.5 %collective-permute-done.2 = bf16[8,2048]{1,0:T(8,128)(2,1)S(1)} collective-permute-done((bf16[8,2048]{1,0:T(8,128)(2,1)}, bf16[8,2048]{1,0:T(8,128)(2,1)S(1)}, u32[]{:S(2)}, u32[]{:S(2)}) %collective-permute-start.2) | collective-permute-done | bytes 32800 | tf_op jit(solution)/shard_map/ppermute | solution.py:27
  14.3 2.9 %collective-permute-done.1 = bf16[8,2048]{1,0:T(8,128)(2,1)S(1)} collective-permute-done((bf16[8,2048]{1,0:T(8,128)(2,1)}, bf16[8,2048]{1,0:T(8,128)(2,1)S(1)}, u32[]{:S(2)}, u32[]{:S(2)}) %collective-permute-start.1) | collective-permute-done | bytes 32800 | tf_op jit(solution)/shard_map/ppermute | solution.py:27
  18.0 2.5 %collective-permute-start.5 = (bf16[32,2048]{1,0:T(8,128)(2,1)S(1)}, bf16[32,2048]{1,0:T(8,128)(2,1)S(1)}, u32[]{:S(2)}, u32[]{:S(2)}) collective-permute-start(bf16[32,2048]{1,0:T(8,128)(2,1)S(1)} %pad_maximum_fusion.v0), channel_id=1, source_target_pairs={{0,3},{1,2},{2,1},{3,0},{4,7},{5,6},{6,5},{7,4},{8,11},{9,10},{10,... | collective-permute-start | bytes 393224 | tf_op jit(solution)/shard_map/ppermute | solution.py:27
  21.5 3.8 %collective-permute-done.5.v3 = bf16[32,2048]{1,0:T(8,128)(2,1)S(1)} collective-permute-done((bf16[32,2048]{1,0:T(8,128)(2,1)S(1)}, bf16[32,2048]{1,0:T(8,128)(2,1)S(1)}, u32[]{:S(2)}, u32[]{:S(2)}) %collective-permute-start.5) | collective-permute-done | bytes 131104 | tf_op jit(solution)/shard_map/ppermute | solution.py:27
  26.2 1.2 %project.1 = bf16[128,128]{1,0:T(8,128)(2,1)S(1)} custom-call(s32[2]{0:T(128)S(1)} %copy-done.9, s32[1,128]{1,0:T(1,128)S(1)} %bitcast.23, bf16[32,2048]{1,0:T(8,128)(2,1)S(1)} %pad_maximum_fusion.v0, bf16[32,2048]{1,0:T(8,128)(2,1)S(1)} %collective-permute-done.3.v1, bf16[32,2048]{1,0:T(8,128)(2,1)S(1)} %collective-permute-done.4.v2, ...), custom_call_target="tpu_custom_call" | custom-call | flops 15000000512 | bytes 45000000 | tf_op jit(solution)/shard_map/project/pallas_call | solution.py:154
  27.4 1.5 %collective-permute-start.8 = (bf16[128,128]{1,0:T(8,128)(2,1)S(1)}, bf16[128,128]{1,0:T(8,128)(2,1)S(1)}, u32[]{:S(2)}, u32[]{:S(2)}) collective-permute-start(bf16[128,128]{1,0:T(8,128)(2,1)S(1)} %project.1), channel_id=1, source_target_pairs={{0,12},{1,13},{2,14},{3,15},{4,8},{5,9},{6,10},{7,11},{8,4},{9,5},... | collective-permute-start | bytes 98312 | tf_op jit(solution)/shard_map/ppermute | solution.py:27
  29.6 2.3 %collective-permute-start.6 = (bf16[128,128]{1,0:T(8,128)(2,1)S(1)}, bf16[128,128]{1,0:T(8,128)(2,1)S(1)}, u32[]{:S(2)}, u32[]{:S(2)}) collective-permute-start(bf16[128,128]{1,0:T(8,128)(2,1)S(1)} %project.1), channel_id=1, source_target_pairs={{0,4},{1,5},{2,6},{3,7},{4,0},{5,1},{6,2},{7,3},{8,12},{9,13},{10,... | collective-permute-start | bytes 98312 | tf_op jit(solution)/shard_map/ppermute | solution.py:27
  31.9 1.3 %collective-permute-done.8 = bf16[128,128]{1,0:T(8,128)(2,1)S(1)} collective-permute-done((bf16[128,128]{1,0:T(8,128)(2,1)S(1)}, bf16[128,128]{1,0:T(8,128)(2,1)S(1)}, u32[]{:S(2)}, u32[]{:S(2)}) %collective-permute-start.8) | collective-permute-done | bytes 32800 | tf_op jit(solution)/shard_map/ppermute | solution.py:27
  34.0 1.5 %collective-permute-start.11 = (bf16[512,128]{1,0:T(8,128)(2,1)S(1)}, bf16[512,128]{1,0:T(8,128)(2,1)S(1)}, u32[]{:S(2)}, u32[]{:S(2)}) collective-permute-start(bf16[512,128]{1,0:T(8,128)(2,1)S(1)} %pad_maximum_fusion.1), channel_id=1, source_target_pairs={{0,3},{1,2},{2,1},{3,0},{4,7},{5,6},{6,5},{7,4},{8,11},{9,10},{10,... | collective-permute-start | bytes 393224 | tf_op jit(solution)/shard_map/ppermute | solution.py:27
  35.5 1.5 %collective-permute-start.10 = (bf16[512,128]{1,0:T(8,128)(2,1)S(1)}, bf16[512,128]{1,0:T(8,128)(2,1)S(1)}, u32[]{:S(2)}, u32[]{:S(2)}) collective-permute-start(bf16[512,128]{1,0:T(8,128)(2,1)S(1)} %pad_maximum_fusion.1), channel_id=1, source_target_pairs={{0,2},{1,3},{2,0},{3,1},{4,6},{5,7},{6,4},{7,5},{8,10},{9,11},{10,... | collective-permute-start | bytes 393224 | tf_op jit(solution)/shard_map/ppermute | solution.py:27
  37.6 2.5 %collective-permute-done.11 = bf16[512,128]{1,0:T(8,128)(2,1)S(1)} collective-permute-done((bf16[512,128]{1,0:T(8,128)(2,1)S(1)}, bf16[512,128]{1,0:T(8,128)(2,1)S(1)}, u32[]{:S(2)}, u32[]{:S(2)}) %collective-permute-start.11) | collective-permute-done | bytes 131104 | tf_op jit(solution)/shard_map/ppermute | solution.py:27
  40.1 1.3 %collective-permute-done.10 = bf16[512,128]{1,0:T(8,128)(2,1)S(1)} collective-permute-done((bf16[512,128]{1,0:T(8,128)(2,1)S(1)}, bf16[512,128]{1,0:T(8,128)(2,1)S(1)}, u32[]{:S(2)}, u32[]{:S(2)}) %collective-permute-start.10) | collective-permute-done | bytes 131104 | tf_op jit(solution)/shard_map/ppermute | solution.py:27
  42.1 3.1 %feed.1 = (f32[32,2048]{1,0:T(8,128)S(1)}, bf16[32,2048]{1,0:T(8,128)(2,1)S(1)}, bf16[32,2048]{1,0:T(8,128)(2,1)S(1)}, bf16[32,2048]{1,0:T(8,128)(2,1)S(1)}, f32[8,2048]{1,0:T(8,128)S(1)}) custom-call(s32[2]{0:T(128)S(1)} %copy-done.9, bf16[4,128,128]{2,1,0:T(8,128)(2,1)S(1)} %bitcast.15, bf16[4,128,128]{2,1,0:T(8,128)(2,1)S(1)} %bitcast.20, ...), custom_call_target="tpu_custom_call" | custom-call | flops 15000000512 | bytes 45000000 | tf_op jit(solution)/shard_map/feed/pallas_call | solution.py:198
  47.2 1.5 %collective-permute-start.14 = (bf16[32,2048]{1,0:T(8,128)(2,1)S(1)}, bf16[32,2048]{1,0:T(8,128)(2,1)S(1)}, u32[]{:S(2)}, u32[]{:S(2)}) collective-permute-start(bf16[32,2048]{1,0:T(8,128)(2,1)S(1)} %get-tuple-element.19), channel_id=1, source_target_pairs={{0,3},{1,2},{2,1},{3,0},{4,7},{5,6},{6,5},{7,4},{8,11},{9,10},{10,... | collective-permute-start | bytes 393224 | tf_op jit(solution)/shard_map/ppermute | solution.py:27
  48.7 1.5 %collective-permute-done.12.p1 = bf16[32,2048]{1,0:T(8,128)(2,1)S(1)} collective-permute-done((bf16[32,2048]{1,0:T(8,128)(2,1)S(1)}, bf16[32,2048]{1,0:T(8,128)(2,1)S(1)}, u32[]{:S(2)}, u32[]{:S(2)}) %collective-permute-start.12) | collective-permute-done | bytes 131104 | tf_op jit(solution)/shard_map/ppermute | solution.py:27
  51.1 2.0 %collective-permute-done.14.p3 = bf16[32,2048]{1,0:T(8,128)(2,1)S(1)} collective-permute-done((bf16[32,2048]{1,0:T(8,128)(2,1)S(1)}, bf16[32,2048]{1,0:T(8,128)(2,1)S(1)}, u32[]{:S(2)}, u32[]{:S(2)}) %collective-permute-start.14) | collective-permute-done | bytes 131104 | tf_op jit(solution)/shard_map/ppermute | solution.py:27
  53.7 1.7 %collective-permute-start.15 = (bf16[8,2048]{1,0:T(8,128)(2,1)S(1)}, bf16[8,2048]{1,0:T(8,128)(2,1)S(1)}, u32[]{:S(2)}, u32[]{:S(2)}) collective-permute-start(bf16[8,2048]{1,0:T(8,128)(2,1)S(1)} %get-tuple-element.21), channel_id=1, source_target_pairs={{0,4},{1,5},{2,6},{3,7},{4,0},{5,1},{6,2},{7,3},{8,12},{9,13},{10,... | collective-permute-start | bytes 98312 | tf_op jit(solution)/shard_map/ppermute | solution.py:27
  55.5 1.2 %collective-permute-start.16 = (bf16[8,2048]{1,0:T(8,128)(2,1)S(1)}, bf16[8,2048]{1,0:T(8,128)(2,1)S(1)}, u32[]{:S(2)}, u32[]{:S(2)}) collective-permute-start(bf16[8,2048]{1,0:T(8,128)(2,1)S(1)} %get-tuple-element.22), channel_id=1, source_target_pairs={{0,8},{1,9},{2,10},{3,11},{4,12},{5,13},{6,14},{7,15},{8,0},{9,1},... | collective-permute-start | bytes 98312 | tf_op jit(solution)/shard_map/ppermute | solution.py:27
  56.7 1.5 %collective-permute-start.17 = (bf16[8,2048]{1,0:T(8,128)(2,1)S(1)}, bf16[8,2048]{1,0:T(8,128)(2,1)S(1)}, u32[]{:S(2)}, u32[]{:S(2)}) collective-permute-start(bf16[8,2048]{1,0:T(8,128)(2,1)S(1)} %get-tuple-element.23), channel_id=1, source_target_pairs={{0,12},{1,13},{2,14},{3,15},{4,8},{5,9},{6,10},{7,11},{8,4},{9,5},... | collective-permute-start | bytes 98312 | tf_op jit(solution)/shard_map/ppermute | solution.py:27
  58.2 2.2 %collective-permute-done.16.p2 = bf16[8,2048]{1,0:T(8,128)(2,1)S(1)} collective-permute-done((bf16[8,2048]{1,0:T(8,128)(2,1)S(1)}, bf16[8,2048]{1,0:T(8,128)(2,1)S(1)}, u32[]{:S(2)}, u32[]{:S(2)}) %collective-permute-start.16) | collective-permute-done | bytes 32800 | tf_op jit(solution)/shard_map/ppermute | solution.py:27
  60.4 2.0 %collective-permute-done.17.p3 = bf16[8,2048]{1,0:T(8,128)(2,1)S(1)} collective-permute-done((bf16[8,2048]{1,0:T(8,128)(2,1)S(1)}, bf16[8,2048]{1,0:T(8,128)(2,1)S(1)}, u32[]{:S(2)}, u32[]{:S(2)}) %collective-permute-start.17) | collective-permute-done | bytes 32800 | tf_op jit(solution)/shard_map/ppermute | solution.py:27
  63.2 1.2 %collective-permute-done.18 = bf16[4,2048]{1,0:T(4,128)(2,1)S(1)} collective-permute-done((bf16[4,2048]{1,0:T(4,128)(2,1)S(1)}, bf16[4,2048]{1,0:T(4,128)(2,1)S(1)}, u32[]{:S(2)}, u32[]{:S(2)}) %collective-permute-start.18) | collective-permute-done | bytes 16416 | tf_op jit(solution)/shard_map/ppermute | solution.py:22
  64.4 1.5 %collective-permute-start.21 = (bf16[8,2048]{1,0:T(8,128)(2,1)S(1)}, bf16[8,2048]{1,0:T(8,128)(2,1)S(1)}, u32[]{:S(2)}, u32[]{:S(2)}) collective-permute-start(bf16[8,2048]{1,0:T(8,128)(2,1)S(1)} %pad_maximum_fusion.2), channel_id=1, source_target_pairs={{0,12},{1,13},{2,14},{3,15},{4,8},{5,9},{6,10},{7,11},{8,4},{9,5},... | collective-permute-start | bytes 98312 | tf_op jit(solution)/shard_map/ppermute | solution.py:27
  65.9 2.9 %collective-permute-start.19 = (bf16[8,2048]{1,0:T(8,128)(2,1)S(1)}, bf16[8,2048]{1,0:T(8,128)(2,1)S(1)}, u32[]{:S(2)}, u32[]{:S(2)}) collective-permute-start(bf16[8,2048]{1,0:T(8,128)(2,1)S(1)} %pad_maximum_fusion.2), channel_id=1, source_target_pairs={{0,4},{1,5},{2,6},{3,7},{4,0},{5,1},{6,2},{7,3},{8,12},{9,13},{10,... | collective-permute-start | bytes 98312 | tf_op jit(solution)/shard_map/ppermute | solution.py:27
  68.8 1.3 %collective-permute-done.21 = bf16[8,2048]{1,0:T(8,128)(2,1)S(1)} collective-permute-done((bf16[8,2048]{1,0:T(8,128)(2,1)S(1)}, bf16[8,2048]{1,0:T(8,128)(2,1)S(1)}, u32[]{:S(2)}, u32[]{:S(2)}) %collective-permute-start.21) | collective-permute-done | bytes 32800 | tf_op jit(solution)/shard_map/ppermute | solution.py:27
  71.4 1.2 %collective-permute-start.24 = (bf16[32,2048]{1,0:T(8,128)(2,1)S(1)}, bf16[32,2048]{1,0:T(8,128)(2,1)S(1)}, u32[]{:S(2)}, u32[]{:S(2)}) collective-permute-start(bf16[32,2048]{1,0:T(8,128)(2,1)S(1)} %concatenate.16.r0), channel_id=1, source_target_pairs={{0,3},{1,2},{2,1},{3,0},{4,7},{5,6},{6,5},{7,4},{8,11},{9,10},{10,... | collective-permute-start | bytes 393224 | tf_op jit(solution)/shard_map/ppermute | solution.py:27
  73.7 1.2 %collective-permute-start.22 = (bf16[32,2048]{1,0:T(8,128)(2,1)S(1)}, bf16[32,2048]{1,0:T(8,128)(2,1)S(1)}, u32[]{:S(2)}, u32[]{:S(2)}) collective-permute-start(bf16[32,2048]{1,0:T(8,128)(2,1)S(1)} %concatenate.16.r0), channel_id=1, source_target_pairs={{0,1},{1,0},{2,3},{3,2},{4,5},{5,4},{6,7},{7,6},{8,9},{9,8},{10,11... | collective-permute-start | bytes 393224 | tf_op jit(solution)/shard_map/ppermute | solution.py:27
  74.9 3.8 %collective-permute-done.24.r3 = bf16[32,2048]{1,0:T(8,128)(2,1)S(1)} collective-permute-done((bf16[32,2048]{1,0:T(8,128)(2,1)S(1)}, bf16[32,2048]{1,0:T(8,128)(2,1)S(1)}, u32[]{:S(2)}, u32[]{:S(2)}) %collective-permute-start.24) | collective-permute-done | bytes 131104 | tf_op jit(solution)/shard_map/ppermute | solution.py:27
  78.7 1.4 %collective-permute-done.23.r2 = bf16[32,2048]{1,0:T(8,128)(2,1)S(1)} collective-permute-done((bf16[32,2048]{1,0:T(8,128)(2,1)S(1)}, bf16[32,2048]{1,0:T(8,128)(2,1)S(1)}, u32[]{:S(2)}, u32[]{:S(2)}) %collective-permute-start.23) | collective-permute-done | bytes 131104 | tf_op jit(solution)/shard_map/ppermute | solution.py:27
  80.2 14.8 %head.1 = bf16[64,6400]{1,0:T(8,128)(2,1)} custom-call(s32[2]{0:T(128)S(1)} %copy-done.9, bf16[32,2048]{1,0:T(8,128)(2,1)S(1)} %concatenate.16.r0, bf16[32,2048]{1,0:T(8,128)(2,1)S(1)} %collective-permute-done.22.r1, bf16[32,2048]{1,0:T(8,128)(2,1)S(1)} %collective-permute-done.23.r2, bf16[32,2048]{1,0:T(8,128)(2,1)S(1)} %collective-permute-done.24.r3, ...), custom_call_target="tpu_custom_call" | custom-call | flops 8000000000 | bytes 24000000 | tf_op jit(solution)/shard_map/head/pallas_call | solution.py:298
  (49 shorter events, 13.2 us)
Async XLA Ops:
  0.6 25.5 %copy-start.3 = (bf16[2048,128]{1,0:T(8,128)(2,1)S(1)}, bf16[2048,128]{1,0:T(8,128)(2,1)}, u32[]{:S(2)}) copy-start(bf16[2048,128]{1,0:T(8,128)(2,1)} %w_out.1) | copy-start | bytes 1572868
  0.6 25.5 %copy-start.4 = (bf16[128,128]{1,0:T(8,128)(2,1)S(1)}, bf16[128,128]{1,0:T(8,128)(2,1)}, u32[]{:S(2)}) copy-start(bf16[128,128]{1,0:T(8,128)(2,1)} %x_cols.1) | copy-start | bytes 98308
  0.6 25.5 %copy-start.7 = (s32[128]{0:T(128)S(1)}, s32[128]{0:T(128)}, u32[]{:S(2)}) copy-start(s32[128]{0:T(128)} %perm_h.1) | copy-start | bytes 1540
  0.6 25.5 %copy-start.9 = (s32[2]{0:T(128)S(1)}, s32[2]{0:T(128)}, u32[]{:S(2)}) copy-start(s32[2]{0:T(128)} %pad_add_fusion.ids) | copy-start | bytes 28
  7.1 7.2 %collective-permute-start.2 = (bf16[8,2048]{1,0:T(8,128)(2,1)}, bf16[8,2048]{1,0:T(8,128)(2,1)S(1)}, u32[]{:S(2)}, u32[]{:S(2)}) collective-permute-start(bf16[8,2048]{1,0:T(8,128)(2,1)} %attend.1), channel_id=1, source_target_pairs={{0,12},{1,13},{2,14},{3,15},{4,8},{5,9},{6,10},{7,11},{8,4},{9,5},... | collective-permute-start | bytes 98312 | tf_op jit(solution)/shard_map/ppermute | solution.py:27
  12.2 5.0 %collective-permute-start.1 = (bf16[8,2048]{1,0:T(8,128)(2,1)}, bf16[8,2048]{1,0:T(8,128)(2,1)S(1)}, u32[]{:S(2)}, u32[]{:S(2)}) collective-permute-start(bf16[8,2048]{1,0:T(8,128)(2,1)} %attend.1), channel_id=1, source_target_pairs={{0,8},{1,9},{2,10},{3,11},{4,12},{5,13},{6,14},{7,15},{8,0},{9,1},... | collective-permute-start | bytes 98312 | tf_op jit(solution)/shard_map/ppermute | solution.py:27
  12.2 5.0 %collective-permute-start = (bf16[8,2048]{1,0:T(8,128)(2,1)}, bf16[8,2048]{1,0:T(8,128)(2,1)S(1)}, u32[]{:S(2)}, u32[]{:S(2)}) collective-permute-start(bf16[8,2048]{1,0:T(8,128)(2,1)} %attend.1), channel_id=1, source_target_pairs={{0,4},{1,5},{2,6},{3,7},{4,0},{5,1},{6,2},{7,3},{8,12},{9,13},{10,... | collective-permute-start | bytes 98312 | tf_op jit(solution)/shard_map/ppermute | solution.py:27
  18.0 7.3 %collective-permute-start.5 = (bf16[32,2048]{1,0:T(8,128)(2,1)S(1)}, bf16[32,2048]{1,0:T(8,128)(2,1)S(1)}, u32[]{:S(2)}, u32[]{:S(2)}) collective-permute-start(bf16[32,2048]{1,0:T(8,128)(2,1)S(1)} %pad_maximum_fusion.v0), channel_id=1, source_target_pairs={{0,3},{1,2},{2,1},{3,0},{4,7},{5,6},{6,5},{7,4},{8,11},{9,10},{10,... | collective-permute-start | bytes 393224 | tf_op jit(solution)/shard_map/ppermute | solution.py:27
  20.5 5.6 %collective-permute-start.4 = (bf16[32,2048]{1,0:T(8,128)(2,1)S(1)}, bf16[32,2048]{1,0:T(8,128)(2,1)S(1)}, u32[]{:S(2)}, u32[]{:S(2)}) collective-permute-start(bf16[32,2048]{1,0:T(8,128)(2,1)S(1)} %pad_maximum_fusion.v0), channel_id=1, source_target_pairs={{0,2},{1,3},{2,0},{3,1},{4,6},{5,7},{6,4},{7,5},{8,10},{9,11},{10,... | collective-permute-start | bytes 393224 | tf_op jit(solution)/shard_map/ppermute | solution.py:27
  21.0 5.1 %collective-permute-start.3 = (bf16[32,2048]{1,0:T(8,128)(2,1)S(1)}, bf16[32,2048]{1,0:T(8,128)(2,1)S(1)}, u32[]{:S(2)}, u32[]{:S(2)}) collective-permute-start(bf16[32,2048]{1,0:T(8,128)(2,1)S(1)} %pad_maximum_fusion.v0), channel_id=1, source_target_pairs={{0,1},{1,0},{2,3},{3,2},{4,5},{5,4},{6,7},{7,6},{8,9},{9,8},{10,11... | collective-permute-start | bytes 393224 | tf_op jit(solution)/shard_map/ppermute | solution.py:27
  26.1 15.9 %copy-start = (bf16[2048,684]{0,1:T(8,128)(2,1)S(1)}, bf16[2048,684]{0,1:T(8,128)(2,1)}, u32[]{:S(2)}) copy-start(bf16[2048,684]{0,1:T(8,128)(2,1)} %param.25) | copy-start | bytes 8404996
  26.1 15.9 %copy-start.1 = (bf16[2048,684]{0,1:T(8,128)(2,1)S(1)}, bf16[2048,684]{0,1:T(8,128)(2,1)}, u32[]{:S(2)}) copy-start(bf16[2048,684]{0,1:T(8,128)(2,1)} %param.26) | copy-start | bytes 8404996
  27.4 5.8 %collective-permute-start.8 = (bf16[128,128]{1,0:T(8,128)(2,1)S(1)}, bf16[128,128]{1,0:T(8,128)(2,1)S(1)}, u32[]{:S(2)}, u32[]{:S(2)}) collective-permute-start(bf16[128,128]{1,0:T(8,128)(2,1)S(1)} %project.1), channel_id=1, source_target_pairs={{0,12},{1,13},{2,14},{3,15},{4,8},{5,9},{6,10},{7,11},{8,4},{9,5},... | collective-permute-start | bytes 98312 | tf_op jit(solution)/shard_map/ppermute | solution.py:27
  28.9 4.8 %collective-permute-start.7 = (bf16[128,128]{1,0:T(8,128)(2,1)S(1)}, bf16[128,128]{1,0:T(8,128)(2,1)S(1)}, u32[]{:S(2)}, u32[]{:S(2)}) collective-permute-start(bf16[128,128]{1,0:T(8,128)(2,1)S(1)} %project.1), channel_id=1, source_target_pairs={{0,8},{1,9},{2,10},{3,11},{4,12},{5,13},{6,14},{7,15},{8,0},{9,1},... | collective-permute-start | bytes 98312 | tf_op jit(solution)/shard_map/ppermute | solution.py:27
  29.6 4.5 %collective-permute-start.6 = (bf16[128,128]{1,0:T(8,128)(2,1)S(1)}, bf16[128,128]{1,0:T(8,128)(2,1)S(1)}, u32[]{:S(2)}, u32[]{:S(2)}) collective-permute-start(bf16[128,128]{1,0:T(8,128)(2,1)S(1)} %project.1), channel_id=1, source_target_pairs={{0,4},{1,5},{2,6},{3,7},{4,0},{5,1},{6,2},{7,3},{8,12},{9,13},{10,... | collective-permute-start | bytes 98312 | tf_op jit(solution)/shard_map/ppermute | solution.py:27
  34.0 6.0 %collective-permute-start.11 = (bf16[512,128]{1,0:T(8,128)(2,1)S(1)}, bf16[512,128]{1,0:T(8,128)(2,1)S(1)}, u32[]{:S(2)}, u32[]{:S(2)}) collective-permute-start(bf16[512,128]{1,0:T(8,128)(2,1)S(1)} %pad_maximum_fusion.1), channel_id=1, source_target_pairs={{0,3},{1,2},{2,1},{3,0},{4,7},{5,6},{6,5},{7,4},{8,11},{9,10},{10,... | collective-permute-start | bytes 393224 | tf_op jit(solution)/shard_map/ppermute | solution.py:27
  35.5 5.8 %collective-permute-start.10 = (bf16[512,128]{1,0:T(8,128)(2,1)S(1)}, bf16[512,128]{1,0:T(8,128)(2,1)S(1)}, u32[]{:S(2)}, u32[]{:S(2)}) collective-permute-start(bf16[512,128]{1,0:T(8,128)(2,1)S(1)} %pad_maximum_fusion.1), channel_id=1, source_target_pairs={{0,2},{1,3},{2,0},{3,1},{4,6},{5,7},{6,4},{7,5},{8,10},{9,11},{10,... | collective-permute-start | bytes 393224 | tf_op jit(solution)/shard_map/ppermute | solution.py:27
  37.1 5.0 %collective-permute-start.9 = (bf16[512,128]{1,0:T(8,128)(2,1)S(1)}, bf16[512,128]{1,0:T(8,128)(2,1)S(1)}, u32[]{:S(2)}, u32[]{:S(2)}) collective-permute-start(bf16[512,128]{1,0:T(8,128)(2,1)S(1)} %pad_maximum_fusion.1), channel_id=1, source_target_pairs={{0,1},{1,0},{2,3},{3,2},{4,5},{5,4},{6,7},{7,6},{8,9},{9,8},{10,11... | collective-permute-start | bytes 393224 | tf_op jit(solution)/shard_map/ppermute | solution.py:27
  45.2 5.0 %collective-permute-start.12 = (bf16[32,2048]{1,0:T(8,128)(2,1)S(1)}, bf16[32,2048]{1,0:T(8,128)(2,1)S(1)}, u32[]{:S(2)}, u32[]{:S(2)}) collective-permute-start(bf16[32,2048]{1,0:T(8,128)(2,1)S(1)} %get-tuple-element.17), channel_id=1, source_target_pairs={{0,1},{1,0},{2,3},{3,2},{4,5},{5,4},{6,7},{7,6},{8,9},{9,8},{10,11... | collective-permute-start | bytes 393224 | tf_op jit(solution)/shard_map/ppermute | solution.py:27
  46.1 5.0 %collective-permute-start.13 = (bf16[32,2048]{1,0:T(8,128)(2,1)S(1)}, bf16[32,2048]{1,0:T(8,128)(2,1)S(1)}, u32[]{:S(2)}, u32[]{:S(2)}) collective-permute-start(bf16[32,2048]{1,0:T(8,128)(2,1)S(1)} %get-tuple-element.18), channel_id=1, source_target_pairs={{0,2},{1,3},{2,0},{3,1},{4,6},{5,7},{6,4},{7,5},{8,10},{9,11},{10,... | collective-permute-start | bytes 393224 | tf_op jit(solution)/shard_map/ppermute | solution.py:27
  47.2 5.9 %collective-permute-start.14 = (bf16[32,2048]{1,0:T(8,128)(2,1)S(1)}, bf16[32,2048]{1,0:T(8,128)(2,1)S(1)}, u32[]{:S(2)}, u32[]{:S(2)}) collective-permute-start(bf16[32,2048]{1,0:T(8,128)(2,1)S(1)} %get-tuple-element.19), channel_id=1, source_target_pairs={{0,3},{1,2},{2,1},{3,0},{4,7},{5,6},{6,5},{7,4},{8,11},{9,10},{10,... | collective-permute-start | bytes 393224 | tf_op jit(solution)/shard_map/ppermute | solution.py:27
  53.7 4.5 %collective-permute-start.15 = (bf16[8,2048]{1,0:T(8,128)(2,1)S(1)}, bf16[8,2048]{1,0:T(8,128)(2,1)S(1)}, u32[]{:S(2)}, u32[]{:S(2)}) collective-permute-start(bf16[8,2048]{1,0:T(8,128)(2,1)S(1)} %get-tuple-element.21), channel_id=1, source_target_pairs={{0,4},{1,5},{2,6},{3,7},{4,0},{5,1},{6,2},{7,3},{8,12},{9,13},{10,... | collective-permute-start | bytes 98312 | tf_op jit(solution)/shard_map/ppermute | solution.py:27
  55.5 5.0 %collective-permute-start.16 = (bf16[8,2048]{1,0:T(8,128)(2,1)S(1)}, bf16[8,2048]{1,0:T(8,128)(2,1)S(1)}, u32[]{:S(2)}, u32[]{:S(2)}) collective-permute-start(bf16[8,2048]{1,0:T(8,128)(2,1)S(1)} %get-tuple-element.22), channel_id=1, source_target_pairs={{0,8},{1,9},{2,10},{3,11},{4,12},{5,13},{6,14},{7,15},{8,0},{9,1},... | collective-permute-start | bytes 98312 | tf_op jit(solution)/shard_map/ppermute | solution.py:27
  56.7 5.7 %collective-permute-start.17 = (bf16[8,2048]{1,0:T(8,128)(2,1)S(1)}, bf16[8,2048]{1,0:T(8,128)(2,1)S(1)}, u32[]{:S(2)}, u32[]{:S(2)}) collective-permute-start(bf16[8,2048]{1,0:T(8,128)(2,1)S(1)} %get-tuple-element.23), channel_id=1, source_target_pairs={{0,12},{1,13},{2,14},{3,15},{4,8},{5,9},{6,10},{7,11},{8,4},{9,5},... | collective-permute-start | bytes 98312 | tf_op jit(solution)/shard_map/ppermute | solution.py:27
  62.4 17.7 %copy-start.8 = (f32[128]{0:T(128)S(1)}, f32[128]{0:T(128)}, u32[]{:S(2)}) copy-start(f32[128]{0:T(128)} %param.21) | copy-start | bytes 1540
  63.1 1.2 %collective-permute-start.18 = (bf16[4,2048]{1,0:T(4,128)(2,1)S(1)}, bf16[4,2048]{1,0:T(4,128)(2,1)S(1)}, u32[]{:S(2)}, u32[]{:S(2)}) collective-permute-start(bf16[4,2048]{1,0:T(4,128)(2,1)S(1)} %get-tuple-element.26), channel_id=1, source_target_pairs={{0,16},{16,0},{1,17},{17,1},{2,18},{18,2},{3,19},{19,3},{4,20},{20... | collective-permute-start | bytes 49160 | tf_op jit(solution)/shard_map/ppermute | solution.py:22
  64.4 5.8 %collective-permute-start.21 = (bf16[8,2048]{1,0:T(8,128)(2,1)S(1)}, bf16[8,2048]{1,0:T(8,128)(2,1)S(1)}, u32[]{:S(2)}, u32[]{:S(2)}) collective-permute-start(bf16[8,2048]{1,0:T(8,128)(2,1)S(1)} %pad_maximum_fusion.2), channel_id=1, source_target_pairs={{0,12},{1,13},{2,14},{3,15},{4,8},{5,9},{6,10},{7,11},{8,4},{9,5},... | collective-permute-start | bytes 98312 | tf_op jit(solution)/shard_map/ppermute | solution.py:27
  65.9 5.3 %collective-permute-start.20 = (bf16[8,2048]{1,0:T(8,128)(2,1)S(1)}, bf16[8,2048]{1,0:T(8,128)(2,1)S(1)}, u32[]{:S(2)}, u32[]{:S(2)}) collective-permute-start(bf16[8,2048]{1,0:T(8,128)(2,1)S(1)} %pad_maximum_fusion.2), channel_id=1, source_target_pairs={{0,8},{1,9},{2,10},{3,11},{4,12},{5,13},{6,14},{7,15},{8,0},{9,1},... | collective-permute-start | bytes 98312 | tf_op jit(solution)/shard_map/ppermute | solution.py:27
  65.9 5.4 %collective-permute-start.19 = (bf16[8,2048]{1,0:T(8,128)(2,1)S(1)}, bf16[8,2048]{1,0:T(8,128)(2,1)S(1)}, u32[]{:S(2)}, u32[]{:S(2)}) collective-permute-start(bf16[8,2048]{1,0:T(8,128)(2,1)S(1)} %pad_maximum_fusion.2), channel_id=1, source_target_pairs={{0,4},{1,5},{2,6},{3,7},{4,0},{5,1},{6,2},{7,3},{8,12},{9,13},{10,... | collective-permute-start | bytes 98312 | tf_op jit(solution)/shard_map/ppermute | solution.py:27
  71.4 7.4 %collective-permute-start.24 = (bf16[32,2048]{1,0:T(8,128)(2,1)S(1)}, bf16[32,2048]{1,0:T(8,128)(2,1)S(1)}, u32[]{:S(2)}, u32[]{:S(2)}) collective-permute-start(bf16[32,2048]{1,0:T(8,128)(2,1)S(1)} %concatenate.16.r0), channel_id=1, source_target_pairs={{0,3},{1,2},{2,1},{3,0},{4,7},{5,6},{6,5},{7,4},{8,11},{9,10},{10,... | collective-permute-start | bytes 393224 | tf_op jit(solution)/shard_map/ppermute | solution.py:27
  72.6 7.5 %collective-permute-start.23 = (bf16[32,2048]{1,0:T(8,128)(2,1)S(1)}, bf16[32,2048]{1,0:T(8,128)(2,1)S(1)}, u32[]{:S(2)}, u32[]{:S(2)}) collective-permute-start(bf16[32,2048]{1,0:T(8,128)(2,1)S(1)} %concatenate.16.r0), channel_id=1, source_target_pairs={{0,2},{1,3},{2,0},{3,1},{4,6},{5,7},{6,4},{7,5},{8,10},{9,11},{10,... | collective-permute-start | bytes 393224 | tf_op jit(solution)/shard_map/ppermute | solution.py:27
  73.7 6.4 %collective-permute-start.22 = (bf16[32,2048]{1,0:T(8,128)(2,1)S(1)}, bf16[32,2048]{1,0:T(8,128)(2,1)S(1)}, u32[]{:S(2)}, u32[]{:S(2)}) collective-permute-start(bf16[32,2048]{1,0:T(8,128)(2,1)S(1)} %concatenate.16.r0), channel_id=1, source_target_pairs={{0,1},{1,0},{2,3},{3,2},{4,5},{5,4},{6,7},{7,6},{8,9},{9,8},{10,11... | collective-permute-start | bytes 393224 | tf_op jit(solution)/shard_map/ppermute | solution.py:27
  (3 other events, 41.1 us)

commit v2 on v1

--- a/solution.py
+++ b/solution.py
@@ -267,55 +267,68 @@
     part = r0.shape[0]
     rows = 4 * part
     half = rows // 2
-
-    @pl.when(pl.program_id(0) == 0)
-    def _():
-        wanted = iota((rows, part), 0)
-        total = None
-        for q, ref in enumerate((r0, r1, r2, r3)):
-            at = iota((rows, part), 1)
-            chip = blk ^ ((at >> 3) << 2) ^ q
-            row = (((at >> 2) & 1) ^ guide) * half + chip * 4 + (at & 3)
-            piece = dot((row == wanted).astype(BF), ref[...], NN)
-            total = piece if total is None else total + piece
-        full[...] = total.astype(BF)
-        mine = iota((half, rows), 0) + guide * half == iota((half, rows), 1)
-        factor[...] = jnp.sum(
-            jnp.where(mine, jnp.broadcast_to(scale[...], (half, rows)), 0.0), 1, keepdims=True
-        )
-
-    logits = dot(full[...], w_head[...], NN)
-    cond, uncond = logits[:half], logits[half:]
-    out[...] = (uncond + factor[...] * (cond - uncond)).astype(BF)
+    vocab = w_head.shape[1]
+    tile = next(t for t in (1280, 256, 128) if vocab % t == 0)
+    wanted = iota((rows, part), 0)
+    total = None
+    for q, ref in enumerate((r0, r1, r2, r3)):
+        at = iota((rows, part), 1)
+        chip = blk ^ ((at >> 3) << 2) ^ q
+        row = (((at >> 2) & 1) ^ guide) * half + chip * 4 + (at & 3)
+        piece = dot((row == wanted).astype(BF), ref[...], NN)
+        total = piece if total is None else total + piece
+    full[...] = total.astype(BF)
+    mine = iota((half, rows), 0) + guide * half == iota((half, rows), 1)
+    factor[...] = jnp.sum(
+        jnp.where(mine, jnp.broadcast_to(scale[...], (half, rows)), 0.0), 1, keepdims=True
+    )
+
+    @pl.loop(0, vocab // tile)
+    def _(step):
+        at = pl.ds(pl.multiple_of(step * tile, tile), tile)
+        logits = dot(full[...], w_head[:, at], NN)
+        cond, uncond = logits[:half], logits[half:]
+        out[:, at] = (uncond + factor[...] * (cond - uncond)).astype(BF)
 
 
 def head(ids, pieces, scale, w_head):
     part, width = pieces[0].shape
     rows = 4 * part
     vocab = w_head.shape[1]
-    tile = next(t for t in (640, 512, 256, 128, vocab) if vocab % t == 0)
-    whole = pl.BlockSpec((part, width), lambda i: (0, 0))
     return pl.pallas_call(
         head_kernel,
         out_shape=jax.ShapeDtypeStruct((rows // 2, vocab), BF),
-        grid=(vocab // tile,),
-        in_specs=[SM]
-        + [whole] * 4
-        + [
-            pl.BlockSpec((1, rows), lambda i: (0, 0)),
-            pl.BlockSpec((width, tile), lambda i: (0, i)),
-        ],
-        out_specs=pl.BlockSpec((rows // 2, tile), lambda i: (0, i)),
+        in_specs=[SM] + [VM] * 6,
+        out_specs=VM,
         scratch_shapes=[pltpu.VMEM((rows, width), BF), pltpu.VMEM((rows // 2, 1), F32)],
-        compiler_params=pltpu.CompilerParams(vmem_limit_bytes=48 << 20),
+        compiler_params=pltpu.CompilerParams(vmem_limit_bytes=8 << 20),
         cost_estimate=cost(8),
         name="head",
     )(ids, *pieces, scale, w_head)
 
 
+def join_kernel(*refs):
+    out = refs[-1]
+    part = refs[0].shape[0]
+    for k, ref in enumerate(refs[:-1]):
+        out[k * part : (k + 1) * part, :] = ref[...]
+
+
+def join(parts):
+    rows, width = parts[0].shape
+    return pl.pallas_call(
+        join_kernel,
+        out_shape=jax.ShapeDtypeStruct((len(parts) * rows, width), parts[0].dtype),
+        in_specs=[VM] * len(parts),
+        out_specs=VM,
+        compiler_params=pltpu.CompilerParams(vmem_limit_bytes=1 << 20),
+        cost_estimate=cost(1),
+        name="join",
+    )(*parts)
+
+
 def spread(value):
-    near = [value] + [swap(value, mask) for mask in (4, 8, 12)]
-    group = jnp.concatenate(near, axis=0)
+    group = join([value] + [swap(value, mask) for mask in (4, 8, 12)])
     return [group] + [swap(group, mask) for mask in (1, 2, 3)]
 
 
@@ -351,7 +364,7 @@
     own, *chunks = reduce_part(ids, own, arrived)
     arrived = [swap(chunk, mask) for chunk, mask in zip(chunks, (4, 8, 12))]
     stay, go = finish(ids, own, arrived, kept, head_gain[None])
-    normed = jnp.concatenate([stay, partner(go, "guide", 0)], axis=0)
+    normed = join([stay, partner(go, "guide", 0)])
     return head(ids, spread(normed), guide_scale[None], w_head)
 
 

time: 95.3 us -> 86.9 us (0.912)
  Pallas kernels: 26.9 us -> 18.6 us
    pallas_call x1, Pallas kernels: 14.8 us -> 6.55 us  [head(): pl.pallas_call(head_kernel, out_shape=jax.ShapeDtypeStruct((rows // 2, vo...]
where the time goes in v2:
time: 86.9 us; the launch traced here: 86.8 us
  starting transfers between devices  33.4 us (38%)
  waiting for transfers between devices  33 us (38%)
  Pallas kernels  18.6 us (21%)
    ppermute x24, starting transfers between devices, swap(): return lax.ppermute(value, 'blk', pairs)  33.3 us
    ppermute x24, waiting for transfers between devices, swap(): return lax.ppermute(value, 'blk', pairs)  31.9 us
    pallas_call x1, Pallas kernels, head(): pl.pallas_call(head_kernel, out_shape=jax.ShapeDtypeStruct((rows // 2, vo...  6.55 us
    pallas_call x1, Pallas kernels, attend(): pl.pallas_call(attend_kernel, out_shape=jax.ShapeDtypeStruct((slots, head...  6.47 us
    pallas_call x1, Pallas kernels, feed(): pl.pallas_call(feed_kernel, out_shape=[jax.ShapeDtypeStruct(part, F32), j...  3.08 us
  transfers between devices with their start and end apart: 25, of which 21 were waited for; matrix products, arithmetic and copies ran while one was open for 0% of the time, Pallas kernels for 0%

profile of v2, /device:TPU:0, one launch (start us, length us, event | category | flops | bytes accessed | tf_op | source)
XLA Modules:
  0.0 86.8 jit_solution(10287203155661949673)
XLA Ops:
  0.6 6.5 %attend.1.refs_0_ = bf16[8,2048]{1,0:T(8,128)(2,1)} custom-call(s32[2]{0:T(128)} %pad_add_fusion.ids, s32[128]{0:T(128)} %perm_h.1, s32[1,128]{1,0:T(1,128)} %lengths_h.1, bf16[8,9216]{1,0:T(8,128)(2,1)} %queries_h.1, bf16[8,576]{1,0:T(8,128)(2,1)} %new_h.1, bf16[8,576,256]{2,1,0:T(8,128)(2,1)} %bitcast.27, bf16[16,512,128]{2,1,0:T(8,128)(2,1)} %w_uv.1), custom_call_target="tpu_custom_call" | custom-call | flops 15000000512 | bytes 45000000 | tf_op jit(solution)/shard_map/attend/pallas_call | solution.py:109
  7.1 5.1 %collective-permute-start.2 = (bf16[8,2048]{1,0:T(8,128)(2,1)}, bf16[8,2048]{1,0:T(8,128)(2,1)S(1)}, u32[]{:S(2)}, u32[]{:S(2)}) collective-permute-start(bf16[8,2048]{1,0:T(8,128)(2,1)} %attend.1.refs_0_), channel_id=1, source_target_pairs={{0,12},{1,13},{2,14},{3,15},{4,8},{5,9},{6,10},{7,11},{8,4},{9,5},... | collective-permute-start | bytes 98312 | tf_op jit(solution)/shard_map/ppermute | solution.py:27
  12.8 1.5 %collective-permute-done.2.refs_3_ = bf16[8,2048]{1,0:T(8,128)(2,1)S(1)} collective-permute-done((bf16[8,2048]{1,0:T(8,128)(2,1)}, bf16[8,2048]{1,0:T(8,128)(2,1)S(1)}, u32[]{:S(2)}, u32[]{:S(2)}) %collective-permute-start.2) | collective-permute-done | bytes 32800 | tf_op jit(solution)/shard_map/ppermute | solution.py:27
  14.3 2.9 %collective-permute-done.1.refs_2_ = bf16[8,2048]{1,0:T(8,128)(2,1)S(1)} collective-permute-done((bf16[8,2048]{1,0:T(8,128)(2,1)}, bf16[8,2048]{1,0:T(8,128)(2,1)S(1)}, u32[]{:S(2)}, u32[]{:S(2)}) %collective-permute-start.1) | collective-permute-done | bytes 32800 | tf_op jit(solution)/shard_map/ppermute | solution.py:27
  18.0 2.5 %collective-permute-start.5 = (bf16[32,2048]{1,0:T(8,128)(2,1)S(1)}, bf16[32,2048]{1,0:T(8,128)(2,1)S(1)}, u32[]{:S(2)}, u32[]{:S(2)}) collective-permute-start(bf16[32,2048]{1,0:T(8,128)(2,1)S(1)} %join.4.v0), channel_id=1, source_target_pairs={{0,3},{1,2},{2,1},{3,0},{4,7},{5,6},{6,5},{7,4},{8,11},{9,10},{10,... | collective-permute-start | bytes 393224 | tf_op jit(solution)/shard_map/ppermute | solution.py:27
  21.6 3.8 %collective-permute-done.5.v3 = bf16[32,2048]{1,0:T(8,128)(2,1)S(1)} collective-permute-done((bf16[32,2048]{1,0:T(8,128)(2,1)S(1)}, bf16[32,2048]{1,0:T(8,128)(2,1)S(1)}, u32[]{:S(2)}, u32[]{:S(2)}) %collective-permute-start.5) | collective-permute-done | bytes 131104 | tf_op jit(solution)/shard_map/ppermute | solution.py:27
  26.2 1.2 %project.1.refs_0_ = bf16[128,128]{1,0:T(8,128)(2,1)S(1)} custom-call(s32[2]{0:T(128)S(1)} %copy-done.10, s32[1,128]{1,0:T(1,128)S(1)} %bitcast.25, bf16[32,2048]{1,0:T(8,128)(2,1)S(1)} %join.4.v0, bf16[32,2048]{1,0:T(8,128)(2,1)S(1)} %collective-permute-done.3.v1, bf16[32,2048]{1,0:T(8,128)(2,1)S(1)} %collective-permute-done.4.v2, ...), custom_call_target="tpu_custom_call" | custom-call | flops 15000000512 | bytes 45000000 | tf_op jit(solution)/shard_map/project/pallas_call | solution.py:154
  27.4 1.5 %collective-permute-start.8 = (bf16[128,128]{1,0:T(8,128)(2,1)S(1)}, bf16[128,128]{1,0:T(8,128)(2,1)S(1)}, u32[]{:S(2)}, u32[]{:S(2)}) collective-permute-start(bf16[128,128]{1,0:T(8,128)(2,1)S(1)} %project.1.refs_0_), channel_id=1, source_target_pairs={{0,12},{1,13},{2,14},{3,15},{4,8},{5,9},{6,10},{7,11},{8,4},{9,5},... | collective-permute-start | bytes 98312 | tf_op jit(solution)/shard_map/ppermute | solution.py:27
  29.6 2.3 %collective-permute-start.6 = (bf16[128,128]{1,0:T(8,128)(2,1)S(1)}, bf16[128,128]{1,0:T(8,128)(2,1)S(1)}, u32[]{:S(2)}, u32[]{:S(2)}) collective-permute-start(bf16[128,128]{1,0:T(8,128)(2,1)S(1)} %project.1.refs_0_), channel_id=1, source_target_pairs={{0,4},{1,5},{2,6},{3,7},{4,0},{5,1},{6,2},{7,3},{8,12},{9,13},{10,... | collective-permute-start | bytes 98312 | tf_op jit(solution)/shard_map/ppermute | solution.py:27
  31.9 1.3 %collective-permute-done.8.refs_3_ = bf16[128,128]{1,0:T(8,128)(2,1)S(1)} collective-permute-done((bf16[128,128]{1,0:T(8,128)(2,1)S(1)}, bf16[128,128]{1,0:T(8,128)(2,1)S(1)}, u32[]{:S(2)}, u32[]{:S(2)}) %collective-permute-start.8) | collective-permute-done | bytes 32800 | tf_op jit(solution)/shard_map/ppermute | solution.py:27
  34.1 1.5 %collective-permute-start.11 = (bf16[512,128]{1,0:T(8,128)(2,1)S(1)}, bf16[512,128]{1,0:T(8,128)(2,1)S(1)}, u32[]{:S(2)}, u32[]{:S(2)}) collective-permute-start(bf16[512,128]{1,0:T(8,128)(2,1)S(1)} %join.5), channel_id=1, source_target_pairs={{0,3},{1,2},{2,1},{3,0},{4,7},{5,6},{6,5},{7,4},{8,11},{9,10},{10,... | collective-permute-start | bytes 393224 | tf_op jit(solution)/shard_map/ppermute | solution.py:27
  35.6 1.5 %collective-permute-start.10 = (bf16[512,128]{1,0:T(8,128)(2,1)S(1)}, bf16[512,128]{1,0:T(8,128)(2,1)S(1)}, u32[]{:S(2)}, u32[]{:S(2)}) collective-permute-start(bf16[512,128]{1,0:T(8,128)(2,1)S(1)} %join.5), channel_id=1, source_target_pairs={{0,2},{1,3},{2,0},{3,1},{4,6},{5,7},{6,4},{7,5},{8,10},{9,11},{10,... | collective-permute-start | bytes 393224 | tf_op jit(solution)/shard_map/ppermute | solution.py:27
  37.6 2.5 %collective-permute-done.11 = bf16[512,128]{1,0:T(8,128)(2,1)S(1)} collective-permute-done((bf16[512,128]{1,0:T(8,128)(2,1)S(1)}, bf16[512,128]{1,0:T(8,128)(2,1)S(1)}, u32[]{:S(2)}, u32[]{:S(2)}) %collective-permute-start.11) | collective-permute-done | bytes 131104 | tf_op jit(solution)/shard_map/ppermute | solution.py:27
  40.1 1.3 %collective-permute-done.10 = bf16[512,128]{1,0:T(8,128)(2,1)S(1)} collective-permute-done((bf16[512,128]{1,0:T(8,128)(2,1)S(1)}, bf16[512,128]{1,0:T(8,128)(2,1)S(1)}, u32[]{:S(2)}, u32[]{:S(2)}) %collective-permute-start.10) | collective-permute-done | bytes 131104 | tf_op jit(solution)/shard_map/ppermute | solution.py:27
  42.1 3.1 %feed.1 = (f32[32,2048]{1,0:T(8,128)S(1)}, bf16[32,2048]{1,0:T(8,128)(2,1)S(1)}, bf16[32,2048]{1,0:T(8,128)(2,1)S(1)}, bf16[32,2048]{1,0:T(8,128)(2,1)S(1)}, f32[8,2048]{1,0:T(8,128)S(1)}) custom-call(s32[2]{0:T(128)S(1)} %copy-done.10, bf16[4,128,128]{2,1,0:T(8,128)(2,1)S(1)} %bitcast.19, bf16[4,128,128]{2,1,0:T(8,128)(2,1)S(1)} %bitcast.22, ...), custom_call_target="tpu_custom_call" | custom-call | flops 15000000512 | bytes 45000000 | tf_op jit(solution)/shard_map/feed/pallas_call | solution.py:198
  47.2 1.5 %collective-permute-start.14 = (bf16[32,2048]{1,0:T(8,128)(2,1)S(1)}, bf16[32,2048]{1,0:T(8,128)(2,1)S(1)}, u32[]{:S(2)}, u32[]{:S(2)}) collective-permute-start(bf16[32,2048]{1,0:T(8,128)(2,1)S(1)} %get-tuple-element.19), channel_id=1, source_target_pairs={{0,3},{1,2},{2,1},{3,0},{4,7},{5,6},{6,5},{7,4},{8,11},{9,10},{10,... | collective-permute-start | bytes 393224 | tf_op jit(solution)/shard_map/ppermute | solution.py:27
  48.7 1.5 %collective-permute-done.12.p1 = bf16[32,2048]{1,0:T(8,128)(2,1)S(1)} collective-permute-done((bf16[32,2048]{1,0:T(8,128)(2,1)S(1)}, bf16[32,2048]{1,0:T(8,128)(2,1)S(1)}, u32[]{:S(2)}, u32[]{:S(2)}) %collective-permute-start.12) | collective-permute-done | bytes 131104 | tf_op jit(solution)/shard_map/ppermute | solution.py:27
  51.1 2.0 %collective-permute-done.14.p3 = bf16[32,2048]{1,0:T(8,128)(2,1)S(1)} collective-permute-done((bf16[32,2048]{1,0:T(8,128)(2,1)S(1)}, bf16[32,2048]{1,0:T(8,128)(2,1)S(1)}, u32[]{:S(2)}, u32[]{:S(2)}) %collective-permute-start.14) | collective-permute-done | bytes 131104 | tf_op jit(solution)/shard_map/ppermute | solution.py:27
  53.7 1.7 %collective-permute-start.15 = (bf16[8,2048]{1,0:T(8,128)(2,1)S(1)}, bf16[8,2048]{1,0:T(8,128)(2,1)S(1)}, u32[]{:S(2)}, u32[]{:S(2)}) collective-permute-start(bf16[8,2048]{1,0:T(8,128)(2,1)S(1)} %get-tuple-element.21), channel_id=1, source_target_pairs={{0,4},{1,5},{2,6},{3,7},{4,0},{5,1},{6,2},{7,3},{8,12},{9,13},{10,... | collective-permute-start | bytes 98312 | tf_op jit(solution)/shard_map/ppermute | solution.py:27
  55.5 1.3 %collective-permute-start.16 = (bf16[8,2048]{1,0:T(8,128)(2,1)S(1)}, bf16[8,2048]{1,0:T(8,128)(2,1)S(1)}, u32[]{:S(2)}, u32[]{:S(2)}) collective-permute-start(bf16[8,2048]{1,0:T(8,128)(2,1)S(1)} %get-tuple-element.22), channel_id=1, source_target_pairs={{0,8},{1,9},{2,10},{3,11},{4,12},{5,13},{6,14},{7,15},{8,0},{9,1},... | collective-permute-start | bytes 98312 | tf_op jit(solution)/shard_map/ppermute | solution.py:27
  56.7 1.5 %collective-permute-start.17 = (bf16[8,2048]{1,0:T(8,128)(2,1)S(1)}, bf16[8,2048]{1,0:T(8,128)(2,1)S(1)}, u32[]{:S(2)}, u32[]{:S(2)}) collective-permute-start(bf16[8,2048]{1,0:T(8,128)(2,1)S(1)} %get-tuple-element.23), channel_id=1, source_target_pairs={{0,12},{1,13},{2,14},{3,15},{4,8},{5,9},{6,10},{7,11},{8,4},{9,5},... | collective-permute-start | bytes 98312 | tf_op jit(solution)/shard_map/ppermute | solution.py:27
  58.2 2.2 %collective-permute-done.16.p2 = bf16[8,2048]{1,0:T(8,128)(2,1)S(1)} collective-permute-done((bf16[8,2048]{1,0:T(8,128)(2,1)S(1)}, bf16[8,2048]{1,0:T(8,128)(2,1)S(1)}, u32[]{:S(2)}, u32[]{:S(2)}) %collective-permute-start.16) | collective-permute-done | bytes 32800 | tf_op jit(solution)/shard_map/ppermute | solution.py:27
  60.4 2.0 %collective-permute-done.17.p3 = bf16[8,2048]{1,0:T(8,128)(2,1)S(1)} collective-permute-done((bf16[8,2048]{1,0:T(8,128)(2,1)S(1)}, bf16[8,2048]{1,0:T(8,128)(2,1)S(1)}, u32[]{:S(2)}, u32[]{:S(2)}) %collective-permute-start.17) | collective-permute-done | bytes 32800 | tf_op jit(solution)/shard_map/ppermute | solution.py:27
  63.2 1.2 %collective-permute-done.18.refs_1_ = bf16[4,2048]{1,0:T(4,128)(2,1)S(1)} collective-permute-done((bf16[4,2048]{1,0:T(4,128)(2,1)S(1)}, bf16[4,2048]{1,0:T(4,128)(2,1)S(1)}, u32[]{:S(2)}, u32[]{:S(2)}) %collective-permute-start.18) | collective-permute-done | bytes 16416 | tf_op jit(solution)/shard_map/ppermute | solution.py:22
  64.4 1.5 %collective-permute-start.21 = (bf16[8,2048]{1,0:T(8,128)(2,1)S(1)}, bf16[8,2048]{1,0:T(8,128)(2,1)S(1)}, u32[]{:S(2)}, u32[]{:S(2)}) collective-permute-start(bf16[8,2048]{1,0:T(8,128)(2,1)S(1)} %join.6.refs_0_), channel_id=1, source_target_pairs={{0,12},{1,13},{2,14},{3,15},{4,8},{5,9},{6,10},{7,11},{8,4},{9,5},... | collective-permute-start | bytes 98312 | tf_op jit(solution)/shard_map/ppermute | solution.py:27
  66.0 2.9 %collective-permute-start.19 = (bf16[8,2048]{1,0:T(8,128)(2,1)S(1)}, bf16[8,2048]{1,0:T(8,128)(2,1)S(1)}, u32[]{:S(2)}, u32[]{:S(2)}) collective-permute-start(bf16[8,2048]{1,0:T(8,128)(2,1)S(1)} %join.6.refs_0_), channel_id=1, source_target_pairs={{0,4},{1,5},{2,6},{3,7},{4,0},{5,1},{6,2},{7,3},{8,12},{9,13},{10,... | collective-permute-start | bytes 98312 | tf_op jit(solution)/shard_map/ppermute | solution.py:27
  68.9 1.3 %collective-permute-done.21.refs_3_ = bf16[8,2048]{1,0:T(8,128)(2,1)S(1)} collective-permute-done((bf16[8,2048]{1,0:T(8,128)(2,1)S(1)}, bf16[8,2048]{1,0:T(8,128)(2,1)S(1)}, u32[]{:S(2)}, u32[]{:S(2)}) %collective-permute-start.21) | collective-permute-done | bytes 32800 | tf_op jit(solution)/shard_map/ppermute | solution.py:27
  71.4 1.2 %collective-permute-start.24 = (bf16[32,2048]{1,0:T(8,128)(2,1)S(1)}, bf16[32,2048]{1,0:T(8,128)(2,1)S(1)}, u32[]{:S(2)}, u32[]{:S(2)}) collective-permute-start(bf16[32,2048]{1,0:T(8,128)(2,1)S(1)} %join.7.r0), channel_id=1, source_target_pairs={{0,3},{1,2},{2,1},{3,0},{4,7},{5,6},{6,5},{7,4},{8,11},{9,10},{10,... | collective-permute-start | bytes 393224 | tf_op jit(solution)/shard_map/ppermute | solution.py:27
  73.7 1.2 %collective-permute-start.22 = (bf16[32,2048]{1,0:T(8,128)(2,1)S(1)}, bf16[32,2048]{1,0:T(8,128)(2,1)S(1)}, u32[]{:S(2)}, u32[]{:S(2)}) collective-permute-start(bf16[32,2048]{1,0:T(8,128)(2,1)S(1)} %join.7.r0), channel_id=1, source_target_pairs={{0,1},{1,0},{2,3},{3,2},{4,5},{5,4},{6,7},{7,6},{8,9},{9,8},{10,11... | collective-permute-start | bytes 393224 | tf_op jit(solution)/shard_map/ppermute | solution.py:27
  74.9 3.8 %collective-permute-done.24.r3 = bf16[32,2048]{1,0:T(8,128)(2,1)S(1)} collective-permute-done((bf16[32,2048]{1,0:T(8,128)(2,1)S(1)}, bf16[32,2048]{1,0:T(8,128)(2,1)S(1)}, u32[]{:S(2)}, u32[]{:S(2)}) %collective-permute-start.24) | collective-permute-done | bytes 131104 | tf_op jit(solution)/shard_map/ppermute | solution.py:27
  78.7 1.4 %collective-permute-done.23.r2 = bf16[32,2048]{1,0:T(8,128)(2,1)S(1)} collective-permute-done((bf16[32,2048]{1,0:T(8,128)(2,1)S(1)}, bf16[32,2048]{1,0:T(8,128)(2,1)S(1)}, u32[]{:S(2)}, u32[]{:S(2)}) %collective-permute-start.23) | collective-permute-done | bytes 131104 | tf_op jit(solution)/shard_map/ppermute | solution.py:27
  80.2 6.5 %head.1 = bf16[64,6400]{1,0:T(8,128)(2,1)} custom-call(s32[2]{0:T(128)S(1)} %copy-done.10, bf16[32,2048]{1,0:T(8,128)(2,1)S(1)} %join.7.r0, bf16[32,2048]{1,0:T(8,128)(2,1)S(1)} %collective-permute-done.22.r1, bf16[32,2048]{1,0:T(8,128)(2,1)S(1)} %collective-permute-done.23.r2, bf16[32,2048]{1,0:T(8,128)(2,1)S(1)} %collective-permute-done.24.r3, ...), custom_call_target="tpu_custom_call" | custom-call | flops 8000000000 | bytes 24000000 | tf_op jit(solution)/shard_map/head/pallas_call | solution.py:298
  (66 shorter events, 13.2 us)
Async XLA Ops:
  0.6 25.5 %copy-start.8 = (s32[128]{0:T(128)S(1)}, s32[128]{0:T(128)}, u32[]{:S(2)}) copy-start(s32[128]{0:T(128)} %perm_h.1) | copy-start | bytes 1540
  0.6 25.5 %copy-start.10 = (s32[2]{0:T(128)S(1)}, s32[2]{0:T(128)}, u32[]{:S(2)}) copy-start(s32[2]{0:T(128)} %pad_add_fusion.ids) | copy-start | bytes 28
  7.1 19.1 %copy-start.3 = (bf16[2048,128]{1,0:T(8,128)(2,1)S(1)}, bf16[2048,128]{1,0:T(8,128)(2,1)}, u32[]{:S(2)}) copy-start(bf16[2048,128]{1,0:T(8,128)(2,1)} %w_out.1) | copy-start | bytes 1572868
  7.1 19.1 %copy-start.4 = (bf16[128,128]{1,0:T(8,128)(2,1)S(1)}, bf16[128,128]{1,0:T(8,128)(2,1)}, u32[]{:S(2)}) copy-start(bf16[128,128]{1,0:T(8,128)(2,1)} %x_cols.1) | copy-start | bytes 98308
  7.1 7.2 %collective-permute-start.2 = (bf16[8,2048]{1,0:T(8,128)(2,1)}, bf16[8,2048]{1,0:T(8,128)(2,1)S(1)}, u32[]{:S(2)}, u32[]{:S(2)}) collective-permute-start(bf16[8,2048]{1,0:T(8,128)(2,1)} %attend.1.refs_0_), channel_id=1, source_target_pairs={{0,12},{1,13},{2,14},{3,15},{4,8},{5,9},{6,10},{7,11},{8,4},{9,5},... | collective-permute-start | bytes 98312 | tf_op jit(solution)/shard_map/ppermute | solution.py:27
  12.2 5.0 %collective-permute-start.1 = (bf16[8,2048]{1,0:T(8,128)(2,1)}, bf16[8,2048]{1,0:T(8,128)(2,1)S(1)}, u32[]{:S(2)}, u32[]{:S(2)}) collective-permute-start(bf16[8,2048]{1,0:T(8,128)(2,1)} %attend.1.refs_0_), channel_id=1, source_target_pairs={{0,8},{1,9},{2,10},{3,11},{4,12},{5,13},{6,14},{7,15},{8,0},{9,1},... | collective-permute-start | bytes 98312 | tf_op jit(solution)/shard_map/ppermute | solution.py:27
  12.2 5.0 %collective-permute-start = (bf16[8,2048]{1,0:T(8,128)(2,1)}, bf16[8,2048]{1,0:T(8,128)(2,1)S(1)}, u32[]{:S(2)}, u32[]{:S(2)}) collective-permute-start(bf16[8,2048]{1,0:T(8,128)(2,1)} %attend.1.refs_0_), channel_id=1, source_target_pairs={{0,4},{1,5},{2,6},{3,7},{4,0},{5,1},{6,2},{7,3},{8,12},{9,13},{10,... | collective-permute-start | bytes 98312 | tf_op jit(solution)/shard_map/ppermute | solution.py:27
  18.0 7.3 %collective-permute-start.5 = (bf16[32,2048]{1,0:T(8,128)(2,1)S(1)}, bf16[32,2048]{1,0:T(8,128)(2,1)S(1)}, u32[]{:S(2)}, u32[]{:S(2)}) collective-permute-start(bf16[32,2048]{1,0:T(8,128)(2,1)S(1)} %join.4.v0), channel_id=1, source_target_pairs={{0,3},{1,2},{2,1},{3,0},{4,7},{5,6},{6,5},{7,4},{8,11},{9,10},{10,... | collective-permute-start | bytes 393224 | tf_op jit(solution)/shard_map/ppermute | solution.py:27
  20.5 5.6 %collective-permute-start.4 = (bf16[32,2048]{1,0:T(8,128)(2,1)S(1)}, bf16[32,2048]{1,0:T(8,128)(2,1)S(1)}, u32[]{:S(2)}, u32[]{:S(2)}) collective-permute-start(bf16[32,2048]{1,0:T(8,128)(2,1)S(1)} %join.4.v0), channel_id=1, source_target_pairs={{0,2},{1,3},{2,0},{3,1},{4,6},{5,7},{6,4},{7,5},{8,10},{9,11},{10,... | collective-permute-start | bytes 393224 | tf_op jit(solution)/shard_map/ppermute | solution.py:27
  21.0 5.1 %collective-permute-start.3 = (bf16[32,2048]{1,0:T(8,128)(2,1)S(1)}, bf16[32,2048]{1,0:T(8,128)(2,1)S(1)}, u32[]{:S(2)}, u32[]{:S(2)}) collective-permute-start(bf16[32,2048]{1,0:T(8,128)(2,1)S(1)} %join.4.v0), channel_id=1, source_target_pairs={{0,1},{1,0},{2,3},{3,2},{4,5},{5,4},{6,7},{7,6},{8,9},{9,8},{10,11... | collective-permute-start | bytes 393224 | tf_op jit(solution)/shard_map/ppermute | solution.py:27
  27.4 5.8 %collective-permute-start.8 = (bf16[128,128]{1,0:T(8,128)(2,1)S(1)}, bf16[128,128]{1,0:T(8,128)(2,1)S(1)}, u32[]{:S(2)}, u32[]{:S(2)}) collective-permute-start(bf16[128,128]{1,0:T(8,128)(2,1)S(1)} %project.1.refs_0_), channel_id=1, source_target_pairs={{0,12},{1,13},{2,14},{3,15},{4,8},{5,9},{6,10},{7,11},{8,4},{9,5},... | collective-permute-start | bytes 98312 | tf_op jit(solution)/shard_map/ppermute | solution.py:27
  28.9 4.8 %collective-permute-start.7 = (bf16[128,128]{1,0:T(8,128)(2,1)S(1)}, bf16[128,128]{1,0:T(8,128)(2,1)S(1)}, u32[]{:S(2)}, u32[]{:S(2)}) collective-permute-start(bf16[128,128]{1,0:T(8,128)(2,1)S(1)} %project.1.refs_0_), channel_id=1, source_target_pairs={{0,8},{1,9},{2,10},{3,11},{4,12},{5,13},{6,14},{7,15},{8,0},{9,1},... | collective-permute-start | bytes 98312 | tf_op jit(solution)/shard_map/ppermute | solution.py:27
  29.6 4.5 %collective-permute-start.6 = (bf16[128,128]{1,0:T(8,128)(2,1)S(1)}, bf16[128,128]{1,0:T(8,128)(2,1)S(1)}, u32[]{:S(2)}, u32[]{:S(2)}) collective-permute-start(bf16[128,128]{1,0:T(8,128)(2,1)S(1)} %project.1.refs_0_), channel_id=1, source_target_pairs={{0,4},{1,5},{2,6},{3,7},{4,0},{5,1},{6,2},{7,3},{8,12},{9,13},{10,... | collective-permute-start | bytes 98312 | tf_op jit(solution)/shard_map/ppermute | solution.py:27
  34.1 6.0 %collective-permute-start.11 = (bf16[512,128]{1,0:T(8,128)(2,1)S(1)}, bf16[512,128]{1,0:T(8,128)(2,1)S(1)}, u32[]{:S(2)}, u32[]{:S(2)}) collective-permute-start(bf16[512,128]{1,0:T(8,128)(2,1)S(1)} %join.5), channel_id=1, source_target_pairs={{0,3},{1,2},{2,1},{3,0},{4,7},{5,6},{6,5},{7,4},{8,11},{9,10},{10,... | collective-permute-start | bytes 393224 | tf_op jit(solution)/shard_map/ppermute | solution.py:27
  35.6 5.8 %collective-permute-start.10 = (bf16[512,128]{1,0:T(8,128)(2,1)S(1)}, bf16[512,128]{1,0:T(8,128)(2,1)S(1)}, u32[]{:S(2)}, u32[]{:S(2)}) collective-permute-start(bf16[512,128]{1,0:T(8,128)(2,1)S(1)} %join.5), channel_id=1, source_target_pairs={{0,2},{1,3},{2,0},{3,1},{4,6},{5,7},{6,4},{7,5},{8,10},{9,11},{10,... | collective-permute-start | bytes 393224 | tf_op jit(solution)/shard_map/ppermute | solution.py:27
  37.1 5.0 %collective-permute-start.9 = (bf16[512,128]{1,0:T(8,128)(2,1)S(1)}, bf16[512,128]{1,0:T(8,128)(2,1)S(1)}, u32[]{:S(2)}, u32[]{:S(2)}) collective-permute-start(bf16[512,128]{1,0:T(8,128)(2,1)S(1)} %join.5), channel_id=1, source_target_pairs={{0,1},{1,0},{2,3},{3,2},{4,5},{5,4},{6,7},{7,6},{8,9},{9,8},{10,11... | collective-permute-start | bytes 393224 | tf_op jit(solution)/shard_map/ppermute | solution.py:27
  45.2 5.0 %collective-permute-start.12 = (bf16[32,2048]{1,0:T(8,128)(2,1)S(1)}, bf16[32,2048]{1,0:T(8,128)(2,1)S(1)}, u32[]{:S(2)}, u32[]{:S(2)}) collective-permute-start(bf16[32,2048]{1,0:T(8,128)(2,1)S(1)} %get-tuple-element.17), channel_id=1, source_target_pairs={{0,1},{1,0},{2,3},{3,2},{4,5},{5,4},{6,7},{7,6},{8,9},{9,8},{10,11... | collective-permute-start | bytes 393224 | tf_op jit(solution)/shard_map/ppermute | solution.py:27
  46.1 5.0 %collective-permute-start.13 = (bf16[32,2048]{1,0:T(8,128)(2,1)S(1)}, bf16[32,2048]{1,0:T(8,128)(2,1)S(1)}, u32[]{:S(2)}, u32[]{:S(2)}) collective-permute-start(bf16[32,2048]{1,0:T(8,128)(2,1)S(1)} %get-tuple-element.18), channel_id=1, source_target_pairs={{0,2},{1,3},{2,0},{3,1},{4,6},{5,7},{6,4},{7,5},{8,10},{9,11},{10,... | collective-permute-start | bytes 393224 | tf_op jit(solution)/shard_map/ppermute | solution.py:27
  47.2 5.9 %collective-permute-start.14 = (bf16[32,2048]{1,0:T(8,128)(2,1)S(1)}, bf16[32,2048]{1,0:T(8,128)(2,1)S(1)}, u32[]{:S(2)}, u32[]{:S(2)}) collective-permute-start(bf16[32,2048]{1,0:T(8,128)(2,1)S(1)} %get-tuple-element.19), channel_id=1, source_target_pairs={{0,3},{1,2},{2,1},{3,0},{4,7},{5,6},{6,5},{7,4},{8,11},{9,10},{10,... | collective-permute-start | bytes 393224 | tf_op jit(solution)/shard_map/ppermute | solution.py:27
  53.7 4.5 %collective-permute-start.15 = (bf16[8,2048]{1,0:T(8,128)(2,1)S(1)}, bf16[8,2048]{1,0:T(8,128)(2,1)S(1)}, u32[]{:S(2)}, u32[]{:S(2)}) collective-permute-start(bf16[8,2048]{1,0:T(8,128)(2,1)S(1)} %get-tuple-element.21), channel_id=1, source_target_pairs={{0,4},{1,5},{2,6},{3,7},{4,0},{5,1},{6,2},{7,3},{8,12},{9,13},{10,... | collective-permute-start | bytes 98312 | tf_op jit(solution)/shard_map/ppermute | solution.py:27
  55.5 5.0 %collective-permute-start.16 = (bf16[8,2048]{1,0:T(8,128)(2,1)S(1)}, bf16[8,2048]{1,0:T(8,128)(2,1)S(1)}, u32[]{:S(2)}, u32[]{:S(2)}) collective-permute-start(bf16[8,2048]{1,0:T(8,128)(2,1)S(1)} %get-tuple-element.22), channel_id=1, source_target_pairs={{0,8},{1,9},{2,10},{3,11},{4,12},{5,13},{6,14},{7,15},{8,0},{9,1},... | collective-permute-start | bytes 98312 | tf_op jit(solution)/shard_map/ppermute | solution.py:27
  56.7 5.7 %collective-permute-start.17 = (bf16[8,2048]{1,0:T(8,128)(2,1)S(1)}, bf16[8,2048]{1,0:T(8,128)(2,1)S(1)}, u32[]{:S(2)}, u32[]{:S(2)}) collective-permute-start(bf16[8,2048]{1,0:T(8,128)(2,1)S(1)} %get-tuple-element.23), channel_id=1, source_target_pairs={{0,12},{1,13},{2,14},{3,15},{4,8},{5,9},{6,10},{7,11},{8,4},{9,5},... | collective-permute-start | bytes 98312 | tf_op jit(solution)/shard_map/ppermute | solution.py:27
  62.4 17.7 %slice-start.3 = ((s8[26214400]{0:T(1024)(128)(4,1)}), s8[4194304]{0:T(1024)(128)(4,1)S(1)}, s32[]{:S(2)}) async-start(s8[26214400]{0:T(1024)(128)(4,1)} %bitcast.15), calls=%async_computation.3 | async-start | bytes 8388608
  62.5 17.7 %slice-start.4 = ((s8[26214400]{0:T(1024)(128)(4,1)}), s8[4194304]{0:T(1024)(128)(4,1)S(1)}, s32[]{:S(2)}) async-start(s8[26214400]{0:T(1024)(128)(4,1)} %bitcast.15), calls=%async_computation.4 | async-start | bytes 8388608
  62.5 17.7 %slice-start.5 = ((s8[26214400]{0:T(1024)(128)(4,1)}), s8[4194304]{0:T(1024)(128)(4,1)S(1)}, s32[]{:S(2)}) async-start(s8[26214400]{0:T(1024)(128)(4,1)} %bitcast.15), calls=%async_computation.5 | async-start | bytes 8388608
  63.2 1.2 %collective-permute-start.18 = (bf16[4,2048]{1,0:T(4,128)(2,1)S(1)}, bf16[4,2048]{1,0:T(4,128)(2,1)S(1)}, u32[]{:S(2)}, u32[]{:S(2)}) collective-permute-start(bf16[4,2048]{1,0:T(4,128)(2,1)S(1)} %get-tuple-element.26), channel_id=1, source_target_pairs={{0,16},{16,0},{1,17},{17,1},{2,18},{18,2},{3,19},{19,3},{4,20},{20... | collective-permute-start | bytes 49160 | tf_op jit(solution)/shard_map/ppermute | solution.py:22
  64.4 5.8 %collective-permute-start.21 = (bf16[8,2048]{1,0:T(8,128)(2,1)S(1)}, bf16[8,2048]{1,0:T(8,128)(2,1)S(1)}, u32[]{:S(2)}, u32[]{:S(2)}) collective-permute-start(bf16[8,2048]{1,0:T(8,128)(2,1)S(1)} %join.6.refs_0_), channel_id=1, source_target_pairs={{0,12},{1,13},{2,14},{3,15},{4,8},{5,9},{6,10},{7,11},{8,4},{9,5},... | collective-permute-start | bytes 98312 | tf_op jit(solution)/shard_map/ppermute | solution.py:27
  66.0 5.3 %collective-permute-start.20 = (bf16[8,2048]{1,0:T(8,128)(2,1)S(1)}, bf16[8,2048]{1,0:T(8,128)(2,1)S(1)}, u32[]{:S(2)}, u32[]{:S(2)}) collective-permute-start(bf16[8,2048]{1,0:T(8,128)(2,1)S(1)} %join.6.refs_0_), channel_id=1, source_target_pairs={{0,8},{1,9},{2,10},{3,11},{4,12},{5,13},{6,14},{7,15},{8,0},{9,1},... | collective-permute-start | bytes 98312 | tf_op jit(solution)/shard_map/ppermute | solution.py:27
  66.0 5.4 %collective-permute-start.19 = (bf16[8,2048]{1,0:T(8,128)(2,1)S(1)}, bf16[8,2048]{1,0:T(8,128)(2,1)S(1)}, u32[]{:S(2)}, u32[]{:S(2)}) collective-permute-start(bf16[8,2048]{1,0:T(8,128)(2,1)S(1)} %join.6.refs_0_), channel_id=1, source_target_pairs={{0,4},{1,5},{2,6},{3,7},{4,0},{5,1},{6,2},{7,3},{8,12},{9,13},{10,... | collective-permute-start | bytes 98312 | tf_op jit(solution)/shard_map/ppermute | solution.py:27
  71.4 7.4 %collective-permute-start.24 = (bf16[32,2048]{1,0:T(8,128)(2,1)S(1)}, bf16[32,2048]{1,0:T(8,128)(2,1)S(1)}, u32[]{:S(2)}, u32[]{:S(2)}) collective-permute-start(bf16[32,2048]{1,0:T(8,128)(2,1)S(1)} %join.7.r0), channel_id=1, source_target_pairs={{0,3},{1,2},{2,1},{3,0},{4,7},{5,6},{6,5},{7,4},{8,11},{9,10},{10,... | collective-permute-start | bytes 393224 | tf_op jit(solution)/shard_map/ppermute | solution.py:27
  72.6 7.5 %collective-permute-start.23 = (bf16[32,2048]{1,0:T(8,128)(2,1)S(1)}, bf16[32,2048]{1,0:T(8,128)(2,1)S(1)}, u32[]{:S(2)}, u32[]{:S(2)}) collective-permute-start(bf16[32,2048]{1,0:T(8,128)(2,1)S(1)} %join.7.r0), channel_id=1, source_target_pairs={{0,2},{1,3},{2,0},{3,1},{4,6},{5,7},{6,4},{7,5},{8,10},{9,11},{10,... | collective-permute-start | bytes 393224 | tf_op jit(solution)/shard_map/ppermute | solution.py:27
  73.7 6.4 %collective-permute-start.22 = (bf16[32,2048]{1,0:T(8,128)(2,1)S(1)}, bf16[32,2048]{1,0:T(8,128)(2,1)S(1)}, u32[]{:S(2)}, u32[]{:S(2)}) collective-permute-start(bf16[32,2048]{1,0:T(8,128)(2,1)S(1)} %join.7.r0), channel_id=1, source_target_pairs={{0,1},{1,0},{2,3},{3,2},{4,5},{5,4},{6,7},{7,6},{8,9},{9,8},{10,11... | collective-permute-start | bytes 393224 | tf_op jit(solution)/shard_map/ppermute | solution.py:27
  (11 other events, 157.9 us)

commit v3 on v2

--- a/solution.py
+++ b/solution.py
@@ -12,7 +12,6 @@
 NT = (((1,), (1,)), ((), ()))
 TN = (((0,), (0,)), ((), ()))
 VM = pl.BlockSpec(memory_space=pltpu.VMEM)
-SM = pl.BlockSpec(memory_space=pltpu.SMEM)
 HB = pl.BlockSpec(memory_space=pltpu.HBM)
 
 
@@ -46,13 +45,13 @@
 
 
 def attend_kernel(
-    ids, perm_h, lengths_h, queries_h, new_h, cache, w_uv, out,
+    perm_h, lengths_h, queries_h, new_h, cache, w_uv, out,
     perm, lengths, queries, new_kv, qs, keys, up, sems, others,
 ):
     slots, width, positions = cache.shape
     heads, latent, nope = w_uv.shape
     rows = heads * slots
-    first = ids[1] * slots
+    first = lax.axis_index("blk") * slots
     small = [
         pltpu.make_async_copy(source, target, others.at[k])
         for k, (source, target) in enumerate(
@@ -103,13 +102,13 @@
         out[:, h * nope : (h + 1) * nope] = dot(rows_h, up[h], NN).astype(BF)
 
 
-def attend(ids, perm, lengths, queries, new_kv, cache, w_uv):
+def attend(perm, lengths, queries, new_kv, cache, w_uv):
     slots, width, positions = cache.shape
     heads, latent, nope = w_uv.shape
     return pl.pallas_call(
         attend_kernel,
         out_shape=jax.ShapeDtypeStruct((slots, heads * nope), BF),
-        in_specs=[SM] + [HB] * 6,
+        in_specs=[HB] * 6,
         out_specs=VM,
         scratch_shapes=[
             pltpu.SMEM(perm.shape, jnp.int32),
@@ -125,19 +124,21 @@
         compiler_params=pltpu.CompilerParams(vmem_limit_bytes=60 << 20),
         cost_estimate=cost(15),
         name="attend",
-    )(ids, perm, lengths, queries, new_kv, cache, w_uv)
+    )(perm, lengths, queries, new_kv, cache, w_uv)
 
 
 def request_of(row, rows):
-    chip = ((row >> 3) & 3) * 4 + (row >> 5)
-    return ((row >> 2) & 1) * (rows // 2) + chip * 4 + (row & 3)
-
-
-def project_kernel(ids, perm, v0, v1, v2, v3, w_out, x_cols, out):
-    blk = ids[1]
+    chip = ((row >> 2) & 3) * 4 + (row >> 5)
+    return ((row >> 4) & 1) * (rows // 2) + chip * 4 + (row & 3)
+
+
+def project_kernel(perm, v0, v1, v2, v3, w_out, x_cols, out, full):
+    blk = lax.axis_index("blk")
     rows = x_cols.shape[0]
-    w = w_out[...]
-    attended = jnp.concatenate([dot(v[...], w, NN) for v in (v0, v1, v2, v3)], axis=0)
+    part = v0.shape[0]
+    for q, ref in enumerate((v0, v1, v2, v3)):
+        full[q * part : (q + 1) * part, :] = ref[...]
+    attended = dot(full[...], w_out[...], NN)
     shape = (rows, rows)
     wanted = request_of(iota(shape, 0), rows)
     by_slot = (jnp.broadcast_to(perm[...], shape) == wanted).astype(F32)
@@ -150,22 +151,23 @@
     out[...] = (base + moved).astype(BF)
 
 
-def project(ids, perm, pieces, w_out, x_cols):
+def project(perm, pieces, w_out, x_cols):
     return pl.pallas_call(
         project_kernel,
         out_shape=jax.ShapeDtypeStruct(x_cols.shape, BF),
-        in_specs=[SM] + [VM] * 7,
+        in_specs=[VM] * 7,
         out_specs=VM,
+        scratch_shapes=[pltpu.VMEM((x_cols.shape[0], w_out.shape[0]), BF)],
         compiler_params=pltpu.CompilerParams(vmem_limit_bytes=4 << 20),
         cost_estimate=cost(15),
         name="project",
-    )(ids, perm, *pieces, w_out, x_cols)
+    )(perm, *pieces, w_out, x_cols)
 
 
 def feed_kernel(
-    ids, r0, r1, r2, r3, gain, w_gate, w_up, w_down, own, c1, c2, c3, kept, full, acc
+    r0, r1, r2, r3, gain, w_gate, w_up, w_down, own, c1, c2, c3, kept, full, acc
 ):
-    blk = ids[1]
+    blk = lax.axis_index("blk")
     groups, rows, cols = r0.shape
     units = w_gate.shape[0]
     for q, ref in enumerate((r0, r1, r2, r3)):
@@ -181,17 +183,15 @@
     hidden = gate * (1.0 / (1.0 + jnp.exp(-gate))) * up
     hidden = jnp.where(unit < FF, hidden, 0.0).astype(BF)
     acc[...] = dot(hidden, w_down[...], NN)
-    low, high = blk & 3, blk >> 2
+    low = blk & 3
     chunk = rows // 4
     for q, ref in enumerate((own, c1, c2, c3)):
         at = pl.multiple_of((low ^ q) * chunk, chunk)
         ref[...] = acc[pl.ds(at, chunk), :].astype(ref.dtype)
-    small = chunk // 4
-    at = pl.multiple_of(low * chunk + high * small, small)
-    kept[...] = full[pl.ds(at, small), :]
-
-
-def feed(ids, pieces, gain, w_gate, w_up, w_down):
+    kept[...] = full[pl.ds(pl.multiple_of(low * chunk, chunk), chunk), :]
+
+
+def feed(pieces, gain, w_gate, w_up, w_down):
     groups, rows, cols = pieces[0].shape
     width = w_down.shape[1]
     part = (rows // 4, width)
@@ -202,109 +202,117 @@
             jax.ShapeDtypeStruct(part, BF),
             jax.ShapeDtypeStruct(part, BF),
             jax.ShapeDtypeStruct(part, BF),
-            jax.ShapeDtypeStruct((rows // 16, width), F32),
+            jax.ShapeDtypeStruct(part, F32),
         ],
-        in_specs=[SM] + [VM] * 8,
+        in_specs=[VM] * 8,
         out_specs=[VM] * 5,
         scratch_shapes=[pltpu.VMEM((rows, width), F32), pltpu.VMEM((rows, width), F32)],
         compiler_params=pltpu.CompilerParams(vmem_limit_bytes=8 << 20),
         cost_estimate=cost(15),
         name="feed",
-    )(ids, *pieces, gain, w_gate, w_up, w_down)
-
-
-def reduce_kernel(ids, own, p1, p2, p3, keep, o1, o2, o3, acc):
-    high = ids[1] >> 2
-    acc[...] = own[...] + p1[...].astype(F32) + p2[...].astype(F32) + p3[...].astype(F32)
-    small = keep.shape[0]
-    for j, ref in enumerate((keep, o1, o2, o3)):
-        at = pl.multiple_of((high ^ j) * small, small)
-        ref[...] = acc[pl.ds(at, small), :].astype(ref.dtype)
-
-
-def reduce_part(ids, own, parts):
-    rows, width = own.shape
-    small = (rows // 4, width)
-    return pl.pallas_call(
-        reduce_kernel,
-        out_shape=[jax.ShapeDtypeStruct(small, F32)] + [jax.ShapeDtypeStruct(small, BF)] * 3,
-        in_specs=[SM] + [VM] * 4,
-        out_specs=[VM] * 4,
-        scratch_shapes=[pltpu.VMEM((rows, width), F32)],
+    )(*pieces, gain, w_gate, w_up, w_down)
+
+
+def sum_kernel(*refs):
+    out = refs[-1]
+    total = refs[0][...].astype(F32)
+    for ref in refs[1:-1]:
+        total += ref[...].astype(F32)
+    out[...] = total.astype(out.dtype)
+
+
+def add(parts):
+    return pl.pallas_call(
+        sum_kernel,
+        out_shape=jax.ShapeDtypeStruct(parts[0].shape, BF),
+        in_specs=[VM] * len(parts),
+        out_specs=VM,
         compiler_params=pltpu.CompilerParams(vmem_limit_bytes=2 << 20),
         cost_estimate=cost(20),
-        name="reduce_part",
-    )(ids, own, *parts)
-
-
-def finish_kernel(ids, own, p1, p2, p3, kept, gain, stay, go):
-    total = own[...] + p1[...].astype(F32) + p2[...].astype(F32) + p3[...].astype(F32)
-    after = (kept[...] + total).astype(BF).astype(F32)
+        name="add",
+    )(*parts)
+
+
+def finish_kernel(own, other, kept, gain, stay, go):
+    after = (kept[...] + (own[...].astype(F32) + other[...].astype(F32))).astype(BF).astype(F32)
     meansq = jnp.mean(after * after, axis=1, keepdims=True)
-    normed = after * lax.rsqrt(meansq + 1e-06) * gain[...]
+    normed = (after * lax.rsqrt(meansq + 1e-06) * gain[...]).astype(BF)
     half = normed.shape[0] // 2
     first, last = normed[:half], normed[half:]
-    lower = ids[0] == 0
-    stay[...] = jnp.where(lower, first, last).astype(BF)
-    go[...] = jnp.where(lower, last, first).astype(BF)
-
-
-def finish(ids, own, parts, kept, gain):
+    lower = lax.axis_index("guide") == 0
+    stay[...] = jnp.where(lower, first, last)
+    go[...] = jnp.where(lower, last, first)
+
+
+def finish(own, other, kept, gain):
     rows, width = own.shape
     return pl.pallas_call(
         finish_kernel,
         out_shape=[jax.ShapeDtypeStruct((rows // 2, width), BF)] * 2,
-        in_specs=[SM] + [VM] * 6,
+        in_specs=[VM] * 4,
         out_specs=[VM] * 2,
-        compiler_params=pltpu.CompilerParams(vmem_limit_bytes=1 << 20),
+        compiler_params=pltpu.CompilerParams(vmem_limit_bytes=2 << 20),
         cost_estimate=cost(20),
         name="finish",
-    )(ids, own, *parts, kept, gain)
-
-
-def head_kernel(ids, r0, r1, r2, r3, scale, w_head, out, full, factor):
-    guide, blk = ids[0], ids[1]
+    )(own, other, kept, gain)
+
+
+def head_kernel(r0, r1, r2, r3, scale, w_head, out, came, full, factor, done, sems):
+    guide, blk = lax.axis_index("guide"), lax.axis_index("blk")
     part = r0.shape[0]
     rows = 4 * part
     half = rows // 2
-    vocab = w_head.shape[1]
-    tile = next(t for t in (1280, 256, 128) if vocab % t == 0)
-    wanted = iota((rows, part), 0)
-    total = None
+    tiles, _, tile = done.shape
     for q, ref in enumerate((r0, r1, r2, r3)):
-        at = iota((rows, part), 1)
-        chip = blk ^ ((at >> 3) << 2) ^ q
-        row = (((at >> 2) & 1) ^ guide) * half + chip * 4 + (at & 3)
-        piece = dot((row == wanted).astype(BF), ref[...], NN)
-        total = piece if total is None else total + piece
-    full[...] = total.astype(BF)
+        came[q * part : (q + 1) * part, :] = ref[...]
+    at = iota((rows, rows), 1)
+    chip = (((at >> 2) & 3) << 2) + ((blk & 3) ^ (at >> 5))
+    row = (((at >> 4) & 1) ^ guide) * half + chip * 4 + (at & 3)
+    order = (row == iota((rows, rows), 0)).astype(BF)
+    full[...] = dot(order, came[...], NN).astype(BF)
     mine = iota((half, rows), 0) + guide * half == iota((half, rows), 1)
     factor[...] = jnp.sum(
         jnp.where(mine, jnp.broadcast_to(scale[...], (half, rows)), 0.0), 1, keepdims=True
     )
 
-    @pl.loop(0, vocab // tile)
+    def store(step):
+        at = pl.ds(pl.multiple_of(step * tile, tile), tile)
+        return pltpu.make_async_copy(done.at[step], out.at[:, at], sems.at[step])
+
+    @pl.loop(0, tiles)
     def _(step):
         at = pl.ds(pl.multiple_of(step * tile, tile), tile)
         logits = dot(full[...], w_head[:, at], NN)
         cond, uncond = logits[:half], logits[half:]
-        out[:, at] = (uncond + factor[...] * (cond - uncond)).astype(BF)
-
-
-def head(ids, pieces, scale, w_head):
+        done[step] = (uncond + factor[...] * (cond - uncond)).astype(BF)
+        store(step).start()
+
+    @pl.loop(0, tiles)
+    def _(step):
+        store(step).wait()
+
+
+def head(pieces, scale, w_head):
     part, width = pieces[0].shape
     rows = 4 * part
     vocab = w_head.shape[1]
+    tile = next(t for t in (1280, 256, 128) if vocab % t == 0)
     return pl.pallas_call(
         head_kernel,
         out_shape=jax.ShapeDtypeStruct((rows // 2, vocab), BF),
-        in_specs=[SM] + [VM] * 6,
-        out_specs=VM,
-        scratch_shapes=[pltpu.VMEM((rows, width), BF), pltpu.VMEM((rows // 2, 1), F32)],
+        in_specs=[VM] * 6,
+        out_specs=HB,
+        scratch_shapes=[
+            pltpu.VMEM((rows, width), BF),
+            pltpu.VMEM((rows, width), BF),
+            pltpu.VMEM((rows // 2, 1), F32),
+            pltpu.VMEM((vocab // tile, rows // 2, tile), BF),
+            pltpu.SemaphoreType.DMA((vocab // tile,)),
+        ],
         compiler_params=pltpu.CompilerParams(vmem_limit_bytes=8 << 20),
         cost_estimate=cost(8),
         name="head",
-    )(ids, *pieces, scale, w_head)
+    )(*pieces, scale, w_head)
 
 
 def join_kernel(*refs):
@@ -349,23 +357,20 @@
     head_gain,
     w_head,
 ):
-    guide_index = lax.axis_index("guide")
-    blk_index = lax.axis_index("blk")
-    ids = jnp.stack([guide_index, blk_index]).astype(jnp.int32)
     rows, cols = x_cols.shape
     keys = jnp.swapaxes(cache[0], 1, 2)
-    values = attend(ids, perm, lengths, queries, new_kv, keys, w_uv)
-    residual = project(ids, perm[None], spread(values), w_out, x_cols)
+    values = attend(perm, lengths, queries, new_kv, keys, w_uv)
+    residual = project(perm[None], spread(values), w_out, x_cols)
     pieces = [piece.reshape(4, rows, cols) for piece in spread(residual)]
     own, *chunks, kept = feed(
-        ids, pieces, mlp_gain[None], jnp.swapaxes(w_gate, 0, 1), jnp.swapaxes(w_up, 0, 1), w_down
+        pieces, mlp_gain[None], jnp.swapaxes(w_gate, 0, 1), jnp.swapaxes(w_up, 0, 1), w_down
     )
     arrived = [swap(chunk, mask) for chunk, mask in zip(chunks, (1, 2, 3))]
-    own, *chunks = reduce_part(ids, own, arrived)
-    arrived = [swap(chunk, mask) for chunk, mask in zip(chunks, (4, 8, 12))]
-    stay, go = finish(ids, own, arrived, kept, head_gain[None])
+    part = add([own] + arrived)
+    part = add([part, swap(part, 4)])
+    stay, go = finish(part, swap(part, 8), kept, head_gain[None])
     normed = join([stay, partner(go, "guide", 0)])
-    return head(ids, spread(normed), guide_scale[None], w_head)
+    return head([normed] + [swap(normed, mask) for mask in (1, 2, 3)], guide_scale[None], w_head)
 
 
 def body(

time: 86.9 us -> 80.4 us (0.925)
  starting transfers between devices: 33.4 us -> 27.2 us
  waiting for transfers between devices: 33 us -> 37.5 us
  Pallas kernels: 18.6 us -> 14.5 us
    ppermute x24 -> x20, starting transfers between devices: 33.3 us -> 27.1 us  [swap(): return lax.ppermute(value, 'blk', pairs)]
    ppermute x24 -> x20, waiting for transfers between devices: 31.9 us -> 36.2 us  [swap(): return lax.ppermute(value, 'blk', pairs)]
    pallas_call x1, Pallas kernels: 6.55 us -> 5.39 us  [head(): pl.pallas_call(head_kernel, out_shape=jax.ShapeDtypeStruct((rows // 2, vo...]
  transfers between devices with their start and end apart: 25 -> 21, of which waited for: 21 -> 18; matrix products, arithmetic and copies ran while one was open for 0% -> 0% of each run, Pallas kernels for 0% -> 0%
where the time goes in v3:
time: 80.4 us; the launch traced here: 80.2 us
  waiting for transfers between devices  37.5 us (47%)
  starting transfers between devices  27.2 us (34%)
  Pallas kernels  14.5 us (18%)
  local copies, waits for them, and re-layouts  0.84 us (1%)
    ppermute x20, waiting for transfers between devices, swap(): return lax.ppermute(value, 'blk', pairs)  36.2 us
    ppermute x20, starting transfers between devices, swap(): return lax.ppermute(value, 'blk', pairs)  27.1 us
    pallas_call x1, Pallas kernels, attend(): pl.pallas_call(attend_kernel, out_shape=jax.ShapeDtypeStruct((slots, head...  5.69 us
    pallas_call x1, Pallas kernels, head(): pl.pallas_call(head_kernel, out_shape=jax.ShapeDtypeStruct((rows // 2, vo...  5.39 us
    pallas_call x1, Pallas kernels, feed(): pl.pallas_call(feed_kernel, out_shape=[jax.ShapeDtypeStruct(part, F32), j...  2.54 us
  transfers between devices with their start and end apart: 21, of which 18 were waited for; matrix products, arithmetic and copies ran while one was open for 0% of the time, Pallas kernels for 0%

profile of v3, /device:TPU:0, one launch (start us, length us, event | category | flops | bytes accessed | tf_op | source)
XLA Modules:
  0.0 80.2 jit_solution(5741007196858292917)
XLA Ops:
  0.0 5.7 %attend.1.refs_0_ = bf16[8,2048]{1,0:T(8,128)(2,1)} custom-call(s32[128]{0:T(128)} %perm_h.1, s32[1,128]{1,0:T(1,128)} %lengths_h.1, bf16[8,9216]{1,0:T(8,128)(2,1)} %queries_h.1, bf16[8,576]{1,0:T(8,128)(2,1)} %new_h.1, bf16[8,576,256]{2,1,0:T(8,128)(2,1)} %bitcast.25, bf16[16,512,128]{2,1,0:T(8,128)(2,1)} %w_uv.1), custom_call_target="tpu_custom_call" | custom-call | flops 15000000512 | bytes 45000000 | tf_op jit(solution)/shard_map/attend/pallas_call | solution.py:108
  5.7 5.1 %collective-permute-start.2 = (bf16[8,2048]{1,0:T(8,128)(2,1)}, bf16[8,2048]{1,0:T(8,128)(2,1)S(1)}, u32[]{:S(2)}, u32[]{:S(2)}) collective-permute-start(bf16[8,2048]{1,0:T(8,128)(2,1)} %attend.1.refs_0_), channel_id=1, source_target_pairs={{0,12},{1,13},{2,14},{3,15},{4,8},{5,9},{6,10},{7,11},{8,4},{9,5},... | collective-permute-start | bytes 98312 | tf_op jit(solution)/shard_map/ppermute | solution.py:26
  11.5 1.5 %collective-permute-done.2.refs_3_ = bf16[8,2048]{1,0:T(8,128)(2,1)S(1)} collective-permute-done((bf16[8,2048]{1,0:T(8,128)(2,1)}, bf16[8,2048]{1,0:T(8,128)(2,1)S(1)}, u32[]{:S(2)}, u32[]{:S(2)}) %collective-permute-start.2) | collective-permute-done | bytes 32800 | tf_op jit(solution)/shard_map/ppermute | solution.py:26
  12.9 2.9 %collective-permute-done.1.refs_2_ = bf16[8,2048]{1,0:T(8,128)(2,1)S(1)} collective-permute-done((bf16[8,2048]{1,0:T(8,128)(2,1)}, bf16[8,2048]{1,0:T(8,128)(2,1)S(1)}, u32[]{:S(2)}, u32[]{:S(2)}) %collective-permute-start.1) | collective-permute-done | bytes 32800 | tf_op jit(solution)/shard_map/ppermute | solution.py:26
  16.6 2.5 %collective-permute-start.5 = (bf16[32,2048]{1,0:T(8,128)(2,1)S(1)}, bf16[32,2048]{1,0:T(8,128)(2,1)S(1)}, u32[]{:S(2)}, u32[]{:S(2)}) collective-permute-start(bf16[32,2048]{1,0:T(8,128)(2,1)S(1)} %join.3.v0), channel_id=1, source_target_pairs={{0,3},{1,2},{2,1},{3,0},{4,7},{5,6},{6,5},{7,4},{8,11},{9,10},{10,... | collective-permute-start | bytes 393224 | tf_op jit(solution)/shard_map/ppermute | solution.py:26
  20.2 3.8 %collective-permute-done.5.v3 = bf16[32,2048]{1,0:T(8,128)(2,1)S(1)} collective-permute-done((bf16[32,2048]{1,0:T(8,128)(2,1)S(1)}, bf16[32,2048]{1,0:T(8,128)(2,1)S(1)}, u32[]{:S(2)}, u32[]{:S(2)}) %collective-permute-start.5) | collective-permute-done | bytes 131104 | tf_op jit(solution)/shard_map/ppermute | solution.py:26
  24.0 0.8 collective-permute-done.4.v2
  25.4 1.5 %collective-permute-start.8 = (bf16[128,128]{1,0:T(8,128)(2,1)S(1)}, bf16[128,128]{1,0:T(8,128)(2,1)S(1)}, u32[]{:S(2)}, u32[]{:S(2)}) collective-permute-start(bf16[128,128]{1,0:T(8,128)(2,1)S(1)} %project.1.refs_0_), channel_id=1, source_target_pairs={{0,12},{1,13},{2,14},{3,15},{4,8},{5,9},{6,10},{7,11},{8,4},{9,5},... | collective-permute-start | bytes 98312 | tf_op jit(solution)/shard_map/ppermute | solution.py:26
  27.5 2.3 %collective-permute-start.6 = (bf16[128,128]{1,0:T(8,128)(2,1)S(1)}, bf16[128,128]{1,0:T(8,128)(2,1)S(1)}, u32[]{:S(2)}, u32[]{:S(2)}) collective-permute-start(bf16[128,128]{1,0:T(8,128)(2,1)S(1)} %project.1.refs_0_), channel_id=1, source_target_pairs={{0,4},{1,5},{2,6},{3,7},{4,0},{5,1},{6,2},{7,3},{8,12},{9,13},{10,... | collective-permute-start | bytes 98312 | tf_op jit(solution)/shard_map/ppermute | solution.py:26
  29.8 1.3 %collective-permute-done.8.refs_3_ = bf16[128,128]{1,0:T(8,128)(2,1)S(1)} collective-permute-done((bf16[128,128]{1,0:T(8,128)(2,1)S(1)}, bf16[128,128]{1,0:T(8,128)(2,1)S(1)}, u32[]{:S(2)}, u32[]{:S(2)}) %collective-permute-start.8) | collective-permute-done | bytes 32800 | tf_op jit(solution)/shard_map/ppermute | solution.py:26
  32.0 1.5 %collective-permute-start.11 = (bf16[512,128]{1,0:T(8,128)(2,1)S(1)}, bf16[512,128]{1,0:T(8,128)(2,1)S(1)}, u32[]{:S(2)}, u32[]{:S(2)}) collective-permute-start(bf16[512,128]{1,0:T(8,128)(2,1)S(1)} %join.4), channel_id=1, source_target_pairs={{0,3},{1,2},{2,1},{3,0},{4,7},{5,6},{6,5},{7,4},{8,11},{9,10},{10,... | collective-permute-start | bytes 393224 | tf_op jit(solution)/shard_map/ppermute | solution.py:26
  33.5 1.5 %collective-permute-start.10 = (bf16[512,128]{1,0:T(8,128)(2,1)S(1)}, bf16[512,128]{1,0:T(8,128)(2,1)S(1)}, u32[]{:S(2)}, u32[]{:S(2)}) collective-permute-start(bf16[512,128]{1,0:T(8,128)(2,1)S(1)} %join.4), channel_id=1, source_target_pairs={{0,2},{1,3},{2,0},{3,1},{4,6},{5,7},{6,4},{7,5},{8,10},{9,11},{10,... | collective-permute-start | bytes 393224 | tf_op jit(solution)/shard_map/ppermute | solution.py:26
  35.6 2.5 %collective-permute-done.11 = bf16[512,128]{1,0:T(8,128)(2,1)S(1)} collective-permute-done((bf16[512,128]{1,0:T(8,128)(2,1)S(1)}, bf16[512,128]{1,0:T(8,128)(2,1)S(1)}, u32[]{:S(2)}, u32[]{:S(2)}) %collective-permute-start.11) | collective-permute-done | bytes 131104 | tf_op jit(solution)/shard_map/ppermute | solution.py:26
  38.0 1.3 %collective-permute-done.10 = bf16[512,128]{1,0:T(8,128)(2,1)S(1)} collective-permute-done((bf16[512,128]{1,0:T(8,128)(2,1)S(1)}, bf16[512,128]{1,0:T(8,128)(2,1)S(1)}, u32[]{:S(2)}, u32[]{:S(2)}) %collective-permute-start.10) | collective-permute-done | bytes 131104 | tf_op jit(solution)/shard_map/ppermute | solution.py:26
  40.1 2.5 %feed.1 = (f32[32,2048]{1,0:T(8,128)S(1)}, bf16[32,2048]{1,0:T(8,128)(2,1)S(1)}, bf16[32,2048]{1,0:T(8,128)(2,1)S(1)}, bf16[32,2048]{1,0:T(8,128)(2,1)S(1)}, f32[32,2048]{1,0:T(8,128)S(1)}) custom-call(bf16[4,128,128]{2,1,0:T(8,128)(2,1)S(1)} %bitcast.17, bf16[4,128,128]{2,1,0:T(8,128)(2,1)S(1)} %bitcast.20, bf16[4,128,128]{2,1,0:T(8,128)(2,1)S(1)} %bitcast.19, ...), custom_call_target="tpu_custom_call" | custom-call | flops 15000000512 | bytes 45000000 | tf_op jit(solution)/shard_map/feed/pallas_call | solution.py:198
  42.6 0.9 %collective-permute-start.12 = (bf16[32,2048]{1,0:T(8,128)(2,1)S(1)}, bf16[32,2048]{1,0:T(8,128)(2,1)S(1)}, u32[]{:S(2)}, u32[]{:S(2)}) collective-permute-start(bf16[32,2048]{1,0:T(8,128)(2,1)S(1)} %get-tuple-element.13), channel_id=1, source_target_pairs={{0,1},{1,0},{2,3},{3,2},{4,5},{5,4},{6,7},{7,6},{8,9},{9,8},{10,11... | collective-permute-start | bytes 393224 | tf_op jit(solution)/shard_map/ppermute | solution.py:26
  43.5 1.1 %collective-permute-start.13 = (bf16[32,2048]{1,0:T(8,128)(2,1)S(1)}, bf16[32,2048]{1,0:T(8,128)(2,1)S(1)}, u32[]{:S(2)}, u32[]{:S(2)}) collective-permute-start(bf16[32,2048]{1,0:T(8,128)(2,1)S(1)} %get-tuple-element.14), channel_id=1, source_target_pairs={{0,2},{1,3},{2,0},{3,1},{4,6},{5,7},{6,4},{7,5},{8,10},{9,11},{10,... | collective-permute-start | bytes 393224 | tf_op jit(solution)/shard_map/ppermute | solution.py:26
  44.7 1.5 %collective-permute-start.14 = (bf16[32,2048]{1,0:T(8,128)(2,1)S(1)}, bf16[32,2048]{1,0:T(8,128)(2,1)S(1)}, u32[]{:S(2)}, u32[]{:S(2)}) collective-permute-start(bf16[32,2048]{1,0:T(8,128)(2,1)S(1)} %get-tuple-element.15), channel_id=1, source_target_pairs={{0,3},{1,2},{2,1},{3,0},{4,7},{5,6},{6,5},{7,4},{8,11},{9,10},{10,... | collective-permute-start | bytes 393224 | tf_op jit(solution)/shard_map/ppermute | solution.py:26
  46.2 1.5 %collective-permute-done.12.refs_1_ = bf16[32,2048]{1,0:T(8,128)(2,1)S(1)} collective-permute-done((bf16[32,2048]{1,0:T(8,128)(2,1)S(1)}, bf16[32,2048]{1,0:T(8,128)(2,1)S(1)}, u32[]{:S(2)}, u32[]{:S(2)}) %collective-permute-start.12) | collective-permute-done | bytes 131104 | tf_op jit(solution)/shard_map/ppermute | solution.py:26
  47.6 0.9 %collective-permute-done.13.refs_2_ = bf16[32,2048]{1,0:T(8,128)(2,1)S(1)} collective-permute-done((bf16[32,2048]{1,0:T(8,128)(2,1)S(1)}, bf16[32,2048]{1,0:T(8,128)(2,1)S(1)}, u32[]{:S(2)}, u32[]{:S(2)}) %collective-permute-start.13) | collective-permute-done | bytes 131104 | tf_op jit(solution)/shard_map/ppermute | solution.py:26
  48.5 2.0 %collective-permute-done.14.refs_3_ = bf16[32,2048]{1,0:T(8,128)(2,1)S(1)} collective-permute-done((bf16[32,2048]{1,0:T(8,128)(2,1)S(1)}, bf16[32,2048]{1,0:T(8,128)(2,1)S(1)}, u32[]{:S(2)}, u32[]{:S(2)}) %collective-permute-start.14) | collective-permute-done | bytes 131104 | tf_op jit(solution)/shard_map/ppermute | solution.py:26
  50.6 1.7 %collective-permute-start.15 = (bf16[32,2048]{1,0:T(8,128)(2,1)S(1)}, bf16[32,2048]{1,0:T(8,128)(2,1)S(1)}, u32[]{:S(2)}, u32[]{:S(2)}) collective-permute-start(bf16[32,2048]{1,0:T(8,128)(2,1)S(1)} %add.2.refs_0_), channel_id=1, source_target_pairs={{0,4},{1,5},{2,6},{3,7},{4,0},{5,1},{6,2},{7,3},{8,12},{9,13},{10,... | collective-permute-start | bytes 393224 | tf_op jit(solution)/shard_map/ppermute | solution.py:26
  52.3 4.1 %collective-permute-done.15.refs_1_ = bf16[32,2048]{1,0:T(8,128)(2,1)S(1)} collective-permute-done((bf16[32,2048]{1,0:T(8,128)(2,1)S(1)}, bf16[32,2048]{1,0:T(8,128)(2,1)S(1)}, u32[]{:S(2)}, u32[]{:S(2)}) %collective-permute-start.15) | collective-permute-done | bytes 131104 | tf_op jit(solution)/shard_map/ppermute | solution.py:26
  56.5 0.9 %collective-permute-start.16 = (bf16[32,2048]{1,0:T(8,128)(2,1)S(1)}, bf16[32,2048]{1,0:T(8,128)(2,1)S(1)}, u32[]{:S(2)}, u32[]{:S(2)}) collective-permute-start(bf16[32,2048]{1,0:T(8,128)(2,1)S(1)} %add.3.own), channel_id=1, source_target_pairs={{0,8},{1,9},{2,10},{3,11},{4,12},{5,13},{6,14},{7,15},{8,0},{9,1},... | collective-permute-start | bytes 393224 | tf_op jit(solution)/shard_map/ppermute | solution.py:26
  57.4 6.4 %collective-permute-done.16.other = bf16[32,2048]{1,0:T(8,128)(2,1)S(1)} collective-permute-done((bf16[32,2048]{1,0:T(8,128)(2,1)S(1)}, bf16[32,2048]{1,0:T(8,128)(2,1)S(1)}, u32[]{:S(2)}, u32[]{:S(2)}) %collective-permute-start.16) | collective-permute-done | bytes 131104 | tf_op jit(solution)/shard_map/ppermute | solution.py:26
  64.2 1.2 %collective-permute-done.17.refs_1_ = bf16[16,2048]{1,0:T(8,128)(2,1)S(1)} collective-permute-done((bf16[16,2048]{1,0:T(8,128)(2,1)S(1)}, bf16[16,2048]{1,0:T(8,128)(2,1)S(1)}, u32[]{:S(2)}, u32[]{:S(2)}) %collective-permute-start.17) | collective-permute-done | bytes 65568 | tf_op jit(solution)/shard_map/ppermute | solution.py:21
  65.4 1.5 %collective-permute-start.20 = (bf16[32,2048]{1,0:T(8,128)(2,1)S(1)}, bf16[32,2048]{1,0:T(8,128)(2,1)S(1)}, u32[]{:S(2)}, u32[]{:S(2)}) collective-permute-start(bf16[32,2048]{1,0:T(8,128)(2,1)S(1)} %join.5.r0), channel_id=1, source_target_pairs={{0,3},{1,2},{2,1},{3,0},{4,7},{5,6},{6,5},{7,4},{8,11},{9,10},{10,... | collective-permute-start | bytes 393224 | tf_op jit(solution)/shard_map/ppermute | solution.py:26
  66.9 1.1 %collective-permute-start.19 = (bf16[32,2048]{1,0:T(8,128)(2,1)S(1)}, bf16[32,2048]{1,0:T(8,128)(2,1)S(1)}, u32[]{:S(2)}, u32[]{:S(2)}) collective-permute-start(bf16[32,2048]{1,0:T(8,128)(2,1)S(1)} %join.5.r0), channel_id=1, source_target_pairs={{0,2},{1,3},{2,0},{3,1},{4,6},{5,7},{6,4},{7,5},{8,10},{9,11},{10,... | collective-permute-start | bytes 393224 | tf_op jit(solution)/shard_map/ppermute | solution.py:26
  68.1 0.9 %collective-permute-start.18 = (bf16[32,2048]{1,0:T(8,128)(2,1)S(1)}, bf16[32,2048]{1,0:T(8,128)(2,1)S(1)}, u32[]{:S(2)}, u32[]{:S(2)}) collective-permute-start(bf16[32,2048]{1,0:T(8,128)(2,1)S(1)} %join.5.r0), channel_id=1, source_target_pairs={{0,1},{1,0},{2,3},{3,2},{4,5},{5,4},{6,7},{7,6},{8,9},{9,8},{10,11... | collective-permute-start | bytes 393224 | tf_op jit(solution)/shard_map/ppermute | solution.py:26
  69.0 3.8 %collective-permute-done.20.r3 = bf16[32,2048]{1,0:T(8,128)(2,1)S(1)} collective-permute-done((bf16[32,2048]{1,0:T(8,128)(2,1)S(1)}, bf16[32,2048]{1,0:T(8,128)(2,1)S(1)}, u32[]{:S(2)}, u32[]{:S(2)}) %collective-permute-start.20) | collective-permute-done | bytes 131104 | tf_op jit(solution)/shard_map/ppermute | solution.py:26
  72.8 2.0 %collective-permute-done.19.r2 = bf16[32,2048]{1,0:T(8,128)(2,1)S(1)} collective-permute-done((bf16[32,2048]{1,0:T(8,128)(2,1)S(1)}, bf16[32,2048]{1,0:T(8,128)(2,1)S(1)}, u32[]{:S(2)}, u32[]{:S(2)}) %collective-permute-start.19) | collective-permute-done | bytes 131104 | tf_op jit(solution)/shard_map/ppermute | solution.py:26
  74.8 5.4 %head.1 = bf16[64,6400]{1,0:T(8,128)(2,1)} custom-call(bf16[32,2048]{1,0:T(8,128)(2,1)S(1)} %join.5.r0, bf16[32,2048]{1,0:T(8,128)(2,1)S(1)} %collective-permute-done.18.r1, bf16[32,2048]{1,0:T(8,128)(2,1)S(1)} %collective-permute-done.19.r2, bf16[32,2048]{1,0:T(8,128)(2,1)S(1)} %collective-permute-done.20.r3, f32[1,128]{1,0:T(1,128)S(1)} %bitcast.24, ...), custom_call_target="tpu_custom_call" | custom-call | flops 8000000000 | bytes 24000000 | tf_op jit(solution)/shard_map/head/pallas_call | solution.py:300
  (55 shorter events, 6.2 us)
Async XLA Ops:
  0.0 24.8 %copy-start.8 = (s32[128]{0:T(128)S(1)}, s32[128]{0:T(128)}, u32[]{:S(2)}) copy-start(s32[128]{0:T(128)} %perm_h.1) | copy-start | bytes 1540
  5.7 19.1 %copy-start.3 = (bf16[2048,128]{1,0:T(8,128)(2,1)S(1)}, bf16[2048,128]{1,0:T(8,128)(2,1)}, u32[]{:S(2)}) copy-start(bf16[2048,128]{1,0:T(8,128)(2,1)} %w_out.1) | copy-start | bytes 1572868
  5.7 19.0 %copy-start.4 = (bf16[128,128]{1,0:T(8,128)(2,1)S(1)}, bf16[128,128]{1,0:T(8,128)(2,1)}, u32[]{:S(2)}) copy-start(bf16[128,128]{1,0:T(8,128)(2,1)} %x_cols.1) | copy-start | bytes 98308
  5.7 7.2 %collective-permute-start.2 = (bf16[8,2048]{1,0:T(8,128)(2,1)}, bf16[8,2048]{1,0:T(8,128)(2,1)S(1)}, u32[]{:S(2)}, u32[]{:S(2)}) collective-permute-start(bf16[8,2048]{1,0:T(8,128)(2,1)} %attend.1.refs_0_), channel_id=1, source_target_pairs={{0,12},{1,13},{2,14},{3,15},{4,8},{5,9},{6,10},{7,11},{8,4},{9,5},... | collective-permute-start | bytes 98312 | tf_op jit(solution)/shard_map/ppermute | solution.py:26
  10.8 5.0 %collective-permute-start.1 = (bf16[8,2048]{1,0:T(8,128)(2,1)}, bf16[8,2048]{1,0:T(8,128)(2,1)S(1)}, u32[]{:S(2)}, u32[]{:S(2)}) collective-permute-start(bf16[8,2048]{1,0:T(8,128)(2,1)} %attend.1.refs_0_), channel_id=1, source_target_pairs={{0,8},{1,9},{2,10},{3,11},{4,12},{5,13},{6,14},{7,15},{8,0},{9,1},... | collective-permute-start | bytes 98312 | tf_op jit(solution)/shard_map/ppermute | solution.py:26
  10.8 5.0 %collective-permute-start = (bf16[8,2048]{1,0:T(8,128)(2,1)}, bf16[8,2048]{1,0:T(8,128)(2,1)S(1)}, u32[]{:S(2)}, u32[]{:S(2)}) collective-permute-start(bf16[8,2048]{1,0:T(8,128)(2,1)} %attend.1.refs_0_), channel_id=1, source_target_pairs={{0,4},{1,5},{2,6},{3,7},{4,0},{5,1},{6,2},{7,3},{8,12},{9,13},{10,... | collective-permute-start | bytes 98312 | tf_op jit(solution)/shard_map/ppermute | solution.py:26
  16.6 7.3 %collective-permute-start.5 = (bf16[32,2048]{1,0:T(8,128)(2,1)S(1)}, bf16[32,2048]{1,0:T(8,128)(2,1)S(1)}, u32[]{:S(2)}, u32[]{:S(2)}) collective-permute-start(bf16[32,2048]{1,0:T(8,128)(2,1)S(1)} %join.3.v0), channel_id=1, source_target_pairs={{0,3},{1,2},{2,1},{3,0},{4,7},{5,6},{6,5},{7,4},{8,11},{9,10},{10,... | collective-permute-start | bytes 393224 | tf_op jit(solution)/shard_map/ppermute | solution.py:26
  19.2 5.6 %collective-permute-start.4 = (bf16[32,2048]{1,0:T(8,128)(2,1)S(1)}, bf16[32,2048]{1,0:T(8,128)(2,1)S(1)}, u32[]{:S(2)}, u32[]{:S(2)}) collective-permute-start(bf16[32,2048]{1,0:T(8,128)(2,1)S(1)} %join.3.v0), channel_id=1, source_target_pairs={{0,2},{1,3},{2,0},{3,1},{4,6},{5,7},{6,4},{7,5},{8,10},{9,11},{10,... | collective-permute-start | bytes 393224 | tf_op jit(solution)/shard_map/ppermute | solution.py:26
  19.7 5.1 %collective-permute-start.3 = (bf16[32,2048]{1,0:T(8,128)(2,1)S(1)}, bf16[32,2048]{1,0:T(8,128)(2,1)S(1)}, u32[]{:S(2)}, u32[]{:S(2)}) collective-permute-start(bf16[32,2048]{1,0:T(8,128)(2,1)S(1)} %join.3.v0), channel_id=1, source_target_pairs={{0,1},{1,0},{2,3},{3,2},{4,5},{5,4},{6,7},{7,6},{8,9},{9,8},{10,11... | collective-permute-start | bytes 393224 | tf_op jit(solution)/shard_map/ppermute | solution.py:26
  24.8 15.3 %copy-start.1 = (bf16[2048,684]{0,1:T(8,128)(2,1)S(1)}, bf16[2048,684]{0,1:T(8,128)(2,1)}, u32[]{:S(2)}) copy-start(bf16[2048,684]{0,1:T(8,128)(2,1)} %param.26) | copy-start | bytes 8404996
  24.8 15.2 %copy-start.2 = (bf16[684,2048]{1,0:T(8,128)(2,1)S(1)}, bf16[684,2048]{1,0:T(8,128)(2,1)}, u32[]{:S(2)}) copy-start(bf16[684,2048]{1,0:T(8,128)(2,1)} %w_down.1) | copy-start | bytes 8404996
  25.4 14.7 %copy-start = (bf16[2048,684]{0,1:T(8,128)(2,1)S(1)}, bf16[2048,684]{0,1:T(8,128)(2,1)}, u32[]{:S(2)}) copy-start(bf16[2048,684]{0,1:T(8,128)(2,1)} %param.25) | copy-start | bytes 8404996
  25.4 14.7 %copy-start.6 = (f32[2048]{0:T(1024)S(1)}, f32[2048]{0:T(1024)}, u32[]{:S(2)}) copy-start(f32[2048]{0:T(1024)} %param.24) | copy-start | bytes 24580
  25.4 5.8 %collective-permute-start.8 = (bf16[128,128]{1,0:T(8,128)(2,1)S(1)}, bf16[128,128]{1,0:T(8,128)(2,1)S(1)}, u32[]{:S(2)}, u32[]{:S(2)}) collective-permute-start(bf16[128,128]{1,0:T(8,128)(2,1)S(1)} %project.1.refs_0_), channel_id=1, source_target_pairs={{0,12},{1,13},{2,14},{3,15},{4,8},{5,9},{6,10},{7,11},{8,4},{9,5},... | collective-permute-start | bytes 98312 | tf_op jit(solution)/shard_map/ppermute | solution.py:26
  26.8 4.8 %collective-permute-start.7 = (bf16[128,128]{1,0:T(8,128)(2,1)S(1)}, bf16[128,128]{1,0:T(8,128)(2,1)S(1)}, u32[]{:S(2)}, u32[]{:S(2)}) collective-permute-start(bf16[128,128]{1,0:T(8,128)(2,1)S(1)} %project.1.refs_0_), channel_id=1, source_target_pairs={{0,8},{1,9},{2,10},{3,11},{4,12},{5,13},{6,14},{7,15},{8,0},{9,1},... | collective-permute-start | bytes 98312 | tf_op jit(solution)/shard_map/ppermute | solution.py:26
  27.5 4.5 %collective-permute-start.6 = (bf16[128,128]{1,0:T(8,128)(2,1)S(1)}, bf16[128,128]{1,0:T(8,128)(2,1)S(1)}, u32[]{:S(2)}, u32[]{:S(2)}) collective-permute-start(bf16[128,128]{1,0:T(8,128)(2,1)S(1)} %project.1.refs_0_), channel_id=1, source_target_pairs={{0,4},{1,5},{2,6},{3,7},{4,0},{5,1},{6,2},{7,3},{8,12},{9,13},{10,... | collective-permute-start | bytes 98312 | tf_op jit(solution)/shard_map/ppermute | solution.py:26
  32.0 6.0 %collective-permute-start.11 = (bf16[512,128]{1,0:T(8,128)(2,1)S(1)}, bf16[512,128]{1,0:T(8,128)(2,1)S(1)}, u32[]{:S(2)}, u32[]{:S(2)}) collective-permute-start(bf16[512,128]{1,0:T(8,128)(2,1)S(1)} %join.4), channel_id=1, source_target_pairs={{0,3},{1,2},{2,1},{3,0},{4,7},{5,6},{6,5},{7,4},{8,11},{9,10},{10,... | collective-permute-start | bytes 393224 | tf_op jit(solution)/shard_map/ppermute | solution.py:26
  33.5 5.8 %collective-permute-start.10 = (bf16[512,128]{1,0:T(8,128)(2,1)S(1)}, bf16[512,128]{1,0:T(8,128)(2,1)S(1)}, u32[]{:S(2)}, u32[]{:S(2)}) collective-permute-start(bf16[512,128]{1,0:T(8,128)(2,1)S(1)} %join.4), channel_id=1, source_target_pairs={{0,2},{1,3},{2,0},{3,1},{4,6},{5,7},{6,4},{7,5},{8,10},{9,11},{10,... | collective-permute-start | bytes 393224 | tf_op jit(solution)/shard_map/ppermute | solution.py:26
  35.1 5.0 %collective-permute-start.9 = (bf16[512,128]{1,0:T(8,128)(2,1)S(1)}, bf16[512,128]{1,0:T(8,128)(2,1)S(1)}, u32[]{:S(2)}, u32[]{:S(2)}) collective-permute-start(bf16[512,128]{1,0:T(8,128)(2,1)S(1)} %join.4), channel_id=1, source_target_pairs={{0,1},{1,0},{2,3},{3,2},{4,5},{5,4},{6,7},{7,6},{8,9},{9,8},{10,11... | collective-permute-start | bytes 393224 | tf_op jit(solution)/shard_map/ppermute | solution.py:26
  42.6 5.0 %collective-permute-start.12 = (bf16[32,2048]{1,0:T(8,128)(2,1)S(1)}, bf16[32,2048]{1,0:T(8,128)(2,1)S(1)}, u32[]{:S(2)}, u32[]{:S(2)}) collective-permute-start(bf16[32,2048]{1,0:T(8,128)(2,1)S(1)} %get-tuple-element.13), channel_id=1, source_target_pairs={{0,1},{1,0},{2,3},{3,2},{4,5},{5,4},{6,7},{7,6},{8,9},{9,8},{10,11... | collective-permute-start | bytes 393224 | tf_op jit(solution)/shard_map/ppermute | solution.py:26
  43.5 5.0 %collective-permute-start.13 = (bf16[32,2048]{1,0:T(8,128)(2,1)S(1)}, bf16[32,2048]{1,0:T(8,128)(2,1)S(1)}, u32[]{:S(2)}, u32[]{:S(2)}) collective-permute-start(bf16[32,2048]{1,0:T(8,128)(2,1)S(1)} %get-tuple-element.14), channel_id=1, source_target_pairs={{0,2},{1,3},{2,0},{3,1},{4,6},{5,7},{6,4},{7,5},{8,10},{9,11},{10,... | collective-permute-start | bytes 393224 | tf_op jit(solution)/shard_map/ppermute | solution.py:26
  44.7 5.9 %collective-permute-start.14 = (bf16[32,2048]{1,0:T(8,128)(2,1)S(1)}, bf16[32,2048]{1,0:T(8,128)(2,1)S(1)}, u32[]{:S(2)}, u32[]{:S(2)}) collective-permute-start(bf16[32,2048]{1,0:T(8,128)(2,1)S(1)} %get-tuple-element.15), channel_id=1, source_target_pairs={{0,3},{1,2},{2,1},{3,0},{4,7},{5,6},{6,5},{7,4},{8,11},{9,10},{10,... | collective-permute-start | bytes 393224 | tf_op jit(solution)/shard_map/ppermute | solution.py:26
  50.6 13.3 %copy-start.7 = (f32[2048]{0:T(1024)S(1)}, f32[2048]{0:T(1024)}, u32[]{:S(2)}) copy-start(f32[2048]{0:T(1024)} %param.28) | copy-start | bytes 24580
  50.6 5.9 %collective-permute-start.15 = (bf16[32,2048]{1,0:T(8,128)(2,1)S(1)}, bf16[32,2048]{1,0:T(8,128)(2,1)S(1)}, u32[]{:S(2)}, u32[]{:S(2)}) collective-permute-start(bf16[32,2048]{1,0:T(8,128)(2,1)S(1)} %add.2.refs_0_), channel_id=1, source_target_pairs={{0,4},{1,5},{2,6},{3,7},{4,0},{5,1},{6,2},{7,3},{8,12},{9,13},{10,... | collective-permute-start | bytes 393224 | tf_op jit(solution)/shard_map/ppermute | solution.py:26
  56.5 7.3 %collective-permute-start.16 = (bf16[32,2048]{1,0:T(8,128)(2,1)S(1)}, bf16[32,2048]{1,0:T(8,128)(2,1)S(1)}, u32[]{:S(2)}, u32[]{:S(2)}) collective-permute-start(bf16[32,2048]{1,0:T(8,128)(2,1)S(1)} %add.3.own), channel_id=1, source_target_pairs={{0,8},{1,9},{2,10},{3,11},{4,12},{5,13},{6,14},{7,15},{8,0},{9,1},... | collective-permute-start | bytes 393224 | tf_op jit(solution)/shard_map/ppermute | solution.py:26
  63.8 10.9 %slice-start.3 = ((s8[26214400]{0:T(1024)(128)(4,1)}), s8[4194304]{0:T(1024)(128)(4,1)S(1)}, s32[]{:S(2)}) async-start(s8[26214400]{0:T(1024)(128)(4,1)} %bitcast.13), calls=%async_computation.3 | async-start | bytes 8388608
  63.9 10.9 %slice-start.4 = ((s8[26214400]{0:T(1024)(128)(4,1)}), s8[4194304]{0:T(1024)(128)(4,1)S(1)}, s32[]{:S(2)}) async-start(s8[26214400]{0:T(1024)(128)(4,1)} %bitcast.13), calls=%async_computation.4 | async-start | bytes 8388608
  63.9 10.9 %slice-start.5 = ((s8[26214400]{0:T(1024)(128)(4,1)}), s8[4194304]{0:T(1024)(128)(4,1)S(1)}, s32[]{:S(2)}) async-start(s8[26214400]{0:T(1024)(128)(4,1)} %bitcast.13), calls=%async_computation.5 | async-start | bytes 8388608
  64.1 1.3 %collective-permute-start.17 = (bf16[16,2048]{1,0:T(8,128)(2,1)S(1)}, bf16[16,2048]{1,0:T(8,128)(2,1)S(1)}, u32[]{:S(2)}, u32[]{:S(2)}) collective-permute-start(bf16[16,2048]{1,0:T(8,128)(2,1)S(1)} %get-tuple-element.18), channel_id=1, source_target_pairs={{0,16},{16,0},{1,17},{17,1},{2,18},{18,2},{3,19},{19,3},{4,20},{20... | collective-permute-start | bytes 196616 | tf_op jit(solution)/shard_map/ppermute | solution.py:21
  65.4 7.3 %collective-permute-start.20 = (bf16[32,2048]{1,0:T(8,128)(2,1)S(1)}, bf16[32,2048]{1,0:T(8,128)(2,1)S(1)}, u32[]{:S(2)}, u32[]{:S(2)}) collective-permute-start(bf16[32,2048]{1,0:T(8,128)(2,1)S(1)} %join.5.r0), channel_id=1, source_target_pairs={{0,3},{1,2},{2,1},{3,0},{4,7},{5,6},{6,5},{7,4},{8,11},{9,10},{10,... | collective-permute-start | bytes 393224 | tf_op jit(solution)/shard_map/ppermute | solution.py:26
  66.9 7.8 %collective-permute-start.19 = (bf16[32,2048]{1,0:T(8,128)(2,1)S(1)}, bf16[32,2048]{1,0:T(8,128)(2,1)S(1)}, u32[]{:S(2)}, u32[]{:S(2)}) collective-permute-start(bf16[32,2048]{1,0:T(8,128)(2,1)S(1)} %join.5.r0), channel_id=1, source_target_pairs={{0,2},{1,3},{2,0},{3,1},{4,6},{5,7},{6,4},{7,5},{8,10},{9,11},{10,... | collective-permute-start | bytes 393224 | tf_op jit(solution)/shard_map/ppermute | solution.py:26
  68.1 6.7 %collective-permute-start.18 = (bf16[32,2048]{1,0:T(8,128)(2,1)S(1)}, bf16[32,2048]{1,0:T(8,128)(2,1)S(1)}, u32[]{:S(2)}, u32[]{:S(2)}) collective-permute-start(bf16[32,2048]{1,0:T(8,128)(2,1)S(1)} %join.5.r0), channel_id=1, source_target_pairs={{0,1},{1,0},{2,3},{3,2},{4,5},{5,4},{6,7},{7,6},{8,9},{9,8},{10,11... | collective-permute-start | bytes 393224 | tf_op jit(solution)/shard_map/ppermute | solution.py:26
  (6 other events, 55.2 us)

commit v4 on v3

--- a/solution.py
+++ b/solution.py
@@ -13,6 +13,12 @@
 TN = (((0,), (0,)), ((), ()))
 VM = pl.BlockSpec(memory_space=pltpu.VMEM)
 HB = pl.BlockSpec(memory_space=pltpu.HBM)
+
+
+def across(value, mask):
+    chips = lax.axis_size("blk")
+    pairs = [(d, (d ^ mask) ^ chips) for d in range(2 * chips)]
+    return lax.ppermute(value, ("guide", "blk"), pairs)
 
 
 def partner(value, axis, apart):
@@ -79,9 +85,10 @@
     live = jnp.zeros((rows, 1), jnp.int32)
     for s in range(slots):
         live = jnp.where(slot_of == s, lengths[0, perm[first + s]], live)
+    for copy in copies:
+        copy.wait()
     scores = jnp.zeros((rows, positions), F32)
     for s in range(slots):
-        copies[s].wait()
         scores = jnp.where(slot_of == s, dot(q, keys[s], NN), scores)
     mask = iota((rows, positions), 1) < live
     scores = jnp.where(mask, scores * scale, -1e30)
@@ -165,7 +172,7 @@
 
 
 def feed_kernel(
-    r0, r1, r2, r3, gain, w_gate, w_up, w_down, own, c1, c2, c3, kept, full, acc
+    r0, r1, r2, r3, gain, w_gate, w_up, w_down, own, c1, c2, c3, stay, go, full, acc
 ):
     blk = lax.axis_index("blk")
     groups, rows, cols = r0.shape
@@ -188,7 +195,11 @@
     for q, ref in enumerate((own, c1, c2, c3)):
         at = pl.multiple_of((low ^ q) * chunk, chunk)
         ref[...] = acc[pl.ds(at, chunk), :].astype(ref.dtype)
-    kept[...] = full[pl.ds(pl.multiple_of(low * chunk, chunk), chunk), :]
+    first = full[pl.ds(pl.multiple_of(low * chunk, chunk), chunk // 2), :]
+    last = full[pl.ds(pl.multiple_of(low * chunk + chunk // 2, chunk // 2), chunk // 2), :]
+    lower = lax.axis_index("guide") == 0
+    stay[...] = jnp.where(lower, first, last).astype(BF)
+    go[...] = jnp.where(lower, last, first).astype(BF)
 
 
 def feed(pieces, gain, w_gate, w_up, w_down):
@@ -202,10 +213,11 @@
             jax.ShapeDtypeStruct(part, BF),
             jax.ShapeDtypeStruct(part, BF),
             jax.ShapeDtypeStruct(part, BF),
-            jax.ShapeDtypeStruct(part, F32),
+            jax.ShapeDtypeStruct((rows // 8, width), BF),
+            jax.ShapeDtypeStruct((rows // 8, width), BF),
         ],
         in_specs=[VM] * 8,
-        out_specs=[VM] * 5,
+        out_specs=[VM] * 6,
         scratch_shapes=[pltpu.VMEM((rows, width), F32), pltpu.VMEM((rows, width), F32)],
         compiler_params=pltpu.CompilerParams(vmem_limit_bytes=8 << 20),
         cost_estimate=cost(15),
@@ -213,48 +225,41 @@
     )(*pieces, gain, w_gate, w_up, w_down)
 
 
-def sum_kernel(*refs):
-    out = refs[-1]
-    total = refs[0][...].astype(F32)
-    for ref in refs[1:-1]:
-        total += ref[...].astype(F32)
-    out[...] = total.astype(out.dtype)
-
-
-def add(parts):
+def part_kernel(own, p1, p2, p3, stay, go):
+    total = own[...] + p1[...].astype(F32) + p2[...].astype(F32) + p3[...].astype(F32)
+    half = total.shape[0] // 2
+    first, last = total[:half], total[half:]
+    lower = lax.axis_index("guide") == 0
+    stay[...] = jnp.where(lower, first, last).astype(BF)
+    go[...] = jnp.where(lower, last, first).astype(BF)
+
+
+def pair_kernel(a, b, c, d, out):
+    half = a.shape[0]
+    out[:half, :] = (a[...].astype(F32) + b[...].astype(F32)).astype(BF)
+    out[half:, :] = (c[...].astype(F32) + d[...].astype(F32)).astype(BF)
+
+
+def finish_kernel(own, other, stay, came, gain, out):
+    half = stay.shape[0]
+    total = own[...].astype(F32) + other[...].astype(F32)
+    for k, ref in enumerate((stay, came)):
+        at = slice(k * half, (k + 1) * half)
+        after = (ref[...].astype(F32) + total[at]).astype(BF).astype(F32)
+        meansq = jnp.mean(after * after, axis=1, keepdims=True)
+        out[at, :] = (after * lax.rsqrt(meansq + 1e-06) * gain[...]).astype(BF)
+
+
+def small(kernel, name, shapes, *args):
     return pl.pallas_call(
-        sum_kernel,
-        out_shape=jax.ShapeDtypeStruct(parts[0].shape, BF),
-        in_specs=[VM] * len(parts),
-        out_specs=VM,
+        kernel,
+        out_shape=[jax.ShapeDtypeStruct(shape, BF) for shape in shapes],
+        in_specs=[VM] * len(args),
+        out_specs=[VM] * len(shapes),
         compiler_params=pltpu.CompilerParams(vmem_limit_bytes=2 << 20),
         cost_estimate=cost(20),
-        name="add",
-    )(*parts)
-
-
-def finish_kernel(own, other, kept, gain, stay, go):
-    after = (kept[...] + (own[...].astype(F32) + other[...].astype(F32))).astype(BF).astype(F32)
-    meansq = jnp.mean(after * after, axis=1, keepdims=True)
-    normed = (after * lax.rsqrt(meansq + 1e-06) * gain[...]).astype(BF)
-    half = normed.shape[0] // 2
-    first, last = normed[:half], normed[half:]
-    lower = lax.axis_index("guide") == 0
-    stay[...] = jnp.where(lower, first, last)
-    go[...] = jnp.where(lower, last, first)
-
-
-def finish(own, other, kept, gain):
-    rows, width = own.shape
-    return pl.pallas_call(
-        finish_kernel,
-        out_shape=[jax.ShapeDtypeStruct((rows // 2, width), BF)] * 2,
-        in_specs=[VM] * 4,
-        out_specs=[VM] * 2,
-        compiler_params=pltpu.CompilerParams(vmem_limit_bytes=2 << 20),
-        cost_estimate=cost(20),
-        name="finish",
-    )(own, other, kept, gain)
+        name=name,
+    )(*args)
 
 
 def head_kernel(r0, r1, r2, r3, scale, w_head, out, came, full, factor, done, sems):
@@ -335,8 +340,8 @@
     )(*parts)
 
 
-def spread(value):
-    group = join([value] + [swap(value, mask) for mask in (4, 8, 12)])
+def spread(value, own):
+    group = join([own] + [swap(value, mask) for mask in (4, 8, 12)])
     return [group] + [swap(group, mask) for mask in (1, 2, 3)]
 
 
@@ -360,16 +365,21 @@
     rows, cols = x_cols.shape
     keys = jnp.swapaxes(cache[0], 1, 2)
     values = attend(perm, lengths, queries, new_kv, keys, w_uv)
-    residual = project(perm[None], spread(values), w_out, x_cols)
-    pieces = [piece.reshape(4, rows, cols) for piece in spread(residual)]
-    own, *chunks, kept = feed(
+    residual = project(perm[None], spread(values, join([values])), w_out, x_cols)
+    pieces = [piece.reshape(4, rows, cols) for piece in spread(residual, residual)]
+    own, *chunks, stay, go = feed(
         pieces, mlp_gain[None], jnp.swapaxes(w_gate, 0, 1), jnp.swapaxes(w_up, 0, 1), w_down
     )
+    came = partner(go, "guide", 0)
     arrived = [swap(chunk, mask) for chunk, mask in zip(chunks, (1, 2, 3))]
-    part = add([own] + arrived)
-    part = add([part, swap(part, 4)])
-    stay, go = finish(part, swap(part, 8), kept, head_gain[None])
-    normed = join([stay, partner(go, "guide", 0)])
+    came, arrived[0] = lax.optimization_barrier((came, arrived[0]))
+    half, part = stay.shape, own.shape
+    mine, his = small(part_kernel, "part", (half, half), own, *arrived)
+    sums = (mine, swap(mine, 4), partner(his, "guide", 0), across(his, 4))
+    (total,) = small(pair_kernel, "pair", (part,), *sums)
+    (normed,) = small(
+        finish_kernel, "finish", (part,), total, swap(total, 8), stay, came, head_gain[None]
+    )
     return head([normed] + [swap(normed, mask) for mask in (1, 2, 3)], guide_scale[None], w_head)
 
 

time: 80.4 us -> 77.3 us (0.961)
  waiting for transfers between devices: 37.5 us -> 34.6 us
  Pallas kernels: 14.5 us -> 13.1 us
  starting transfers between devices: 27.2 us -> 28.3 us
    ppermute x20, waiting for transfers between devices: 36.2 us -> 32 us  [swap(): return lax.ppermute(value, 'blk', pairs)]
    pallas_call x1, Pallas kernels: 5.69 us -> 4.27 us  [attend(): pl.pallas_call(attend_kernel, out_shape=jax.ShapeDtypeStruct((slots, head...]
    ppermute x0 -> x1, waiting for transfers between devices: none -> 1.4 us  [across(): return lax.ppermute(value, ('guide', 'blk'), pairs)]
  transfers between devices with their start and end apart: 21 -> 23, of which waited for: 18 -> 20; matrix products, arithmetic and copies ran while one was open for 0% -> 0% of each run, Pallas kernels for 0% -> 0%
where the time goes in v4:
time: 77.3 us; the launch traced here: 77.1 us
  waiting for transfers between devices  34.6 us (45%)
  starting transfers between devices  28.3 us (37%)
  Pallas kernels  13.1 us (17%)
  local copies, waits for them, and re-layouts  0.87 us (1%)
    ppermute x20, waiting for transfers between devices, swap(): return lax.ppermute(value, 'blk', pairs)  32 us
    ppermute x20, starting transfers between devices, swap(): return lax.ppermute(value, 'blk', pairs)  27.8 us
    pallas_call x1, Pallas kernels, head(): pl.pallas_call(head_kernel, out_shape=jax.ShapeDtypeStruct((rows // 2, vo...  5.39 us
    pallas_call x1, Pallas kernels, attend(): pl.pallas_call(attend_kernel, out_shape=jax.ShapeDtypeStruct((slots, head...  4.27 us
    pallas_call x1, Pallas kernels, feed(): pl.pallas_call(feed_kernel, out_shape=[jax.ShapeDtypeStruct(part, F32), j...  2.56 us
  transfers between devices with their start and end apart: 23, of which 20 were waited for; matrix products, arithmetic and copies ran while one was open for 0% of the time, Pallas kernels for 0%

profile of v4, /device:TPU:0, one launch (start us, length us, event | category | flops | bytes accessed | tf_op | source)
XLA Modules:
  0.0 77.1 jit_solution(7314384651771967951)
XLA Ops:
  0.0 4.3 %attend.1.refs_0_ = bf16[8,2048]{1,0:T(8,128)(2,1)} custom-call(s32[128]{0:T(128)} %perm_h.1, s32[1,128]{1,0:T(1,128)} %lengths_h.1, bf16[8,9216]{1,0:T(8,128)(2,1)} %queries_h.1, bf16[8,576]{1,0:T(8,128)(2,1)} %new_h.1, bf16[8,576,256]{2,1,0:T(8,128)(2,1)} %bitcast.25, bf16[16,512,128]{2,1,0:T(8,128)(2,1)} %w_uv.1), custom_call_target="tpu_custom_call" | custom-call | flops 15000000512 | bytes 45000000 | tf_op jit(solution)/shard_map/attend/pallas_call | solution.py:115
  4.3 5.1 %collective-permute-start.2 = (bf16[8,2048]{1,0:T(8,128)(2,1)}, bf16[8,2048]{1,0:T(8,128)(2,1)S(1)}, u32[]{:S(2)}, u32[]{:S(2)}) collective-permute-start(bf16[8,2048]{1,0:T(8,128)(2,1)} %attend.1.refs_0_), channel_id=1, source_target_pairs={{0,12},{1,13},{2,14},{3,15},{4,8},{5,9},{6,10},{7,11},{8,4},{9,5},... | collective-permute-start | bytes 98312 | tf_op jit(solution)/shard_map/ppermute | solution.py:32
  10.1 0.8 %copy-done.5 = bf16[8,2048]{1,0:T(8,128)(2,1)S(1)} copy-done((bf16[8,2048]{1,0:T(8,128)(2,1)S(1)}, bf16[8,2048]{1,0:T(8,128)(2,1)}, u32[]{:S(2)}) %copy-start.5) | copy-done | bytes 32792
  11.5 2.9 %collective-permute-done.1.refs_2_ = bf16[8,2048]{1,0:T(8,128)(2,1)S(1)} collective-permute-done((bf16[8,2048]{1,0:T(8,128)(2,1)}, bf16[8,2048]{1,0:T(8,128)(2,1)S(1)}, u32[]{:S(2)}, u32[]{:S(2)}) %collective-permute-start.1) | collective-permute-done | bytes 32800 | tf_op jit(solution)/shard_map/ppermute | solution.py:32
  14.5 2.5 %collective-permute-start.5 = (bf16[32,2048]{1,0:T(8,128)(2,1)S(1)}, bf16[32,2048]{1,0:T(8,128)(2,1)S(1)}, u32[]{:S(2)}, u32[]{:S(2)}) collective-permute-start(bf16[32,2048]{1,0:T(8,128)(2,1)S(1)} %join.4.v0), channel_id=1, source_target_pairs={{0,3},{1,2},{2,1},{3,0},{4,7},{5,6},{6,5},{7,4},{8,11},{9,10},{10,... | collective-permute-start | bytes 393224 | tf_op jit(solution)/shard_map/ppermute | solution.py:32
  18.0 3.8 %collective-permute-done.5.v3 = bf16[32,2048]{1,0:T(8,128)(2,1)S(1)} collective-permute-done((bf16[32,2048]{1,0:T(8,128)(2,1)S(1)}, bf16[32,2048]{1,0:T(8,128)(2,1)S(1)}, u32[]{:S(2)}, u32[]{:S(2)}) %collective-permute-start.5) | collective-permute-done | bytes 131104 | tf_op jit(solution)/shard_map/ppermute | solution.py:32
  21.8 0.8 %collective-permute-done.4.v2 = bf16[32,2048]{1,0:T(8,128)(2,1)S(1)} collective-permute-done((bf16[32,2048]{1,0:T(8,128)(2,1)S(1)}, bf16[32,2048]{1,0:T(8,128)(2,1)S(1)}, u32[]{:S(2)}, u32[]{:S(2)}) %collective-permute-start.4) | collective-permute-done | bytes 131104 | tf_op jit(solution)/shard_map/ppermute | solution.py:32
  23.2 1.5 %collective-permute-start.8 = (bf16[128,128]{1,0:T(8,128)(2,1)S(1)}, bf16[128,128]{1,0:T(8,128)(2,1)S(1)}, u32[]{:S(2)}, u32[]{:S(2)}) collective-permute-start(bf16[128,128]{1,0:T(8,128)(2,1)S(1)} %project.1.refs_0_), channel_id=1, source_target_pairs={{0,12},{1,13},{2,14},{3,15},{4,8},{5,9},{6,10},{7,11},{8,4},{9,5},... | collective-permute-start | bytes 98312 | tf_op jit(solution)/shard_map/ppermute | solution.py:32
  24.7 0.7 collective-permute-start.7
  25.4 2.3 %collective-permute-start.6 = (bf16[128,128]{1,0:T(8,128)(2,1)S(1)}, bf16[128,128]{1,0:T(8,128)(2,1)S(1)}, u32[]{:S(2)}, u32[]{:S(2)}) collective-permute-start(bf16[128,128]{1,0:T(8,128)(2,1)S(1)} %project.1.refs_0_), channel_id=1, source_target_pairs={{0,4},{1,5},{2,6},{3,7},{4,0},{5,1},{6,2},{7,3},{8,12},{9,13},{10,... | collective-permute-start | bytes 98312 | tf_op jit(solution)/shard_map/ppermute | solution.py:32
  27.7 1.3 %collective-permute-done.8.refs_3_ = bf16[128,128]{1,0:T(8,128)(2,1)S(1)} collective-permute-done((bf16[128,128]{1,0:T(8,128)(2,1)S(1)}, bf16[128,128]{1,0:T(8,128)(2,1)S(1)}, u32[]{:S(2)}, u32[]{:S(2)}) %collective-permute-start.8) | collective-permute-done | bytes 32800 | tf_op jit(solution)/shard_map/ppermute | solution.py:32
  29.9 1.5 %collective-permute-start.11 = (bf16[512,128]{1,0:T(8,128)(2,1)S(1)}, bf16[512,128]{1,0:T(8,128)(2,1)S(1)}, u32[]{:S(2)}, u32[]{:S(2)}) collective-permute-start(bf16[512,128]{1,0:T(8,128)(2,1)S(1)} %join.5), channel_id=1, source_target_pairs={{0,3},{1,2},{2,1},{3,0},{4,7},{5,6},{6,5},{7,4},{8,11},{9,10},{10,... | collective-permute-start | bytes 393224 | tf_op jit(solution)/shard_map/ppermute | solution.py:32
  31.4 1.5 %collective-permute-start.10 = (bf16[512,128]{1,0:T(8,128)(2,1)S(1)}, bf16[512,128]{1,0:T(8,128)(2,1)S(1)}, u32[]{:S(2)}, u32[]{:S(2)}) collective-permute-start(bf16[512,128]{1,0:T(8,128)(2,1)S(1)} %join.5), channel_id=1, source_target_pairs={{0,2},{1,3},{2,0},{3,1},{4,6},{5,7},{6,4},{7,5},{8,10},{9,11},{10,... | collective-permute-start | bytes 393224 | tf_op jit(solution)/shard_map/ppermute | solution.py:32
  33.4 2.5 %collective-permute-done.11 = bf16[512,128]{1,0:T(8,128)(2,1)S(1)} collective-permute-done((bf16[512,128]{1,0:T(8,128)(2,1)S(1)}, bf16[512,128]{1,0:T(8,128)(2,1)S(1)}, u32[]{:S(2)}, u32[]{:S(2)}) %collective-permute-start.11) | collective-permute-done | bytes 131104 | tf_op jit(solution)/shard_map/ppermute | solution.py:32
  35.9 1.3 %collective-permute-done.10 = bf16[512,128]{1,0:T(8,128)(2,1)S(1)} collective-permute-done((bf16[512,128]{1,0:T(8,128)(2,1)S(1)}, bf16[512,128]{1,0:T(8,128)(2,1)S(1)}, u32[]{:S(2)}, u32[]{:S(2)}) %collective-permute-start.10) | collective-permute-done | bytes 131104 | tf_op jit(solution)/shard_map/ppermute | solution.py:32
  37.9 2.6 %feed.1 = (f32[32,2048]{1,0:T(8,128)S(1)}, bf16[32,2048]{1,0:T(8,128)(2,1)S(1)}, bf16[32,2048]{1,0:T(8,128)(2,1)S(1)}, bf16[32,2048]{1,0:T(8,128)(2,1)S(1)}, bf1...) custom-call(bf16[4,128,128]{2,1,0:T(8,128)(2,1)S(1)} %bitcast.17, bf16[4,128,128]{2,1,0:T(8,128)(2,1)S(1)} %bitcast.20, ...), custom_call_target="tpu_custom_call" | custom-call | flops 15000000512 | bytes 45000000 | tf_op jit(solution)/shard_map/feed/pallas_call | solution.py:209
  40.4 0.9 %collective-permute-start.13 = (bf16[32,2048]{1,0:T(8,128)(2,1)S(1)}, bf16[32,2048]{1,0:T(8,128)(2,1)S(1)}, u32[]{:S(2)}, u32[]{:S(2)}) collective-permute-start(bf16[32,2048]{1,0:T(8,128)(2,1)S(1)} %get-tuple-element.17), channel_id=1, source_target_pairs={{0,1},{1,0},{2,3},{3,2},{4,5},{5,4},{6,7},{7,6},{8,9},{9,8},{10,11... | collective-permute-start | bytes 393224 | tf_op jit(solution)/shard_map/ppermute | solution.py:32
  41.4 1.1 %collective-permute-start.14 = (bf16[32,2048]{1,0:T(8,128)(2,1)S(1)}, bf16[32,2048]{1,0:T(8,128)(2,1)S(1)}, u32[]{:S(2)}, u32[]{:S(2)}) collective-permute-start(bf16[32,2048]{1,0:T(8,128)(2,1)S(1)} %get-tuple-element.19), channel_id=1, source_target_pairs={{0,2},{1,3},{2,0},{3,1},{4,6},{5,7},{6,4},{7,5},{8,10},{9,11},{10,... | collective-permute-start | bytes 393224 | tf_op jit(solution)/shard_map/ppermute | solution.py:32
  42.5 1.5 %collective-permute-start.15 = (bf16[32,2048]{1,0:T(8,128)(2,1)S(1)}, bf16[32,2048]{1,0:T(8,128)(2,1)S(1)}, u32[]{:S(2)}, u32[]{:S(2)}) collective-permute-start(bf16[32,2048]{1,0:T(8,128)(2,1)S(1)} %get-tuple-element.20), channel_id=1, source_target_pairs={{0,3},{1,2},{2,1},{3,0},{4,7},{5,6},{6,5},{7,4},{8,11},{9,10},{10,... | collective-permute-start | bytes 393224 | tf_op jit(solution)/shard_map/ppermute | solution.py:32
  44.0 1.3 %collective-permute-done.12.came = bf16[16,2048]{1,0:T(8,128)(2,1)S(1)} collective-permute-done((bf16[16,2048]{1,0:T(8,128)(2,1)S(1)}, bf16[16,2048]{1,0:T(8,128)(2,1)S(1)}, u32[]{:S(2)}, u32[]{:S(2)}) %collective-permute-start.12) | collective-permute-done | bytes 65568 | tf_op jit(solution)/shard_map/ppermute | solution.py:27
  45.5 0.9 %collective-permute-done.14.p2 = bf16[32,2048]{1,0:T(8,128)(2,1)S(1)} collective-permute-done((bf16[32,2048]{1,0:T(8,128)(2,1)S(1)}, bf16[32,2048]{1,0:T(8,128)(2,1)S(1)}, u32[]{:S(2)}, u32[]{:S(2)}) %collective-permute-start.14) | collective-permute-done | bytes 131104 | tf_op jit(solution)/shard_map/ppermute | solution.py:32
  46.3 2.0 %collective-permute-done.15.p3 = bf16[32,2048]{1,0:T(8,128)(2,1)S(1)} collective-permute-done((bf16[32,2048]{1,0:T(8,128)(2,1)S(1)}, bf16[32,2048]{1,0:T(8,128)(2,1)S(1)}, u32[]{:S(2)}, u32[]{:S(2)}) %collective-permute-start.15) | collective-permute-done | bytes 131104 | tf_op jit(solution)/shard_map/ppermute | solution.py:32
  48.4 1.7 %collective-permute-start.16 = (bf16[16,2048]{1,0:T(8,128)(2,1)S(1)}, bf16[16,2048]{1,0:T(8,128)(2,1)S(1)}, u32[]{:S(2)}, u32[]{:S(2)}) collective-permute-start(bf16[16,2048]{1,0:T(8,128)(2,1)S(1)} %get-tuple-element.21.a), channel_id=1, source_target_pairs={{0,4},{1,5},{2,6},{3,7},{4,0},{5,1},{6,2},{7,3},{8,12},{9,13},{10,... | collective-permute-start | bytes 196616 | tf_op jit(solution)/shard_map/ppermute | solution.py:32
  50.6 2.1 %collective-permute-done.16.b = bf16[16,2048]{1,0:T(8,128)(2,1)S(1)} collective-permute-done((bf16[16,2048]{1,0:T(8,128)(2,1)S(1)}, bf16[16,2048]{1,0:T(8,128)(2,1)S(1)}, u32[]{:S(2)}, u32[]{:S(2)}) %collective-permute-start.16) | collective-permute-done | bytes 65568 | tf_op jit(solution)/shard_map/ppermute | solution.py:32
  52.8 1.4 %collective-permute-done.18.d = bf16[16,2048]{1,0:T(8,128)(2,1)S(1)} collective-permute-done((bf16[16,2048]{1,0:T(8,128)(2,1)S(1)}, bf16[16,2048]{1,0:T(8,128)(2,1)S(1)}, u32[]{:S(2)}, u32[]{:S(2)}) %collective-permute-start.18) | collective-permute-done | bytes 65568 | tf_op jit(solution)/shard_map/ppermute | solution.py:21
  54.2 1.7 %collective-permute-start.19 = (bf16[32,2048]{1,0:T(8,128)(2,1)S(1)}, bf16[32,2048]{1,0:T(8,128)(2,1)S(1)}, u32[]{:S(2)}, u32[]{:S(2)}) collective-permute-start(bf16[32,2048]{1,0:T(8,128)(2,1)S(1)} %pair.1.own), channel_id=1, source_target_pairs={{0,8},{1,9},{2,10},{3,11},{4,12},{5,13},{6,14},{7,15},{8,0},{9,1},... | collective-permute-start | bytes 393224 | tf_op jit(solution)/shard_map/ppermute | solution.py:32
  55.9 7.2 %collective-permute-done.19.other = bf16[32,2048]{1,0:T(8,128)(2,1)S(1)} collective-permute-done((bf16[32,2048]{1,0:T(8,128)(2,1)S(1)}, bf16[32,2048]{1,0:T(8,128)(2,1)S(1)}, u32[]{:S(2)}, u32[]{:S(2)}) %collective-permute-start.19) | collective-permute-done | bytes 131104 | tf_op jit(solution)/shard_map/ppermute | solution.py:32
  63.3 2.0 %collective-permute-start.22 = (bf16[32,2048]{1,0:T(8,128)(2,1)S(1)}, bf16[32,2048]{1,0:T(8,128)(2,1)S(1)}, u32[]{:S(2)}, u32[]{:S(2)}) collective-permute-start(bf16[32,2048]{1,0:T(8,128)(2,1)S(1)} %finish.1.r0), channel_id=1, source_target_pairs={{0,3},{1,2},{2,1},{3,0},{4,7},{5,6},{6,5},{7,4},{8,11},{9,10},{10,... | collective-permute-start | bytes 393224 | tf_op jit(solution)/shard_map/ppermute | solution.py:32
  65.7 1.2 %collective-permute-start.20 = (bf16[32,2048]{1,0:T(8,128)(2,1)S(1)}, bf16[32,2048]{1,0:T(8,128)(2,1)S(1)}, u32[]{:S(2)}, u32[]{:S(2)}) collective-permute-start(bf16[32,2048]{1,0:T(8,128)(2,1)S(1)} %finish.1.r0), channel_id=1, source_target_pairs={{0,1},{1,0},{2,3},{3,2},{4,5},{5,4},{6,7},{7,6},{8,9},{9,8},{10,11... | collective-permute-start | bytes 393224 | tf_op jit(solution)/shard_map/ppermute | solution.py:32
  66.9 3.4 %collective-permute-done.22.r3 = bf16[32,2048]{1,0:T(8,128)(2,1)S(1)} collective-permute-done((bf16[32,2048]{1,0:T(8,128)(2,1)S(1)}, bf16[32,2048]{1,0:T(8,128)(2,1)S(1)}, u32[]{:S(2)}, u32[]{:S(2)}) %collective-permute-start.22) | collective-permute-done | bytes 131104 | tf_op jit(solution)/shard_map/ppermute | solution.py:32
  70.3 1.1 %collective-permute-done.21.r2 = bf16[32,2048]{1,0:T(8,128)(2,1)S(1)} collective-permute-done((bf16[32,2048]{1,0:T(8,128)(2,1)S(1)}, bf16[32,2048]{1,0:T(8,128)(2,1)S(1)}, u32[]{:S(2)}, u32[]{:S(2)}) %collective-permute-start.21) | collective-permute-done | bytes 131104 | tf_op jit(solution)/shard_map/ppermute | solution.py:32
  71.7 5.4 %head.1 = bf16[64,6400]{1,0:T(8,128)(2,1)} custom-call(bf16[32,2048]{1,0:T(8,128)(2,1)S(1)} %finish.1.r0, bf16[32,2048]{1,0:T(8,128)(2,1)S(1)} %collective-permute-done.20.r1, bf16[32,2048]{1,0:T(8,128)(2,1)S(1)} %collective-permute-done.21.r2, bf16[32,2048]{1,0:T(8,128)(2,1)S(1)} %collective-permute-done.22.r3, f32[1,128]{1,0:T(1,128)S(1)} %bitcast.24, ...), custom_call_target="tpu_custom_call" | custom-call | flops 8000000000 | bytes 24000000 | tf_op jit(solution)/shard_map/head/pallas_call | solution.py:305
  (59 shorter events, 6.6 us)
Async XLA Ops:
  0.0 22.6 %copy-start.8 = (s32[128]{0:T(128)S(1)}, s32[128]{0:T(128)}, u32[]{:S(2)}) copy-start(s32[128]{0:T(128)} %perm_h.1) | copy-start | bytes 1540
  4.3 18.3 %copy-start.3 = (bf16[2048,128]{1,0:T(8,128)(2,1)S(1)}, bf16[2048,128]{1,0:T(8,128)(2,1)}, u32[]{:S(2)}) copy-start(bf16[2048,128]{1,0:T(8,128)(2,1)} %w_out.1) | copy-start | bytes 1572868
  4.3 18.3 %copy-start.4 = (bf16[128,128]{1,0:T(8,128)(2,1)S(1)}, bf16[128,128]{1,0:T(8,128)(2,1)}, u32[]{:S(2)}) copy-start(bf16[128,128]{1,0:T(8,128)(2,1)} %x_cols.1) | copy-start | bytes 98308
  4.3 7.2 %collective-permute-start.2 = (bf16[8,2048]{1,0:T(8,128)(2,1)}, bf16[8,2048]{1,0:T(8,128)(2,1)S(1)}, u32[]{:S(2)}, u32[]{:S(2)}) collective-permute-start(bf16[8,2048]{1,0:T(8,128)(2,1)} %attend.1.refs_0_), channel_id=1, source_target_pairs={{0,12},{1,13},{2,14},{3,15},{4,8},{5,9},{6,10},{7,11},{8,4},{9,5},... | collective-permute-start | bytes 98312 | tf_op jit(solution)/shard_map/ppermute | solution.py:32
  9.4 5.0 %collective-permute-start.1 = (bf16[8,2048]{1,0:T(8,128)(2,1)}, bf16[8,2048]{1,0:T(8,128)(2,1)S(1)}, u32[]{:S(2)}, u32[]{:S(2)}) collective-permute-start(bf16[8,2048]{1,0:T(8,128)(2,1)} %attend.1.refs_0_), channel_id=1, source_target_pairs={{0,8},{1,9},{2,10},{3,11},{4,12},{5,13},{6,14},{7,15},{8,0},{9,1},... | collective-permute-start | bytes 98312 | tf_op jit(solution)/shard_map/ppermute | solution.py:32
  9.4 5.0 %collective-permute-start = (bf16[8,2048]{1,0:T(8,128)(2,1)}, bf16[8,2048]{1,0:T(8,128)(2,1)S(1)}, u32[]{:S(2)}, u32[]{:S(2)}) collective-permute-start(bf16[8,2048]{1,0:T(8,128)(2,1)} %attend.1.refs_0_), channel_id=1, source_target_pairs={{0,4},{1,5},{2,6},{3,7},{4,0},{5,1},{6,2},{7,3},{8,12},{9,13},{10,... | collective-permute-start | bytes 98312 | tf_op jit(solution)/shard_map/ppermute | solution.py:32
  14.5 7.3 %collective-permute-start.5 = (bf16[32,2048]{1,0:T(8,128)(2,1)S(1)}, bf16[32,2048]{1,0:T(8,128)(2,1)S(1)}, u32[]{:S(2)}, u32[]{:S(2)}) collective-permute-start(bf16[32,2048]{1,0:T(8,128)(2,1)S(1)} %join.4.v0), channel_id=1, source_target_pairs={{0,3},{1,2},{2,1},{3,0},{4,7},{5,6},{6,5},{7,4},{8,11},{9,10},{10,... | collective-permute-start | bytes 393224 | tf_op jit(solution)/shard_map/ppermute | solution.py:32
  17.0 5.6 %collective-permute-start.4 = (bf16[32,2048]{1,0:T(8,128)(2,1)S(1)}, bf16[32,2048]{1,0:T(8,128)(2,1)S(1)}, u32[]{:S(2)}, u32[]{:S(2)}) collective-permute-start(bf16[32,2048]{1,0:T(8,128)(2,1)S(1)} %join.4.v0), channel_id=1, source_target_pairs={{0,2},{1,3},{2,0},{3,1},{4,6},{5,7},{6,4},{7,5},{8,10},{9,11},{10,... | collective-permute-start | bytes 393224 | tf_op jit(solution)/shard_map/ppermute | solution.py:32
  17.5 5.1 %collective-permute-start.3 = (bf16[32,2048]{1,0:T(8,128)(2,1)S(1)}, bf16[32,2048]{1,0:T(8,128)(2,1)S(1)}, u32[]{:S(2)}, u32[]{:S(2)}) collective-permute-start(bf16[32,2048]{1,0:T(8,128)(2,1)S(1)} %join.4.v0), channel_id=1, source_target_pairs={{0,1},{1,0},{2,3},{3,2},{4,5},{5,4},{6,7},{7,6},{8,9},{9,8},{10,11... | collective-permute-start | bytes 393224 | tf_op jit(solution)/shard_map/ppermute | solution.py:32
  22.6 15.3 %copy-start.1 = (bf16[2048,684]{0,1:T(8,128)(2,1)S(1)}, bf16[2048,684]{0,1:T(8,128)(2,1)}, u32[]{:S(2)}) copy-start(bf16[2048,684]{0,1:T(8,128)(2,1)} %param.26) | copy-start | bytes 8404996
  22.6 15.2 %copy-start.2 = (bf16[684,2048]{1,0:T(8,128)(2,1)S(1)}, bf16[684,2048]{1,0:T(8,128)(2,1)}, u32[]{:S(2)}) copy-start(bf16[684,2048]{1,0:T(8,128)(2,1)} %w_down.1) | copy-start | bytes 8404996
  23.2 5.8 %collective-permute-start.8 = (bf16[128,128]{1,0:T(8,128)(2,1)S(1)}, bf16[128,128]{1,0:T(8,128)(2,1)S(1)}, u32[]{:S(2)}, u32[]{:S(2)}) collective-permute-start(bf16[128,128]{1,0:T(8,128)(2,1)S(1)} %project.1.refs_0_), channel_id=1, source_target_pairs={{0,12},{1,13},{2,14},{3,15},{4,8},{5,9},{6,10},{7,11},{8,4},{9,5},... | collective-permute-start | bytes 98312 | tf_op jit(solution)/shard_map/ppermute | solution.py:32
  24.7 4.8 %collective-permute-start.7 = (bf16[128,128]{1,0:T(8,128)(2,1)S(1)}, bf16[128,128]{1,0:T(8,128)(2,1)S(1)}, u32[]{:S(2)}, u32[]{:S(2)}) collective-permute-start(bf16[128,128]{1,0:T(8,128)(2,1)S(1)} %project.1.refs_0_), channel_id=1, source_target_pairs={{0,8},{1,9},{2,10},{3,11},{4,12},{5,13},{6,14},{7,15},{8,0},{9,1},... | collective-permute-start | bytes 98312 | tf_op jit(solution)/shard_map/ppermute | solution.py:32
  25.4 4.5 %collective-permute-start.6 = (bf16[128,128]{1,0:T(8,128)(2,1)S(1)}, bf16[128,128]{1,0:T(8,128)(2,1)S(1)}, u32[]{:S(2)}, u32[]{:S(2)}) collective-permute-start(bf16[128,128]{1,0:T(8,128)(2,1)S(1)} %project.1.refs_0_), channel_id=1, source_target_pairs={{0,4},{1,5},{2,6},{3,7},{4,0},{5,1},{6,2},{7,3},{8,12},{9,13},{10,... | collective-permute-start | bytes 98312 | tf_op jit(solution)/shard_map/ppermute | solution.py:32
  29.9 6.0 %collective-permute-start.11 = (bf16[512,128]{1,0:T(8,128)(2,1)S(1)}, bf16[512,128]{1,0:T(8,128)(2,1)S(1)}, u32[]{:S(2)}, u32[]{:S(2)}) collective-permute-start(bf16[512,128]{1,0:T(8,128)(2,1)S(1)} %join.5), channel_id=1, source_target_pairs={{0,3},{1,2},{2,1},{3,0},{4,7},{5,6},{6,5},{7,4},{8,11},{9,10},{10,... | collective-permute-start | bytes 393224 | tf_op jit(solution)/shard_map/ppermute | solution.py:32
  31.4 5.8 %collective-permute-start.10 = (bf16[512,128]{1,0:T(8,128)(2,1)S(1)}, bf16[512,128]{1,0:T(8,128)(2,1)S(1)}, u32[]{:S(2)}, u32[]{:S(2)}) collective-permute-start(bf16[512,128]{1,0:T(8,128)(2,1)S(1)} %join.5), channel_id=1, source_target_pairs={{0,2},{1,3},{2,0},{3,1},{4,6},{5,7},{6,4},{7,5},{8,10},{9,11},{10,... | collective-permute-start | bytes 393224 | tf_op jit(solution)/shard_map/ppermute | solution.py:32
  32.9 5.0 %collective-permute-start.9 = (bf16[512,128]{1,0:T(8,128)(2,1)S(1)}, bf16[512,128]{1,0:T(8,128)(2,1)S(1)}, u32[]{:S(2)}, u32[]{:S(2)}) collective-permute-start(bf16[512,128]{1,0:T(8,128)(2,1)S(1)} %join.5), channel_id=1, source_target_pairs={{0,1},{1,0},{2,3},{3,2},{4,5},{5,4},{6,7},{7,6},{8,9},{9,8},{10,11... | collective-permute-start | bytes 393224 | tf_op jit(solution)/shard_map/ppermute | solution.py:32
  40.4 5.0 %collective-permute-start.13 = (bf16[32,2048]{1,0:T(8,128)(2,1)S(1)}, bf16[32,2048]{1,0:T(8,128)(2,1)S(1)}, u32[]{:S(2)}, u32[]{:S(2)}) collective-permute-start(bf16[32,2048]{1,0:T(8,128)(2,1)S(1)} %get-tuple-element.17), channel_id=1, source_target_pairs={{0,1},{1,0},{2,3},{3,2},{4,5},{5,4},{6,7},{7,6},{8,9},{9,8},{10,11... | collective-permute-start | bytes 393224 | tf_op jit(solution)/shard_map/ppermute | solution.py:32
  41.4 5.0 %collective-permute-start.14 = (bf16[32,2048]{1,0:T(8,128)(2,1)S(1)}, bf16[32,2048]{1,0:T(8,128)(2,1)S(1)}, u32[]{:S(2)}, u32[]{:S(2)}) collective-permute-start(bf16[32,2048]{1,0:T(8,128)(2,1)S(1)} %get-tuple-element.19), channel_id=1, source_target_pairs={{0,2},{1,3},{2,0},{3,1},{4,6},{5,7},{6,4},{7,5},{8,10},{9,11},{10,... | collective-permute-start | bytes 393224 | tf_op jit(solution)/shard_map/ppermute | solution.py:32
  42.5 5.9 %collective-permute-start.15 = (bf16[32,2048]{1,0:T(8,128)(2,1)S(1)}, bf16[32,2048]{1,0:T(8,128)(2,1)S(1)}, u32[]{:S(2)}, u32[]{:S(2)}) collective-permute-start(bf16[32,2048]{1,0:T(8,128)(2,1)S(1)} %get-tuple-element.20), channel_id=1, source_target_pairs={{0,3},{1,2},{2,1},{3,0},{4,7},{5,6},{6,5},{7,4},{8,11},{9,10},{10,... | collective-permute-start | bytes 393224 | tf_op jit(solution)/shard_map/ppermute | solution.py:32
  44.0 1.3 %collective-permute-start.12 = (bf16[16,2048]{1,0:T(8,128)(2,1)S(1)}, bf16[16,2048]{1,0:T(8,128)(2,1)S(1)}, u32[]{:S(2)}, u32[]{:S(2)}) collective-permute-start(bf16[16,2048]{1,0:T(8,128)(2,1)S(1)} %get-tuple-element.16), channel_id=1, source_target_pairs={{0,16},{16,0},{1,17},{17,1},{2,18},{18,2},{3,19},{19,3},{4,20},{20... | collective-permute-start | bytes 196616 | tf_op jit(solution)/shard_map/ppermute | solution.py:27
  48.4 4.3 %collective-permute-start.16 = (bf16[16,2048]{1,0:T(8,128)(2,1)S(1)}, bf16[16,2048]{1,0:T(8,128)(2,1)S(1)}, u32[]{:S(2)}, u32[]{:S(2)}) collective-permute-start(bf16[16,2048]{1,0:T(8,128)(2,1)S(1)} %get-tuple-element.21.a), channel_id=1, source_target_pairs={{0,4},{1,5},{2,6},{3,7},{4,0},{5,1},{6,2},{7,3},{8,12},{9,13},{10,... | collective-permute-start | bytes 196616 | tf_op jit(solution)/shard_map/ppermute | solution.py:32
  50.2 4.0 %collective-permute-start.18 = (bf16[16,2048]{1,0:T(8,128)(2,1)S(1)}, bf16[16,2048]{1,0:T(8,128)(2,1)S(1)}, u32[]{:S(2)}, u32[]{:S(2)}) collective-permute-start(bf16[16,2048]{1,0:T(8,128)(2,1)S(1)} %get-tuple-element.22), channel_id=1, source_target_pairs={{0,20},{1,21},{2,22},{3,23},{4,16},{5,17},{6,18},{7,19},{8,28},{9,... | collective-permute-start | bytes 196616 | tf_op jit(solution)/shard_map/ppermute | solution.py:21
  50.2 4.0 %collective-permute-start.17 = (bf16[16,2048]{1,0:T(8,128)(2,1)S(1)}, bf16[16,2048]{1,0:T(8,128)(2,1)S(1)}, u32[]{:S(2)}, u32[]{:S(2)}) collective-permute-start(bf16[16,2048]{1,0:T(8,128)(2,1)S(1)} %get-tuple-element.22), channel_id=1, source_target_pairs={{0,16},{16,0},{1,17},{17,1},{2,18},{18,2},{3,19},{19,3},{4,20},{20... | collective-permute-start | bytes 196616 | tf_op jit(solution)/shard_map/ppermute | solution.py:27
  54.2 17.5 %slice-start = ((s8[26214400]{0:T(1024)(128)(4,1)}), s8[4194304]{0:T(1024)(128)(4,1)S(1)}, s32[]{:S(2)}) async-start(s8[26214400]{0:T(1024)(128)(4,1)} %bitcast.13), calls=%async_computation | async-start | bytes 8388608
  54.2 17.5 %slice-start.1 = ((s8[26214400]{0:T(1024)(128)(4,1)}), s8[4194304]{0:T(1024)(128)(4,1)S(1)}, s32[]{:S(2)}) async-start(s8[26214400]{0:T(1024)(128)(4,1)} %bitcast.13), calls=%async_computation.1 | async-start | bytes 8388608
  54.2 17.5 %slice-start.2 = ((s8[26214400]{0:T(1024)(128)(4,1)}), s8[4194304]{0:T(1024)(128)(4,1)S(1)}, s32[]{:S(2)}) async-start(s8[26214400]{0:T(1024)(128)(4,1)} %bitcast.13), calls=%async_computation.2 | async-start | bytes 8388608
  54.2 17.5 %slice-start.3 = ((s8[26214400]{0:T(1024)(128)(4,1)}), s8[4194304]{0:T(1024)(128)(4,1)S(1)}, s32[]{:S(2)}) async-start(s8[26214400]{0:T(1024)(128)(4,1)} %bitcast.13), calls=%async_computation.3 | async-start | bytes 8388608
  54.2 8.9 %collective-permute-start.19 = (bf16[32,2048]{1,0:T(8,128)(2,1)S(1)}, bf16[32,2048]{1,0:T(8,128)(2,1)S(1)}, u32[]{:S(2)}, u32[]{:S(2)}) collective-permute-start(bf16[32,2048]{1,0:T(8,128)(2,1)S(1)} %pair.1.own), channel_id=1, source_target_pairs={{0,8},{1,9},{2,10},{3,11},{4,12},{5,13},{6,14},{7,15},{8,0},{9,1},... | collective-permute-start | bytes 393224 | tf_op jit(solution)/shard_map/ppermute | solution.py:32
  63.3 7.0 %collective-permute-start.22 = (bf16[32,2048]{1,0:T(8,128)(2,1)S(1)}, bf16[32,2048]{1,0:T(8,128)(2,1)S(1)}, u32[]{:S(2)}, u32[]{:S(2)}) collective-permute-start(bf16[32,2048]{1,0:T(8,128)(2,1)S(1)} %finish.1.r0), channel_id=1, source_target_pairs={{0,3},{1,2},{2,1},{3,0},{4,7},{5,6},{6,5},{7,4},{8,11},{9,10},{10,... | collective-permute-start | bytes 393224 | tf_op jit(solution)/shard_map/ppermute | solution.py:32
  65.3 6.2 %collective-permute-start.21 = (bf16[32,2048]{1,0:T(8,128)(2,1)S(1)}, bf16[32,2048]{1,0:T(8,128)(2,1)S(1)}, u32[]{:S(2)}, u32[]{:S(2)}) collective-permute-start(bf16[32,2048]{1,0:T(8,128)(2,1)S(1)} %finish.1.r0), channel_id=1, source_target_pairs={{0,2},{1,3},{2,0},{3,1},{4,6},{5,7},{6,4},{7,5},{8,10},{9,11},{10,... | collective-permute-start | bytes 393224 | tf_op jit(solution)/shard_map/ppermute | solution.py:32
  65.7 6.0 %collective-permute-start.20 = (bf16[32,2048]{1,0:T(8,128)(2,1)S(1)}, bf16[32,2048]{1,0:T(8,128)(2,1)S(1)}, u32[]{:S(2)}, u32[]{:S(2)}) collective-permute-start(bf16[32,2048]{1,0:T(8,128)(2,1)S(1)} %finish.1.r0), channel_id=1, source_target_pairs={{0,1},{1,0},{2,3},{3,2},{4,5},{5,4},{6,7},{7,6},{8,9},{9,8},{10,11... | collective-permute-start | bytes 393224 | tf_op jit(solution)/shard_map/ppermute | solution.py:32
  (8 other events, 77.3 us)

commit v5 on v4

--- a/solution.py
+++ b/solution.py
@@ -1,3 +1,5 @@
+import functools
+
 import jax
 import jax.numpy as jnp
 from jax import lax
@@ -134,12 +136,7 @@
     )(perm, lengths, queries, new_kv, cache, w_uv)
 
 
-def request_of(row, rows):
-    chip = ((row >> 2) & 3) * 4 + (row >> 5)
-    return ((row >> 4) & 1) * (rows // 2) + chip * 4 + (row & 3)
-
-
-def project_kernel(perm, v0, v1, v2, v3, w_out, x_cols, out, full):
+def project_kernel(perm, v3, v2, v1, v0, w_out, x_cols, out, full):
     blk = lax.axis_index("blk")
     rows = x_cols.shape[0]
     part = v0.shape[0]
@@ -147,8 +144,7 @@
         full[q * part : (q + 1) * part, :] = ref[...]
     attended = dot(full[...], w_out[...], NN)
     shape = (rows, rows)
-    wanted = request_of(iota(shape, 0), rows)
-    by_slot = (jnp.broadcast_to(perm[...], shape) == wanted).astype(F32)
+    by_slot = (jnp.broadcast_to(perm[...], shape) == iota(shape, 0)).astype(F32)
     arrived = iota(shape, 1)
     slot = ((blk ^ (((arrived >> 3) & 3) * 4) ^ (arrived >> 5)) << 3) | (arrived & 7)
     move = (iota(shape, 0) == slot).astype(F32)
@@ -168,11 +164,11 @@
         compiler_params=pltpu.CompilerParams(vmem_limit_bytes=4 << 20),
         cost_estimate=cost(15),
         name="project",
-    )(perm, *pieces, w_out, x_cols)
+    )(perm, *reversed(pieces), w_out, x_cols)
 
 
 def feed_kernel(
-    r0, r1, r2, r3, gain, w_gate, w_up, w_down, own, c1, c2, c3, stay, go, full, acc
+    r3, r2, r1, r0, gain, w_gate, w_up, w_down, own, c1, c2, c3, stay, go, full, acc
 ):
     blk = lax.axis_index("blk")
     groups, rows, cols = r0.shape
@@ -191,12 +187,12 @@
     hidden = jnp.where(unit < FF, hidden, 0.0).astype(BF)
     acc[...] = dot(hidden, w_down[...], NN)
     low = blk & 3
-    chunk = rows // 4
+    chunk = acc.shape[1] // 4
     for q, ref in enumerate((own, c1, c2, c3)):
         at = pl.multiple_of((low ^ q) * chunk, chunk)
-        ref[...] = acc[pl.ds(at, chunk), :].astype(ref.dtype)
-    first = full[pl.ds(pl.multiple_of(low * chunk, chunk), chunk // 2), :]
-    last = full[pl.ds(pl.multiple_of(low * chunk + chunk // 2, chunk // 2), chunk // 2), :]
+        ref[...] = acc[:, pl.ds(at, chunk)].astype(ref.dtype)
+    kept = full[:, pl.ds(pl.multiple_of(low * chunk, chunk), chunk)]
+    first, last = kept[: rows // 2], kept[rows // 2 :]
     lower = lax.axis_index("guide") == 0
     stay[...] = jnp.where(lower, first, last).astype(BF)
     go[...] = jnp.where(lower, last, first).astype(BF)
@@ -205,7 +201,7 @@
 def feed(pieces, gain, w_gate, w_up, w_down):
     groups, rows, cols = pieces[0].shape
     width = w_down.shape[1]
-    part = (rows // 4, width)
+    part = (rows, width // 4)
     return pl.pallas_call(
         feed_kernel,
         out_shape=[
@@ -213,16 +209,16 @@
             jax.ShapeDtypeStruct(part, BF),
             jax.ShapeDtypeStruct(part, BF),
             jax.ShapeDtypeStruct(part, BF),
-            jax.ShapeDtypeStruct((rows // 8, width), BF),
-            jax.ShapeDtypeStruct((rows // 8, width), BF),
+            jax.ShapeDtypeStruct((rows // 2, width // 4), BF),
+            jax.ShapeDtypeStruct((rows // 2, width // 4), BF),
         ],
         in_specs=[VM] * 8,
         out_specs=[VM] * 6,
         scratch_shapes=[pltpu.VMEM((rows, width), F32), pltpu.VMEM((rows, width), F32)],
         compiler_params=pltpu.CompilerParams(vmem_limit_bytes=8 << 20),
-        cost_estimate=cost(15),
+        cost_estimate=cost(40),
         name="feed",
-    )(*pieces, gain, w_gate, w_up, w_down)
+    )(*reversed(pieces), gain, w_gate, w_up, w_down)
 
 
 def part_kernel(own, p1, p2, p3, stay, go):
@@ -240,14 +236,12 @@
     out[half:, :] = (c[...].astype(F32) + d[...].astype(F32)).astype(BF)
 
 
-def finish_kernel(own, other, stay, came, gain, out):
+def finish_kernel(own, other, stay, came, out):
     half = stay.shape[0]
     total = own[...].astype(F32) + other[...].astype(F32)
     for k, ref in enumerate((stay, came)):
         at = slice(k * half, (k + 1) * half)
-        after = (ref[...].astype(F32) + total[at]).astype(BF).astype(F32)
-        meansq = jnp.mean(after * after, axis=1, keepdims=True)
-        out[at, :] = (after * lax.rsqrt(meansq + 1e-06) * gain[...]).astype(BF)
+        out[at, :] = (ref[...].astype(F32) + total[at]).astype(BF)
 
 
 def small(kernel, name, shapes, *args):
@@ -257,24 +251,42 @@
         in_specs=[VM] * len(args),
         out_specs=[VM] * len(shapes),
         compiler_params=pltpu.CompilerParams(vmem_limit_bytes=2 << 20),
-        cost_estimate=cost(20),
+        cost_estimate=cost(1),
         name=name,
     )(*args)
 
 
-def head_kernel(r0, r1, r2, r3, scale, w_head, out, came, full, factor, done, sems):
-    guide, blk = lax.axis_index("guide"), lax.axis_index("blk")
-    part = r0.shape[0]
-    rows = 4 * part
+def block_product(ref, q, gain, w_head, at):
+    width = ref.shape[1]
+    first = pl.multiple_of(((lax.axis_index("blk") & 3) ^ q) * width, width)
+    scaled = (ref[...].astype(F32) * gain[:, pl.ds(first, width)]).astype(BF)
+    return dot(scaled, w_head[pl.ds(first, width), at], NN)
+
+
+def open_kernel(piece, gain, w_head, acc, *, tile):
+    @pl.loop(0, w_head.shape[1] // tile)
+    def _(step):
+        at = pl.ds(pl.multiple_of(step * tile, tile), tile)
+        acc[:, at] = block_product(piece, 0, gain, w_head, at)
+
+
+def more_kernel(piece, gain, w_head, old, acc, *, tile):
+    @pl.loop(0, w_head.shape[1] // tile)
+    def _(step):
+        at = pl.ds(pl.multiple_of(step * tile, tile), tile)
+        acc[:, at] = old[:, at] + block_product(piece, 3, gain, w_head, at)
+
+
+def close_kernel(r0, r1, r2, r3, gain, scale, w_head, acc, out, factor, rms, done, sems):
+    guide = lax.axis_index("guide")
+    rows, width = r0.shape
     half = rows // 2
     tiles, _, tile = done.shape
-    for q, ref in enumerate((r0, r1, r2, r3)):
-        came[q * part : (q + 1) * part, :] = ref[...]
-    at = iota((rows, rows), 1)
-    chip = (((at >> 2) & 3) << 2) + ((blk & 3) ^ (at >> 5))
-    row = (((at >> 4) & 1) ^ guide) * half + chip * 4 + (at & 3)
-    order = (row == iota((rows, rows), 0)).astype(BF)
-    full[...] = dot(order, came[...], NN).astype(BF)
+    squares = jnp.zeros((rows, 1), F32)
+    for ref in (r0, r1, r2, r3):
+        values = ref[...].astype(F32)
+        squares += jnp.sum(values * values, axis=1, keepdims=True)
+    rms[...] = lax.rsqrt(squares / (4 * width) + 1e-06)
     mine = iota((half, rows), 0) + guide * half == iota((half, rows), 1)
     factor[...] = jnp.sum(
         jnp.where(mine, jnp.broadcast_to(scale[...], (half, rows)), 0.0), 1, keepdims=True
@@ -287,8 +299,13 @@
     @pl.loop(0, tiles)
     def _(step):
         at = pl.ds(pl.multiple_of(step * tile, tile), tile)
-        logits = dot(full[...], w_head[:, at], NN)
-        cond, uncond = logits[:half], logits[half:]
+        logits = acc[:, at]
+        for q, ref in ((2, r2), (1, r1)):
+            logits += block_product(ref, q, gain, w_head, at)
+        logits *= rms[...]
+        own, other = logits[:half], logits[half:]
+        cond = jnp.where(guide == 0, own, other)
+        uncond = jnp.where(guide == 0, other, own)
         done[step] = (uncond + factor[...] * (cond - uncond)).astype(BF)
         store(step).start()
 
@@ -297,33 +314,53 @@
         store(step).wait()
 
 
-def head(pieces, scale, w_head):
-    part, width = pieces[0].shape
-    rows = 4 * part
+def head(piece, scale, gain, w_head):
+    rows, width = piece.shape
     vocab = w_head.shape[1]
-    tile = next(t for t in (1280, 256, 128) if vocab % t == 0)
+    tile = next(t for t in (3200, 1280, 256, 128) if vocab % t == 0)
+    pieces = [piece] + [swap(piece, mask) for mask in (1, 2, 3)]
+    sums = jax.ShapeDtypeStruct((rows, vocab), F32)
+    params = pltpu.CompilerParams(vmem_limit_bytes=4 << 20)
+    acc = pl.pallas_call(
+        functools.partial(open_kernel, tile=tile),
+        out_shape=sums,
+        in_specs=[VM] * 3,
+        out_specs=VM,
+        compiler_params=params,
+        cost_estimate=cost(2),
+        name="open",
+    )(piece, gain, w_head)
+    acc = pl.pallas_call(
+        functools.partial(more_kernel, tile=tile),
+        out_shape=sums,
+        in_specs=[VM] * 4,
+        out_specs=VM,
+        input_output_aliases={3: 0},
+        compiler_params=params,
+        cost_estimate=cost(2),
+        name="more",
+    )(pieces[3], gain, w_head, acc)
     return pl.pallas_call(
-        head_kernel,
+        close_kernel,
         out_shape=jax.ShapeDtypeStruct((rows // 2, vocab), BF),
-        in_specs=[VM] * 6,
+        in_specs=[VM] * 8,
         out_specs=HB,
         scratch_shapes=[
-            pltpu.VMEM((rows, width), BF),
-            pltpu.VMEM((rows, width), BF),
             pltpu.VMEM((rows // 2, 1), F32),
+            pltpu.VMEM((rows, 1), F32),
             pltpu.VMEM((vocab // tile, rows // 2, tile), BF),
             pltpu.SemaphoreType.DMA((vocab // tile,)),
         ],
         compiler_params=pltpu.CompilerParams(vmem_limit_bytes=8 << 20),
-        cost_estimate=cost(8),
-        name="head",
-    )(*pieces, scale, w_head)
+        cost_estimate=cost(3),
+        name="close",
+    )(*pieces, gain, scale, w_head, acc)
 
 
 def join_kernel(*refs):
     out = refs[-1]
     part = refs[0].shape[0]
-    for k, ref in enumerate(refs[:-1]):
+    for k, ref in enumerate(refs[-2::-1]):
         out[k * part : (k + 1) * part, :] = ref[...]
 
 
@@ -337,7 +374,7 @@
         compiler_params=pltpu.CompilerParams(vmem_limit_bytes=1 << 20),
         cost_estimate=cost(1),
         name="join",
-    )(*parts)
+    )(*reversed(parts))
 
 
 def spread(value, own):
@@ -375,12 +412,10 @@
     came, arrived[0] = lax.optimization_barrier((came, arrived[0]))
     half, part = stay.shape, own.shape
     mine, his = small(part_kernel, "part", (half, half), own, *arrived)
-    sums = (mine, swap(mine, 4), partner(his, "guide", 0), across(his, 4))
+    sums = (mine, swap(mine, 8), partner(his, "guide", 0), across(his, 8))
     (total,) = small(pair_kernel, "pair", (part,), *sums)
-    (normed,) = small(
-        finish_kernel, "finish", (part,), total, swap(total, 8), stay, came, head_gain[None]
-    )
-    return head([normed] + [swap(normed, mask) for mask in (1, 2, 3)], guide_scale[None], w_head)
+    (after,) = small(finish_kernel, "finish", (part,), total, swap(total, 4), stay, came)
+    return head(after, guide_scale[None], head_gain[None], w_head)
 
 
 def body(

time: 77.3 us -> 75.5 us (0.977)
  waiting for transfers between devices: 34.6 us -> 32.8 us
    ppermute x20, waiting for transfers between devices: 32 us -> 27.7 us  [swap(): return lax.ppermute(value, 'blk', pairs)]
    ppermute x1, waiting for transfers between devices: 1.4 us -> 3.85 us  [across(): return lax.ppermute(value, ('guide', 'blk'), pairs)]
    ppermute x20, starting transfers between devices: 27.8 us -> 26.3 us  [swap(): return lax.ppermute(value, 'blk', pairs)]
    ppermute x1, starting transfers between devices: 0.01 us -> 1.34 us  [across(): return lax.ppermute(value, ('guide', 'blk'), pairs)]
    pallas_call x1 -> x3, Pallas kernels: 5.39 us -> 6.2 us  [the longest x1 3.29 us: head(): pl.pallas_call(close_kernel, out_shape=jax.ShapeDtypeStruct((rows // 2, v...]
  transfers between devices with their start and end apart: 23 -> 23, of which waited for: 20 -> 18; matrix products, arithmetic and copies ran while one was open for 0% -> 0% of each run, Pallas kernels for 0% -> 4%
where the time goes in v5:
time: 75.5 us; the launch traced here: 75.3 us
  waiting for transfers between devices  32.8 us (43%)
  starting transfers between devices  27.6 us (37%)
  Pallas kernels  13.8 us (18%)
  local copies, waits for them, and re-layouts  0.88 us (1%)
    ppermute x20, waiting for transfers between devices, swap(): return lax.ppermute(value, 'blk', pairs)  27.7 us
    ppermute x20, starting transfers between devices, swap(): return lax.ppermute(value, 'blk', pairs)  26.3 us
    pallas_call x1, Pallas kernels, attend(): pl.pallas_call(attend_kernel, out_shape=jax.ShapeDtypeStruct((slots, head...  4.27 us
    ppermute x1, waiting for transfers between devices, across(): return lax.ppermute(value, ('guide', 'blk'), pairs)  3.85 us
    pallas_call x1, Pallas kernels, head(): pl.pallas_call(close_kernel, out_shape=jax.ShapeDtypeStruct((rows // 2, v...  3.29 us
    pallas_call x1, Pallas kernels, feed(): pl.pallas_call(feed_kernel, out_shape=[jax.ShapeDtypeStruct(part, F32), j...  2.56 us
    pallas_call x1, Pallas kernels, head(): pl.pallas_call(functools.partial(more_kernel, tile=tile), out_shape=sums,...  1.67 us
  transfers between devices with their start and end apart: 23, of which 18 were waited for; matrix products, arithmetic and copies ran while one was open for 0% of the time, Pallas kernels for 4%

profile of v5, /device:TPU:0, one launch (start us, length us, event | category | flops | bytes accessed | tf_op | source)
XLA Modules:
  0.0 75.3 jit_solution(16633273905811426286)
XLA Ops:
  0.0 4.3 %attend.1.refs_0_ = bf16[8,2048]{1,0:T(8,128)(2,1)} custom-call(s32[128]{0:T(128)} %perm_h.1, s32[1,128]{1,0:T(1,128)} %lengths_h.1, bf16[8,9216]{1,0:T(8,128)(2,1)} %queries_h.1, bf16[8,576]{1,0:T(8,128)(2,1)} %new_h.1, bf16[8,576,256]{2,1,0:T(8,128)(2,1)} %bitcast.27, bf16[16,512,128]{2,1,0:T(8,128)(2,1)} %w_uv.1), custom_call_target="tpu_custom_call" | custom-call | flops 15000000512 | bytes 45000000 | tf_op jit(solution)/shard_map/attend/pallas_call | solution.py:117
  4.3 5.1 %collective-permute-start = (bf16[8,2048]{1,0:T(8,128)(2,1)}, bf16[8,2048]{1,0:T(8,128)(2,1)S(1)}, u32[]{:S(2)}, u32[]{:S(2)}) collective-permute-start(bf16[8,2048]{1,0:T(8,128)(2,1)} %attend.1.refs_0_), channel_id=1, source_target_pairs={{0,12},{1,13},{2,14},{3,15},{4,8},{5,9},{6,10},{7,11},{8,4},{9,5},... | collective-permute-start | bytes 98312 | tf_op jit(solution)/shard_map/ppermute | solution.py:34
  10.1 0.8 %copy-done.7 = bf16[8,2048]{1,0:T(8,128)(2,1)S(1)} copy-done((bf16[8,2048]{1,0:T(8,128)(2,1)S(1)}, bf16[8,2048]{1,0:T(8,128)(2,1)}, u32[]{:S(2)}) %copy-start.7) | copy-done | bytes 32792
  11.5 2.9 %collective-permute-done.1.refs_1_ = bf16[8,2048]{1,0:T(8,128)(2,1)S(1)} collective-permute-done((bf16[8,2048]{1,0:T(8,128)(2,1)}, bf16[8,2048]{1,0:T(8,128)(2,1)S(1)}, u32[]{:S(2)}, u32[]{:S(2)}) %collective-permute-start.1) | collective-permute-done | bytes 32800 | tf_op jit(solution)/shard_map/ppermute | solution.py:34
  14.5 2.5 %collective-permute-start.3 = (bf16[32,2048]{1,0:T(8,128)(2,1)S(1)}, bf16[32,2048]{1,0:T(8,128)(2,1)S(1)}, u32[]{:S(2)}, u32[]{:S(2)}) collective-permute-start(bf16[32,2048]{1,0:T(8,128)(2,1)S(1)} %join.4.v0), channel_id=1, source_target_pairs={{0,3},{1,2},{2,1},{3,0},{4,7},{5,6},{6,5},{7,4},{8,11},{9,10},{10,... | collective-permute-start | bytes 393224 | tf_op jit(solution)/shard_map/ppermute | solution.py:34
  18.0 3.8 %collective-permute-done.3.v3 = bf16[32,2048]{1,0:T(8,128)(2,1)S(1)} collective-permute-done((bf16[32,2048]{1,0:T(8,128)(2,1)S(1)}, bf16[32,2048]{1,0:T(8,128)(2,1)S(1)}, u32[]{:S(2)}, u32[]{:S(2)}) %collective-permute-start.3) | collective-permute-done | bytes 131104 | tf_op jit(solution)/shard_map/ppermute | solution.py:34
  23.2 1.5 %collective-permute-start.6 = (bf16[128,128]{1,0:T(8,128)(2,1)S(1)}, bf16[128,128]{1,0:T(8,128)(2,1)S(1)}, u32[]{:S(2)}, u32[]{:S(2)}) collective-permute-start(bf16[128,128]{1,0:T(8,128)(2,1)S(1)} %project.1.refs_3_), channel_id=1, source_target_pairs={{0,12},{1,13},{2,14},{3,15},{4,8},{5,9},{6,10},{7,11},{8,4},{9,5},... | collective-permute-start | bytes 98312 | tf_op jit(solution)/shard_map/ppermute | solution.py:34
  25.4 2.3 %collective-permute-start.8 = (bf16[128,128]{1,0:T(8,128)(2,1)S(1)}, bf16[128,128]{1,0:T(8,128)(2,1)S(1)}, u32[]{:S(2)}, u32[]{:S(2)}) collective-permute-start(bf16[128,128]{1,0:T(8,128)(2,1)S(1)} %project.1.refs_3_), channel_id=1, source_target_pairs={{0,4},{1,5},{2,6},{3,7},{4,0},{5,1},{6,2},{7,3},{8,12},{9,13},{10,... | collective-permute-start | bytes 98312 | tf_op jit(solution)/shard_map/ppermute | solution.py:34
  27.7 1.3 %collective-permute-done.6.refs_0_ = bf16[128,128]{1,0:T(8,128)(2,1)S(1)} collective-permute-done((bf16[128,128]{1,0:T(8,128)(2,1)S(1)}, bf16[128,128]{1,0:T(8,128)(2,1)S(1)}, u32[]{:S(2)}, u32[]{:S(2)}) %collective-permute-start.6) | collective-permute-done | bytes 32800 | tf_op jit(solution)/shard_map/ppermute | solution.py:34
  29.8 1.5 %collective-permute-start.9 = (bf16[512,128]{1,0:T(8,128)(2,1)S(1)}, bf16[512,128]{1,0:T(8,128)(2,1)S(1)}, u32[]{:S(2)}, u32[]{:S(2)}) collective-permute-start(bf16[512,128]{1,0:T(8,128)(2,1)S(1)} %join.5), channel_id=1, source_target_pairs={{0,3},{1,2},{2,1},{3,0},{4,7},{5,6},{6,5},{7,4},{8,11},{9,10},{10,... | collective-permute-start | bytes 393224 | tf_op jit(solution)/shard_map/ppermute | solution.py:34
  31.4 1.5 %collective-permute-start.10 = (bf16[512,128]{1,0:T(8,128)(2,1)S(1)}, bf16[512,128]{1,0:T(8,128)(2,1)S(1)}, u32[]{:S(2)}, u32[]{:S(2)}) collective-permute-start(bf16[512,128]{1,0:T(8,128)(2,1)S(1)} %join.5), channel_id=1, source_target_pairs={{0,2},{1,3},{2,0},{3,1},{4,6},{5,7},{6,4},{7,5},{8,10},{9,11},{10,... | collective-permute-start | bytes 393224 | tf_op jit(solution)/shard_map/ppermute | solution.py:34
  33.4 2.5 %collective-permute-done.9 = bf16[512,128]{1,0:T(8,128)(2,1)S(1)} collective-permute-done((bf16[512,128]{1,0:T(8,128)(2,1)S(1)}, bf16[512,128]{1,0:T(8,128)(2,1)S(1)}, u32[]{:S(2)}, u32[]{:S(2)}) %collective-permute-start.9) | collective-permute-done | bytes 131104 | tf_op jit(solution)/shard_map/ppermute | solution.py:34
  35.9 1.3 %collective-permute-done.10 = bf16[512,128]{1,0:T(8,128)(2,1)S(1)} collective-permute-done((bf16[512,128]{1,0:T(8,128)(2,1)S(1)}, bf16[512,128]{1,0:T(8,128)(2,1)S(1)}, u32[]{:S(2)}, u32[]{:S(2)}) %collective-permute-start.10) | collective-permute-done | bytes 131104 | tf_op jit(solution)/shard_map/ppermute | solution.py:34
  37.9 2.6 %feed.1 = (f32[128,512]{1,0:T(8,128)S(1)}, bf16[128,512]{1,0:T(8,128)(2,1)S(1)}, bf16[128,512]{1,0:T(8,128)(2,1)S(1)}, bf16[128,512]{1,0:T(8,128)(2,1)S(1)}, bf1...) custom-call(bf16[4,128,128]{2,1,0:T(8,128)(2,1)S(1)} %bitcast.22, bf16[4,128,128]{2,1,0:T(8,128)(2,1)S(1)} %bitcast.23, ...), custom_call_target="tpu_custom_call" | custom-call | flops 40000000000 | bytes 120000000 | tf_op jit(solution)/shard_map/feed/pallas_call | solution.py:205
  40.5 0.9 %collective-permute-start.13 = (bf16[128,512]{1,0:T(8,128)(2,1)S(1)}, bf16[128,512]{1,0:T(8,128)(2,1)S(1)}, u32[]{:S(2)}, u32[]{:S(2)}) collective-permute-start(bf16[128,512]{1,0:T(8,128)(2,1)S(1)} %get-tuple-element.17), channel_id=1, source_target_pairs={{0,1},{1,0},{2,3},{3,2},{4,5},{5,4},{6,7},{7,6},{8,9},{9,8},{10,11... | collective-permute-start | bytes 393224 | tf_op jit(solution)/shard_map/ppermute | solution.py:34
  41.4 1.1 %collective-permute-start.14 = (bf16[128,512]{1,0:T(8,128)(2,1)S(1)}, bf16[128,512]{1,0:T(8,128)(2,1)S(1)}, u32[]{:S(2)}, u32[]{:S(2)}) collective-permute-start(bf16[128,512]{1,0:T(8,128)(2,1)S(1)} %get-tuple-element.19), channel_id=1, source_target_pairs={{0,2},{1,3},{2,0},{3,1},{4,6},{5,7},{6,4},{7,5},{8,10},{9,11},{10,... | collective-permute-start | bytes 393224 | tf_op jit(solution)/shard_map/ppermute | solution.py:34
  42.6 1.5 %collective-permute-start.15 = (bf16[128,512]{1,0:T(8,128)(2,1)S(1)}, bf16[128,512]{1,0:T(8,128)(2,1)S(1)}, u32[]{:S(2)}, u32[]{:S(2)}) collective-permute-start(bf16[128,512]{1,0:T(8,128)(2,1)S(1)} %get-tuple-element.20), channel_id=1, source_target_pairs={{0,3},{1,2},{2,1},{3,0},{4,7},{5,6},{6,5},{7,4},{8,11},{9,10},{10,... | collective-permute-start | bytes 393224 | tf_op jit(solution)/shard_map/ppermute | solution.py:34
  44.1 1.3 %collective-permute-done.12.came = bf16[64,512]{1,0:T(8,128)(2,1)S(1)} collective-permute-done((bf16[64,512]{1,0:T(8,128)(2,1)S(1)}, bf16[64,512]{1,0:T(8,128)(2,1)S(1)}, u32[]{:S(2)}, u32[]{:S(2)}) %collective-permute-start.12) | collective-permute-done | bytes 65568 | tf_op jit(solution)/shard_map/ppermute | solution.py:29
  45.5 0.8 %collective-permute-done.14.p2 = bf16[128,512]{1,0:T(8,128)(2,1)S(1)} collective-permute-done((bf16[128,512]{1,0:T(8,128)(2,1)S(1)}, bf16[128,512]{1,0:T(8,128)(2,1)S(1)}, u32[]{:S(2)}, u32[]{:S(2)}) %collective-permute-start.14) | collective-permute-done | bytes 131104 | tf_op jit(solution)/shard_map/ppermute | solution.py:34
  46.4 2.0 %collective-permute-done.15.p3 = bf16[128,512]{1,0:T(8,128)(2,1)S(1)} collective-permute-done((bf16[128,512]{1,0:T(8,128)(2,1)S(1)}, bf16[128,512]{1,0:T(8,128)(2,1)S(1)}, u32[]{:S(2)}, u32[]{:S(2)}) %collective-permute-start.15) | collective-permute-done | bytes 131104 | tf_op jit(solution)/shard_map/ppermute | solution.py:34
  48.5 1.8 %collective-permute-start.16 = (bf16[64,512]{1,0:T(8,128)(2,1)S(1)}, bf16[64,512]{1,0:T(8,128)(2,1)S(1)}, u32[]{:S(2)}, u32[]{:S(2)}) collective-permute-start(bf16[64,512]{1,0:T(8,128)(2,1)S(1)} %get-tuple-element.21.a), channel_id=1, source_target_pairs={{0,8},{1,9},{2,10},{3,11},{4,12},{5,13},{6,14},{7,15},{8,0},{9,1},... | collective-permute-start | bytes 196616 | tf_op jit(solution)/shard_map/ppermute | solution.py:34
  50.3 1.3 %collective-permute-start.18 = (bf16[64,512]{1,0:T(8,128)(2,1)S(1)}, bf16[64,512]{1,0:T(8,128)(2,1)S(1)}, u32[]{:S(2)}, u32[]{:S(2)}) collective-permute-start(bf16[64,512]{1,0:T(8,128)(2,1)S(1)} %get-tuple-element.22), channel_id=1, source_target_pairs={{0,24},{1,25},{2,26},{3,27},{4,28},{5,29},{6,30},{7,31},{8,16},{9,... | collective-permute-start | bytes 196616 | tf_op jit(solution)/shard_map/ppermute | solution.py:23
  51.6 2.1 %collective-permute-done.16.b = bf16[64,512]{1,0:T(8,128)(2,1)S(1)} collective-permute-done((bf16[64,512]{1,0:T(8,128)(2,1)S(1)}, bf16[64,512]{1,0:T(8,128)(2,1)S(1)}, u32[]{:S(2)}, u32[]{:S(2)}) %collective-permute-start.16) | collective-permute-done | bytes 65568 | tf_op jit(solution)/shard_map/ppermute | solution.py:34
  53.7 3.8 %collective-permute-done.18.d = bf16[64,512]{1,0:T(8,128)(2,1)S(1)} collective-permute-done((bf16[64,512]{1,0:T(8,128)(2,1)S(1)}, bf16[64,512]{1,0:T(8,128)(2,1)S(1)}, u32[]{:S(2)}, u32[]{:S(2)}) %collective-permute-start.18) | collective-permute-done | bytes 65568 | tf_op jit(solution)/shard_map/ppermute | solution.py:23
  57.7 5.5 %collective-permute-done.19.other = bf16[128,512]{1,0:T(8,128)(2,1)S(1)} collective-permute-done((bf16[128,512]{1,0:T(8,128)(2,1)S(1)}, bf16[128,512]{1,0:T(8,128)(2,1)S(1)}, u32[]{:S(2)}, u32[]{:S(2)}) %collective-permute-start.19) | collective-permute-done | bytes 131104 | tf_op jit(solution)/shard_map/ppermute | solution.py:34
  63.3 1.2 %collective-permute-start.22 = (bf16[128,512]{1,0:T(8,128)(2,1)S(1)}, bf16[128,512]{1,0:T(8,128)(2,1)S(1)}, u32[]{:S(2)}, u32[]{:S(2)}) collective-permute-start(bf16[128,512]{1,0:T(8,128)(2,1)S(1)} %finish.1.piece.r0), channel_id=1, source_target_pairs={{0,3},{1,2},{2,1},{3,0},{4,7},{5,6},{6,5},{7,4},{8,11},{9,10},{10,... | collective-permute-start | bytes 393224 | tf_op jit(solution)/shard_map/ppermute | solution.py:34
  64.5 0.9 %collective-permute-start.20 = (bf16[128,512]{1,0:T(8,128)(2,1)S(1)}, bf16[128,512]{1,0:T(8,128)(2,1)S(1)}, u32[]{:S(2)}, u32[]{:S(2)}) collective-permute-start(bf16[128,512]{1,0:T(8,128)(2,1)S(1)} %finish.1.piece.r0), channel_id=1, source_target_pairs={{0,1},{1,0},{2,3},{3,2},{4,5},{5,4},{6,7},{7,6},{8,9},{9,8},{10,11... | collective-permute-start | bytes 393224 | tf_op jit(solution)/shard_map/ppermute | solution.py:34
  65.4 1.4 %collective-permute-start.21 = (bf16[128,512]{1,0:T(8,128)(2,1)S(1)}, bf16[128,512]{1,0:T(8,128)(2,1)S(1)}, u32[]{:S(2)}, u32[]{:S(2)}) collective-permute-start(bf16[128,512]{1,0:T(8,128)(2,1)S(1)} %finish.1.piece.r0), channel_id=1, source_target_pairs={{0,2},{1,3},{2,0},{3,1},{4,6},{5,7},{6,4},{7,5},{8,10},{9,11},{10,... | collective-permute-start | bytes 393224 | tf_op jit(solution)/shard_map/ppermute | solution.py:34
  66.9 1.2 %open.1.old = f32[128,6400]{1,0:T(8,128)S(1)} custom-call(bf16[128,512]{1,0:T(8,128)(2,1)S(1)} %finish.1.piece.r0, f32[1,2048]{1,0:T(1,128)S(1)} %bitcast.15, bf16[2048,6400]{1,0:T(8,128)(2,1)S(1)} %bitcast.14), custom_call_target="tpu_custom_call" | custom-call | flops 2000000000 | bytes 6000000 | tf_op jit(solution)/shard_map/open/pallas_call | solution.py:324
  68.1 2.2 %collective-permute-done.22.piece.r3 = bf16[128,512]{1,0:T(8,128)(2,1)S(1)} collective-permute-done((bf16[128,512]{1,0:T(8,128)(2,1)S(1)}, bf16[128,512]{1,0:T(8,128)(2,1)S(1)}, u32[]{:S(2)}, u32[]{:S(2)}) %collective-permute-start.22) | collective-permute-done | bytes 131104 | tf_op jit(solution)/shard_map/ppermute | solution.py:34
  70.3 1.7 %more.1.acc = f32[128,6400]{1,0:T(8,128)S(1)} custom-call(bf16[128,512]{1,0:T(8,128)(2,1)S(1)} %collective-permute-done.22.piece.r3, f32[1,2048]{1,0:T(1,128)S(1)} %bitcast.16, bf16[2048,6400]{1,0:T(8,128)(2,1)S(1)} %bitcast.14, f32[128,6400]{1,0:T(8,128)S(1)} %open.1.old), custom_call_target="tpu_custom_call", output_to_operand_aliasing={{}: (3, {})} | custom-call | flops 2000000000 | bytes 6000000 | tf_op jit(solution)/shard_map/more/pallas_call | solution.py:333
  72.1 3.3 %close.1 = bf16[64,6400]{1,0:T(8,128)(2,1)} custom-call(bf16[128,512]{1,0:T(8,128)(2,1)S(1)} %finish.1.piece.r0, bf16[128,512]{1,0:T(8,128)(2,1)S(1)} %collective-permute-done.20.r1, bf16[128,512]{1,0:T(8,128)(2,1)S(1)} %collective-permute-done.21.r2, bf16[128,512]{1,0:T(8,128)(2,1)S(1)} %collective-permute-done.22.piece.r3, f32[1,2048]{1,0:T(1,128)S(1)} %bitcast.17, ...), custom_call_target="tpu_custom_call" | custom-call | flops 3000000000 | bytes 9000000 | tf_op jit(solution)/shard_map/close/pallas_call | solution.py:343
  (61 shorter events, 7.0 us)
Async XLA Ops:
  0.0 22.6 %copy-start.9 = (s32[128]{0:T(128)S(1)}, s32[128]{0:T(128)}, u32[]{:S(2)}) copy-start(s32[128]{0:T(128)} %perm_h.1) | copy-start | bytes 1540
  4.3 18.3 %copy-start.5 = (bf16[2048,128]{1,0:T(8,128)(2,1)S(1)}, bf16[2048,128]{1,0:T(8,128)(2,1)}, u32[]{:S(2)}) copy-start(bf16[2048,128]{1,0:T(8,128)(2,1)} %w_out.1) | copy-start | bytes 1572868
  4.3 7.2 %collective-permute-start = (bf16[8,2048]{1,0:T(8,128)(2,1)}, bf16[8,2048]{1,0:T(8,128)(2,1)S(1)}, u32[]{:S(2)}, u32[]{:S(2)}) collective-permute-start(bf16[8,2048]{1,0:T(8,128)(2,1)} %attend.1.refs_0_), channel_id=1, source_target_pairs={{0,12},{1,13},{2,14},{3,15},{4,8},{5,9},{6,10},{7,11},{8,4},{9,5},... | collective-permute-start | bytes 98312 | tf_op jit(solution)/shard_map/ppermute | solution.py:34
  9.4 5.0 %collective-permute-start.1 = (bf16[8,2048]{1,0:T(8,128)(2,1)}, bf16[8,2048]{1,0:T(8,128)(2,1)S(1)}, u32[]{:S(2)}, u32[]{:S(2)}) collective-permute-start(bf16[8,2048]{1,0:T(8,128)(2,1)} %attend.1.refs_0_), channel_id=1, source_target_pairs={{0,8},{1,9},{2,10},{3,11},{4,12},{5,13},{6,14},{7,15},{8,0},{9,1},... | collective-permute-start | bytes 98312 | tf_op jit(solution)/shard_map/ppermute | solution.py:34
  9.4 5.0 %collective-permute-start.2 = (bf16[8,2048]{1,0:T(8,128)(2,1)}, bf16[8,2048]{1,0:T(8,128)(2,1)S(1)}, u32[]{:S(2)}, u32[]{:S(2)}) collective-permute-start(bf16[8,2048]{1,0:T(8,128)(2,1)} %attend.1.refs_0_), channel_id=1, source_target_pairs={{0,4},{1,5},{2,6},{3,7},{4,0},{5,1},{6,2},{7,3},{8,12},{9,13},{10,... | collective-permute-start | bytes 98312 | tf_op jit(solution)/shard_map/ppermute | solution.py:34
  14.5 7.3 %collective-permute-start.3 = (bf16[32,2048]{1,0:T(8,128)(2,1)S(1)}, bf16[32,2048]{1,0:T(8,128)(2,1)S(1)}, u32[]{:S(2)}, u32[]{:S(2)}) collective-permute-start(bf16[32,2048]{1,0:T(8,128)(2,1)S(1)} %join.4.v0), channel_id=1, source_target_pairs={{0,3},{1,2},{2,1},{3,0},{4,7},{5,6},{6,5},{7,4},{8,11},{9,10},{10,... | collective-permute-start | bytes 393224 | tf_op jit(solution)/shard_map/ppermute | solution.py:34
  17.0 5.6 %collective-permute-start.4 = (bf16[32,2048]{1,0:T(8,128)(2,1)S(1)}, bf16[32,2048]{1,0:T(8,128)(2,1)S(1)}, u32[]{:S(2)}, u32[]{:S(2)}) collective-permute-start(bf16[32,2048]{1,0:T(8,128)(2,1)S(1)} %join.4.v0), channel_id=1, source_target_pairs={{0,2},{1,3},{2,0},{3,1},{4,6},{5,7},{6,4},{7,5},{8,10},{9,11},{10,... | collective-permute-start | bytes 393224 | tf_op jit(solution)/shard_map/ppermute | solution.py:34
  17.5 5.1 %collective-permute-start.5 = (bf16[32,2048]{1,0:T(8,128)(2,1)S(1)}, bf16[32,2048]{1,0:T(8,128)(2,1)S(1)}, u32[]{:S(2)}, u32[]{:S(2)}) collective-permute-start(bf16[32,2048]{1,0:T(8,128)(2,1)S(1)} %join.4.v0), channel_id=1, source_target_pairs={{0,1},{1,0},{2,3},{3,2},{4,5},{5,4},{6,7},{7,6},{8,9},{9,8},{10,11... | collective-permute-start | bytes 393224 | tf_op jit(solution)/shard_map/ppermute | solution.py:34
  23.2 5.8 %collective-permute-start.6 = (bf16[128,128]{1,0:T(8,128)(2,1)S(1)}, bf16[128,128]{1,0:T(8,128)(2,1)S(1)}, u32[]{:S(2)}, u32[]{:S(2)}) collective-permute-start(bf16[128,128]{1,0:T(8,128)(2,1)S(1)} %project.1.refs_3_), channel_id=1, source_target_pairs={{0,12},{1,13},{2,14},{3,15},{4,8},{5,9},{6,10},{7,11},{8,4},{9,5},... | collective-permute-start | bytes 98312 | tf_op jit(solution)/shard_map/ppermute | solution.py:34
  24.7 4.8 %collective-permute-start.7 = (bf16[128,128]{1,0:T(8,128)(2,1)S(1)}, bf16[128,128]{1,0:T(8,128)(2,1)S(1)}, u32[]{:S(2)}, u32[]{:S(2)}) collective-permute-start(bf16[128,128]{1,0:T(8,128)(2,1)S(1)} %project.1.refs_3_), channel_id=1, source_target_pairs={{0,8},{1,9},{2,10},{3,11},{4,12},{5,13},{6,14},{7,15},{8,0},{9,1},... | collective-permute-start | bytes 98312 | tf_op jit(solution)/shard_map/ppermute | solution.py:34
  25.4 4.5 %collective-permute-start.8 = (bf16[128,128]{1,0:T(8,128)(2,1)S(1)}, bf16[128,128]{1,0:T(8,128)(2,1)S(1)}, u32[]{:S(2)}, u32[]{:S(2)}) collective-permute-start(bf16[128,128]{1,0:T(8,128)(2,1)S(1)} %project.1.refs_3_), channel_id=1, source_target_pairs={{0,4},{1,5},{2,6},{3,7},{4,0},{5,1},{6,2},{7,3},{8,12},{9,13},{10,... | collective-permute-start | bytes 98312 | tf_op jit(solution)/shard_map/ppermute | solution.py:34
  29.8 37.0 %slice-start = ((s8[26214400]{0:T(1024)(128)(4,1)}), s8[4194304]{0:T(1024)(128)(4,1)S(1)}, s32[]{:S(2)}) async-start(s8[26214400]{0:T(1024)(128)(4,1)} %bitcast.13), calls=%async_computation | async-start | bytes 8388608
  29.8 6.0 %collective-permute-start.9 = (bf16[512,128]{1,0:T(8,128)(2,1)S(1)}, bf16[512,128]{1,0:T(8,128)(2,1)S(1)}, u32[]{:S(2)}, u32[]{:S(2)}) collective-permute-start(bf16[512,128]{1,0:T(8,128)(2,1)S(1)} %join.5), channel_id=1, source_target_pairs={{0,3},{1,2},{2,1},{3,0},{4,7},{5,6},{6,5},{7,4},{8,11},{9,10},{10,... | collective-permute-start | bytes 393224 | tf_op jit(solution)/shard_map/ppermute | solution.py:34
  31.4 5.8 %collective-permute-start.10 = (bf16[512,128]{1,0:T(8,128)(2,1)S(1)}, bf16[512,128]{1,0:T(8,128)(2,1)S(1)}, u32[]{:S(2)}, u32[]{:S(2)}) collective-permute-start(bf16[512,128]{1,0:T(8,128)(2,1)S(1)} %join.5), channel_id=1, source_target_pairs={{0,2},{1,3},{2,0},{3,1},{4,6},{5,7},{6,4},{7,5},{8,10},{9,11},{10,... | collective-permute-start | bytes 393224 | tf_op jit(solution)/shard_map/ppermute | solution.py:34
  32.9 5.0 %collective-permute-start.11 = (bf16[512,128]{1,0:T(8,128)(2,1)S(1)}, bf16[512,128]{1,0:T(8,128)(2,1)S(1)}, u32[]{:S(2)}, u32[]{:S(2)}) collective-permute-start(bf16[512,128]{1,0:T(8,128)(2,1)S(1)} %join.5), channel_id=1, source_target_pairs={{0,1},{1,0},{2,3},{3,2},{4,5},{5,4},{6,7},{7,6},{8,9},{9,8},{10,11... | collective-permute-start | bytes 393224 | tf_op jit(solution)/shard_map/ppermute | solution.py:34
  37.9 28.9 %slice-start.1 = ((s8[26214400]{0:T(1024)(128)(4,1)}), s8[4194304]{0:T(1024)(128)(4,1)S(1)}, s32[]{:S(2)}) async-start(s8[26214400]{0:T(1024)(128)(4,1)} %bitcast.13), calls=%async_computation.1 | async-start | bytes 8388608
  37.9 28.9 %slice-start.2 = ((s8[26214400]{0:T(1024)(128)(4,1)}), s8[4194304]{0:T(1024)(128)(4,1)S(1)}, s32[]{:S(2)}) async-start(s8[26214400]{0:T(1024)(128)(4,1)} %bitcast.13), calls=%async_computation.2 | async-start | bytes 8388608
  37.9 28.9 %slice-start.3 = ((s8[26214400]{0:T(1024)(128)(4,1)}), s8[4194304]{0:T(1024)(128)(4,1)S(1)}, s32[]{:S(2)}) async-start(s8[26214400]{0:T(1024)(128)(4,1)} %bitcast.13), calls=%async_computation.3 | async-start | bytes 8388608
  37.9 28.9 %slice-start.4 = ((s8[26214400]{0:T(1024)(128)(4,1)}), s8[4194304]{0:T(1024)(128)(4,1)S(1)}, s32[]{:S(2)}) async-start(s8[26214400]{0:T(1024)(128)(4,1)} %bitcast.13), calls=%async_computation.4 | async-start | bytes 8388608
  37.9 28.9 %slice-start.5 = ((s8[26214400]{0:T(1024)(128)(4,1)}), s8[4194304]{0:T(1024)(128)(4,1)S(1)}, s32[]{:S(2)}) async-start(s8[26214400]{0:T(1024)(128)(4,1)} %bitcast.13), calls=%async_computation.5 | async-start | bytes 8388608
  37.9 28.9 %slice-start.6 = ((s8[26214400]{0:T(1024)(128)(4,1)}), s8[1048576]{0:T(1024)(128)(4,1)S(1)}, s32[]{:S(2)}) async-start(s8[26214400]{0:T(1024)(128)(4,1)} %bitcast.13), calls=%async_computation.6 | async-start | bytes 2097152
  40.5 5.0 %collective-permute-start.13 = (bf16[128,512]{1,0:T(8,128)(2,1)S(1)}, bf16[128,512]{1,0:T(8,128)(2,1)S(1)}, u32[]{:S(2)}, u32[]{:S(2)}) collective-permute-start(bf16[128,512]{1,0:T(8,128)(2,1)S(1)} %get-tuple-element.17), channel_id=1, source_target_pairs={{0,1},{1,0},{2,3},{3,2},{4,5},{5,4},{6,7},{7,6},{8,9},{9,8},{10,11... | collective-permute-start | bytes 393224 | tf_op jit(solution)/shard_map/ppermute | solution.py:34
  41.4 5.0 %collective-permute-start.14 = (bf16[128,512]{1,0:T(8,128)(2,1)S(1)}, bf16[128,512]{1,0:T(8,128)(2,1)S(1)}, u32[]{:S(2)}, u32[]{:S(2)}) collective-permute-start(bf16[128,512]{1,0:T(8,128)(2,1)S(1)} %get-tuple-element.19), channel_id=1, source_target_pairs={{0,2},{1,3},{2,0},{3,1},{4,6},{5,7},{6,4},{7,5},{8,10},{9,11},{10,... | collective-permute-start | bytes 393224 | tf_op jit(solution)/shard_map/ppermute | solution.py:34
  42.6 5.9 %collective-permute-start.15 = (bf16[128,512]{1,0:T(8,128)(2,1)S(1)}, bf16[128,512]{1,0:T(8,128)(2,1)S(1)}, u32[]{:S(2)}, u32[]{:S(2)}) collective-permute-start(bf16[128,512]{1,0:T(8,128)(2,1)S(1)} %get-tuple-element.20), channel_id=1, source_target_pairs={{0,3},{1,2},{2,1},{3,0},{4,7},{5,6},{6,5},{7,4},{8,11},{9,10},{10,... | collective-permute-start | bytes 393224 | tf_op jit(solution)/shard_map/ppermute | solution.py:34
  44.1 1.3 %collective-permute-start.12 = (bf16[64,512]{1,0:T(8,128)(2,1)S(1)}, bf16[64,512]{1,0:T(8,128)(2,1)S(1)}, u32[]{:S(2)}, u32[]{:S(2)}) collective-permute-start(bf16[64,512]{1,0:T(8,128)(2,1)S(1)} %get-tuple-element.16), channel_id=1, source_target_pairs={{0,16},{16,0},{1,17},{17,1},{2,18},{18,2},{3,19},{19,3},{4,20},{20... | collective-permute-start | bytes 196616 | tf_op jit(solution)/shard_map/ppermute | solution.py:29
  48.5 5.2 %collective-permute-start.16 = (bf16[64,512]{1,0:T(8,128)(2,1)S(1)}, bf16[64,512]{1,0:T(8,128)(2,1)S(1)}, u32[]{:S(2)}, u32[]{:S(2)}) collective-permute-start(bf16[64,512]{1,0:T(8,128)(2,1)S(1)} %get-tuple-element.21.a), channel_id=1, source_target_pairs={{0,8},{1,9},{2,10},{3,11},{4,12},{5,13},{6,14},{7,15},{8,0},{9,1},... | collective-permute-start | bytes 196616 | tf_op jit(solution)/shard_map/ppermute | solution.py:34
  50.3 3.5 %collective-permute-start.17 = (bf16[64,512]{1,0:T(8,128)(2,1)S(1)}, bf16[64,512]{1,0:T(8,128)(2,1)S(1)}, u32[]{:S(2)}, u32[]{:S(2)}) collective-permute-start(bf16[64,512]{1,0:T(8,128)(2,1)S(1)} %get-tuple-element.22), channel_id=1, source_target_pairs={{0,16},{16,0},{1,17},{17,1},{2,18},{18,2},{3,19},{19,3},{4,20},{20... | collective-permute-start | bytes 196616 | tf_op jit(solution)/shard_map/ppermute | solution.py:29
  50.3 7.3 %collective-permute-start.18 = (bf16[64,512]{1,0:T(8,128)(2,1)S(1)}, bf16[64,512]{1,0:T(8,128)(2,1)S(1)}, u32[]{:S(2)}, u32[]{:S(2)}) collective-permute-start(bf16[64,512]{1,0:T(8,128)(2,1)S(1)} %get-tuple-element.22), channel_id=1, source_target_pairs={{0,24},{1,25},{2,26},{3,27},{4,28},{5,29},{6,30},{7,31},{8,16},{9,... | collective-permute-start | bytes 196616 | tf_op jit(solution)/shard_map/ppermute | solution.py:23
  57.6 5.6 %collective-permute-start.19 = (bf16[128,512]{1,0:T(8,128)(2,1)S(1)}, bf16[128,512]{1,0:T(8,128)(2,1)S(1)}, u32[]{:S(2)}, u32[]{:S(2)}) collective-permute-start(bf16[128,512]{1,0:T(8,128)(2,1)S(1)} %pair.1.own), channel_id=1, source_target_pairs={{0,4},{1,5},{2,6},{3,7},{4,0},{5,1},{6,2},{7,3},{8,12},{9,13},{10,... | collective-permute-start | bytes 393224 | tf_op jit(solution)/shard_map/ppermute | solution.py:34
  63.3 7.1 %collective-permute-start.22 = (bf16[128,512]{1,0:T(8,128)(2,1)S(1)}, bf16[128,512]{1,0:T(8,128)(2,1)S(1)}, u32[]{:S(2)}, u32[]{:S(2)}) collective-permute-start(bf16[128,512]{1,0:T(8,128)(2,1)S(1)} %finish.1.piece.r0), channel_id=1, source_target_pairs={{0,3},{1,2},{2,1},{3,0},{4,7},{5,6},{6,5},{7,4},{8,11},{9,10},{10,... | collective-permute-start | bytes 393224 | tf_op jit(solution)/shard_map/ppermute | solution.py:34
  64.5 7.5 %collective-permute-start.20 = (bf16[128,512]{1,0:T(8,128)(2,1)S(1)}, bf16[128,512]{1,0:T(8,128)(2,1)S(1)}, u32[]{:S(2)}, u32[]{:S(2)}) collective-permute-start(bf16[128,512]{1,0:T(8,128)(2,1)S(1)} %finish.1.piece.r0), channel_id=1, source_target_pairs={{0,1},{1,0},{2,3},{3,2},{4,5},{5,4},{6,7},{7,6},{8,9},{9,8},{10,11... | collective-permute-start | bytes 393224 | tf_op jit(solution)/shard_map/ppermute | solution.py:34
  65.4 6.6 %collective-permute-start.21 = (bf16[128,512]{1,0:T(8,128)(2,1)S(1)}, bf16[128,512]{1,0:T(8,128)(2,1)S(1)}, u32[]{:S(2)}, u32[]{:S(2)}) collective-permute-start(bf16[128,512]{1,0:T(8,128)(2,1)S(1)} %finish.1.piece.r0), channel_id=1, source_target_pairs={{0,2},{1,3},{2,0},{3,1},{4,6},{5,7},{6,4},{7,5},{8,10},{9,11},{10,... | collective-permute-start | bytes 393224 | tf_op jit(solution)/shard_map/ppermute | solution.py:34
  (8 other events, 99.5 us)

commit v6 on v5

--- a/solution.py
+++ b/solution.py
@@ -221,7 +221,7 @@
     )(*reversed(pieces), gain, w_gate, w_up, w_down)
 
 
-def part_kernel(own, p1, p2, p3, stay, go):
+def part_kernel(p3, p2, p1, own, stay, go):
     total = own[...] + p1[...].astype(F32) + p2[...].astype(F32) + p3[...].astype(F32)
     half = total.shape[0] // 2
     first, last = total[:half], total[half:]
@@ -230,7 +230,7 @@
     go[...] = jnp.where(lower, last, first).astype(BF)
 
 
-def pair_kernel(a, b, c, d, out):
+def pair_kernel(d, c, b, a, out):
     half = a.shape[0]
     out[:half, :] = (a[...].astype(F32) + b[...].astype(F32)).astype(BF)
     out[half:, :] = (c[...].astype(F32) + d[...].astype(F32)).astype(BF)
@@ -411,9 +411,9 @@
     arrived = [swap(chunk, mask) for chunk, mask in zip(chunks, (1, 2, 3))]
     came, arrived[0] = lax.optimization_barrier((came, arrived[0]))
     half, part = stay.shape, own.shape
-    mine, his = small(part_kernel, "part", (half, half), own, *arrived)
+    mine, his = small(part_kernel, "part", (half, half), *reversed(arrived), own)
     sums = (mine, swap(mine, 8), partner(his, "guide", 0), across(his, 8))
-    (total,) = small(pair_kernel, "pair", (part,), *sums)
+    (total,) = small(pair_kernel, "pair", (part,), *reversed(sums))
     (after,) = small(finish_kernel, "finish", (part,), total, swap(total, 4), stay, came)
     return head(after, guide_scale[None], head_gain[None], w_head)
 

time: 75.5 us -> 75.5 us (level)
    ppermute x2, starting transfers between devices: 0.01 us -> 1.78 us  [partner(): return lax.ppermute(value, axis, pairs)]
    ppermute x1, starting transfers between devices: 1.34 us -> 0.07 us  [across(): return lax.ppermute(value, ('guide', 'blk'), pairs)]
where the time goes in v6:
time: 75.5 us; the launch traced here: 75.3 us
  waiting for transfers between devices  32.8 us (43%)
  starting transfers between devices  27.6 us (37%)
  Pallas kernels  13.8 us (18%)
  local copies, waits for them, and re-layouts  0.88 us (1%)
    ppermute x20, waiting for transfers between devices, swap(): return lax.ppermute(value, 'blk', pairs)  27.8 us
    ppermute x20, starting transfers between devices, swap(): return lax.ppermute(value, 'blk', pairs)  25.8 us
    pallas_call x1, Pallas kernels, attend(): pl.pallas_call(attend_kernel, out_shape=jax.ShapeDtypeStruct((slots, head...  4.27 us
    ppermute x1, waiting for transfers between devices, across(): return lax.ppermute(value, ('guide', 'blk'), pairs)  3.78 us
    pallas_call x1, Pallas kernels, head(): pl.pallas_call(close_kernel, out_shape=jax.ShapeDtypeStruct((rows // 2, v...  3.29 us
    pallas_call x1, Pallas kernels, feed(): pl.pallas_call(feed_kernel, out_shape=[jax.ShapeDtypeStruct(part, F32), j...  2.56 us
    ppermute x2, starting transfers between devices, partner(): return lax.ppermute(value, axis, pairs)  1.78 us
    pallas_call x1, Pallas kernels, head(): pl.pallas_call(functools.partial(more_kernel, tile=tile), out_shape=sums,...  1.67 us
  transfers between devices with their start and end apart: 23, of which 18 were waited for; matrix products, arithmetic and copies ran while one was open for 0% of the time, Pallas kernels for 4%

profile of v6, /device:TPU:0, one launch (start us, length us, event | category | flops | bytes accessed | tf_op | source)
XLA Modules:
  0.0 75.3 jit_solution(5593988875367050545)
XLA Ops:
  0.0 4.3 %attend.1.refs_0_ = bf16[8,2048]{1,0:T(8,128)(2,1)} custom-call(s32[128]{0:T(128)} %perm_h.1, s32[1,128]{1,0:T(1,128)} %lengths_h.1, bf16[8,9216]{1,0:T(8,128)(2,1)} %queries_h.1, bf16[8,576]{1,0:T(8,128)(2,1)} %new_h.1, bf16[8,576,256]{2,1,0:T(8,128)(2,1)} %bitcast.27, bf16[16,512,128]{2,1,0:T(8,128)(2,1)} %w_uv.1), custom_call_target="tpu_custom_call" | custom-call | flops 15000000512 | bytes 45000000 | tf_op jit(solution)/shard_map/attend/pallas_call | solution.py:117
  4.3 5.1 %collective-permute-start = (bf16[8,2048]{1,0:T(8,128)(2,1)}, bf16[8,2048]{1,0:T(8,128)(2,1)S(1)}, u32[]{:S(2)}, u32[]{:S(2)}) collective-permute-start(bf16[8,2048]{1,0:T(8,128)(2,1)} %attend.1.refs_0_), channel_id=1, source_target_pairs={{0,12},{1,13},{2,14},{3,15},{4,8},{5,9},{6,10},{7,11},{8,4},{9,5},... | collective-permute-start | bytes 98312 | tf_op jit(solution)/shard_map/ppermute | solution.py:34
  10.1 0.8 %copy-done.7 = bf16[8,2048]{1,0:T(8,128)(2,1)S(1)} copy-done((bf16[8,2048]{1,0:T(8,128)(2,1)S(1)}, bf16[8,2048]{1,0:T(8,128)(2,1)}, u32[]{:S(2)}) %copy-start.7) | copy-done | bytes 32792
  11.5 2.9 %collective-permute-done.1.refs_1_ = bf16[8,2048]{1,0:T(8,128)(2,1)S(1)} collective-permute-done((bf16[8,2048]{1,0:T(8,128)(2,1)}, bf16[8,2048]{1,0:T(8,128)(2,1)S(1)}, u32[]{:S(2)}, u32[]{:S(2)}) %collective-permute-start.1) | collective-permute-done | bytes 32800 | tf_op jit(solution)/shard_map/ppermute | solution.py:34
  14.5 2.5 %collective-permute-start.3 = (bf16[32,2048]{1,0:T(8,128)(2,1)S(1)}, bf16[32,2048]{1,0:T(8,128)(2,1)S(1)}, u32[]{:S(2)}, u32[]{:S(2)}) collective-permute-start(bf16[32,2048]{1,0:T(8,128)(2,1)S(1)} %join.4.v0), channel_id=1, source_target_pairs={{0,3},{1,2},{2,1},{3,0},{4,7},{5,6},{6,5},{7,4},{8,11},{9,10},{10,... | collective-permute-start | bytes 393224 | tf_op jit(solution)/shard_map/ppermute | solution.py:34
  18.0 3.8 %collective-permute-done.3.v3 = bf16[32,2048]{1,0:T(8,128)(2,1)S(1)} collective-permute-done((bf16[32,2048]{1,0:T(8,128)(2,1)S(1)}, bf16[32,2048]{1,0:T(8,128)(2,1)S(1)}, u32[]{:S(2)}, u32[]{:S(2)}) %collective-permute-start.3) | collective-permute-done | bytes 131104 | tf_op jit(solution)/shard_map/ppermute | solution.py:34
  23.2 1.5 %collective-permute-start.6 = (bf16[128,128]{1,0:T(8,128)(2,1)S(1)}, bf16[128,128]{1,0:T(8,128)(2,1)S(1)}, u32[]{:S(2)}, u32[]{:S(2)}) collective-permute-start(bf16[128,128]{1,0:T(8,128)(2,1)S(1)} %project.1.refs_3_), channel_id=1, source_target_pairs={{0,12},{1,13},{2,14},{3,15},{4,8},{5,9},{6,10},{7,11},{8,4},{9,5},... | collective-permute-start | bytes 98312 | tf_op jit(solution)/shard_map/ppermute | solution.py:34
  25.4 2.3 %collective-permute-start.8 = (bf16[128,128]{1,0:T(8,128)(2,1)S(1)}, bf16[128,128]{1,0:T(8,128)(2,1)S(1)}, u32[]{:S(2)}, u32[]{:S(2)}) collective-permute-start(bf16[128,128]{1,0:T(8,128)(2,1)S(1)} %project.1.refs_3_), channel_id=1, source_target_pairs={{0,4},{1,5},{2,6},{3,7},{4,0},{5,1},{6,2},{7,3},{8,12},{9,13},{10,... | collective-permute-start | bytes 98312 | tf_op jit(solution)/shard_map/ppermute | solution.py:34
  27.7 1.3 %collective-permute-done.6.refs_0_ = bf16[128,128]{1,0:T(8,128)(2,1)S(1)} collective-permute-done((bf16[128,128]{1,0:T(8,128)(2,1)S(1)}, bf16[128,128]{1,0:T(8,128)(2,1)S(1)}, u32[]{:S(2)}, u32[]{:S(2)}) %collective-permute-start.6) | collective-permute-done | bytes 32800 | tf_op jit(solution)/shard_map/ppermute | solution.py:34
  29.8 1.5 %collective-permute-start.9 = (bf16[512,128]{1,0:T(8,128)(2,1)S(1)}, bf16[512,128]{1,0:T(8,128)(2,1)S(1)}, u32[]{:S(2)}, u32[]{:S(2)}) collective-permute-start(bf16[512,128]{1,0:T(8,128)(2,1)S(1)} %join.5), channel_id=1, source_target_pairs={{0,3},{1,2},{2,1},{3,0},{4,7},{5,6},{6,5},{7,4},{8,11},{9,10},{10,... | collective-permute-start | bytes 393224 | tf_op jit(solution)/shard_map/ppermute | solution.py:34
  31.4 1.5 %collective-permute-start.10 = (bf16[512,128]{1,0:T(8,128)(2,1)S(1)}, bf16[512,128]{1,0:T(8,128)(2,1)S(1)}, u32[]{:S(2)}, u32[]{:S(2)}) collective-permute-start(bf16[512,128]{1,0:T(8,128)(2,1)S(1)} %join.5), channel_id=1, source_target_pairs={{0,2},{1,3},{2,0},{3,1},{4,6},{5,7},{6,4},{7,5},{8,10},{9,11},{10,... | collective-permute-start | bytes 393224 | tf_op jit(solution)/shard_map/ppermute | solution.py:34
  33.4 2.5 %collective-permute-done.9 = bf16[512,128]{1,0:T(8,128)(2,1)S(1)} collective-permute-done((bf16[512,128]{1,0:T(8,128)(2,1)S(1)}, bf16[512,128]{1,0:T(8,128)(2,1)S(1)}, u32[]{:S(2)}, u32[]{:S(2)}) %collective-permute-start.9) | collective-permute-done | bytes 131104 | tf_op jit(solution)/shard_map/ppermute | solution.py:34
  35.9 1.3 %collective-permute-done.10 = bf16[512,128]{1,0:T(8,128)(2,1)S(1)} collective-permute-done((bf16[512,128]{1,0:T(8,128)(2,1)S(1)}, bf16[512,128]{1,0:T(8,128)(2,1)S(1)}, u32[]{:S(2)}, u32[]{:S(2)}) %collective-permute-start.10) | collective-permute-done | bytes 131104 | tf_op jit(solution)/shard_map/ppermute | solution.py:34
  37.9 2.6 %feed.1 = (f32[128,512]{1,0:T(8,128)S(1)}, bf16[128,512]{1,0:T(8,128)(2,1)S(1)}, bf16[128,512]{1,0:T(8,128)(2,1)S(1)}, bf16[128,512]{1,0:T(8,128)(2,1)S(1)}, bf1...) custom-call(bf16[4,128,128]{2,1,0:T(8,128)(2,1)S(1)} %bitcast.22, bf16[4,128,128]{2,1,0:T(8,128)(2,1)S(1)} %bitcast.23, ...), custom_call_target="tpu_custom_call" | custom-call | flops 40000000000 | bytes 120000000 | tf_op jit(solution)/shard_map/feed/pallas_call | solution.py:205
  40.5 0.9 %collective-permute-start.15 = (bf16[128,512]{1,0:T(8,128)(2,1)S(1)}, bf16[128,512]{1,0:T(8,128)(2,1)S(1)}, u32[]{:S(2)}, u32[]{:S(2)}) collective-permute-start(bf16[128,512]{1,0:T(8,128)(2,1)S(1)} %get-tuple-element.18), channel_id=1, source_target_pairs={{0,1},{1,0},{2,3},{3,2},{4,5},{5,4},{6,7},{7,6},{8,9},{9,8},{10,11... | collective-permute-start | bytes 393224 | tf_op jit(solution)/shard_map/ppermute | solution.py:34
  41.4 1.4 %collective-permute-start.12 = (bf16[128,512]{1,0:T(8,128)(2,1)S(1)}, bf16[128,512]{1,0:T(8,128)(2,1)S(1)}, u32[]{:S(2)}, u32[]{:S(2)}) collective-permute-start(bf16[128,512]{1,0:T(8,128)(2,1)S(1)} %get-tuple-element.15), channel_id=1, source_target_pairs={{0,3},{1,2},{2,1},{3,0},{4,7},{5,6},{6,5},{7,4},{8,11},{9,10},{10,... | collective-permute-start | bytes 393224 | tf_op jit(solution)/shard_map/ppermute | solution.py:34
  42.8 1.2 %collective-permute-start.13 = (bf16[128,512]{1,0:T(8,128)(2,1)S(1)}, bf16[128,512]{1,0:T(8,128)(2,1)S(1)}, u32[]{:S(2)}, u32[]{:S(2)}) collective-permute-start(bf16[128,512]{1,0:T(8,128)(2,1)S(1)} %get-tuple-element.16), channel_id=1, source_target_pairs={{0,2},{1,3},{2,0},{3,1},{4,6},{5,7},{6,4},{7,5},{8,10},{9,11},{10,... | collective-permute-start | bytes 393224 | tf_op jit(solution)/shard_map/ppermute | solution.py:34
  44.1 1.3 %collective-permute-done.14.came = bf16[64,512]{1,0:T(8,128)(2,1)S(1)} collective-permute-done((bf16[64,512]{1,0:T(8,128)(2,1)S(1)}, bf16[64,512]{1,0:T(8,128)(2,1)S(1)}, u32[]{:S(2)}, u32[]{:S(2)}) %collective-permute-start.14) | collective-permute-done | bytes 65568 | tf_op jit(solution)/shard_map/ppermute | solution.py:29
  45.5 1.8 %collective-permute-done.12.p3 = bf16[128,512]{1,0:T(8,128)(2,1)S(1)} collective-permute-done((bf16[128,512]{1,0:T(8,128)(2,1)S(1)}, bf16[128,512]{1,0:T(8,128)(2,1)S(1)}, u32[]{:S(2)}, u32[]{:S(2)}) %collective-permute-start.12) | collective-permute-done | bytes 131104 | tf_op jit(solution)/shard_map/ppermute | solution.py:34
  47.4 1.3 %collective-permute-done.13.p2 = bf16[128,512]{1,0:T(8,128)(2,1)S(1)} collective-permute-done((bf16[128,512]{1,0:T(8,128)(2,1)S(1)}, bf16[128,512]{1,0:T(8,128)(2,1)S(1)}, u32[]{:S(2)}, u32[]{:S(2)}) %collective-permute-start.13) | collective-permute-done | bytes 131104 | tf_op jit(solution)/shard_map/ppermute | solution.py:34
  48.8 1.8 %collective-permute-start.17 = (bf16[64,512]{1,0:T(8,128)(2,1)S(1)}, bf16[64,512]{1,0:T(8,128)(2,1)S(1)}, u32[]{:S(2)}, u32[]{:S(2)}) collective-permute-start(bf16[64,512]{1,0:T(8,128)(2,1)S(1)} %get-tuple-element.21), channel_id=1, source_target_pairs={{0,16},{16,0},{1,17},{17,1},{2,18},{18,2},{3,19},{19,3},{4,20},{20... | collective-permute-start | bytes 196616 | tf_op jit(solution)/shard_map/ppermute | solution.py:29
  50.6 1.3 %collective-permute-start.18 = (bf16[64,512]{1,0:T(8,128)(2,1)S(1)}, bf16[64,512]{1,0:T(8,128)(2,1)S(1)}, u32[]{:S(2)}, u32[]{:S(2)}) collective-permute-start(bf16[64,512]{1,0:T(8,128)(2,1)S(1)} %get-tuple-element.22.a), channel_id=1, source_target_pairs={{0,8},{1,9},{2,10},{3,11},{4,12},{5,13},{6,14},{7,15},{8,0},{9,1},... | collective-permute-start | bytes 196616 | tf_op jit(solution)/shard_map/ppermute | solution.py:34
  51.9 3.8 %collective-permute-done.16.d = bf16[64,512]{1,0:T(8,128)(2,1)S(1)} collective-permute-done((bf16[64,512]{1,0:T(8,128)(2,1)S(1)}, bf16[64,512]{1,0:T(8,128)(2,1)S(1)}, u32[]{:S(2)}, u32[]{:S(2)}) %collective-permute-start.16) | collective-permute-done | bytes 65568 | tf_op jit(solution)/shard_map/ppermute | solution.py:23
  55.7 1.9 %collective-permute-done.18.b = bf16[64,512]{1,0:T(8,128)(2,1)S(1)} collective-permute-done((bf16[64,512]{1,0:T(8,128)(2,1)S(1)}, bf16[64,512]{1,0:T(8,128)(2,1)S(1)}, u32[]{:S(2)}, u32[]{:S(2)}) %collective-permute-start.18) | collective-permute-done | bytes 65568 | tf_op jit(solution)/shard_map/ppermute | solution.py:34
  57.7 5.5 %collective-permute-done.19.other = bf16[128,512]{1,0:T(8,128)(2,1)S(1)} collective-permute-done((bf16[128,512]{1,0:T(8,128)(2,1)S(1)}, bf16[128,512]{1,0:T(8,128)(2,1)S(1)}, u32[]{:S(2)}, u32[]{:S(2)}) %collective-permute-start.19) | collective-permute-done | bytes 131104 | tf_op jit(solution)/shard_map/ppermute | solution.py:34
  63.2 1.6 %collective-permute-start.22 = (bf16[128,512]{1,0:T(8,128)(2,1)S(1)}, bf16[128,512]{1,0:T(8,128)(2,1)S(1)}, u32[]{:S(2)}, u32[]{:S(2)}) collective-permute-start(bf16[128,512]{1,0:T(8,128)(2,1)S(1)} %finish.1.piece.r0), channel_id=1, source_target_pairs={{0,3},{1,2},{2,1},{3,0},{4,7},{5,6},{6,5},{7,4},{8,11},{9,10},{10,... | collective-permute-start | bytes 393224 | tf_op jit(solution)/shard_map/ppermute | solution.py:34
  64.8 1.2 %collective-permute-start.20 = (bf16[128,512]{1,0:T(8,128)(2,1)S(1)}, bf16[128,512]{1,0:T(8,128)(2,1)S(1)}, u32[]{:S(2)}, u32[]{:S(2)}) collective-permute-start(bf16[128,512]{1,0:T(8,128)(2,1)S(1)} %finish.1.piece.r0), channel_id=1, source_target_pairs={{0,1},{1,0},{2,3},{3,2},{4,5},{5,4},{6,7},{7,6},{8,9},{9,8},{10,11... | collective-permute-start | bytes 393224 | tf_op jit(solution)/shard_map/ppermute | solution.py:34
  66.0 0.8 %collective-permute-start.21 = (bf16[128,512]{1,0:T(8,128)(2,1)S(1)}, bf16[128,512]{1,0:T(8,128)(2,1)S(1)}, u32[]{:S(2)}, u32[]{:S(2)}) collective-permute-start(bf16[128,512]{1,0:T(8,128)(2,1)S(1)} %finish.1.piece.r0), channel_id=1, source_target_pairs={{0,2},{1,3},{2,0},{3,1},{4,6},{5,7},{6,4},{7,5},{8,10},{9,11},{10,... | collective-permute-start | bytes 393224 | tf_op jit(solution)/shard_map/ppermute | solution.py:34
  66.9 1.2 %open.1.old = f32[128,6400]{1,0:T(8,128)S(1)} custom-call(bf16[128,512]{1,0:T(8,128)(2,1)S(1)} %finish.1.piece.r0, f32[1,2048]{1,0:T(1,128)S(1)} %bitcast.15, bf16[2048,6400]{1,0:T(8,128)(2,1)S(1)} %bitcast.14), custom_call_target="tpu_custom_call" | custom-call | flops 2000000000 | bytes 6000000 | tf_op jit(solution)/shard_map/open/pallas_call | solution.py:324
  68.1 2.2 %collective-permute-done.22.piece.r3 = bf16[128,512]{1,0:T(8,128)(2,1)S(1)} collective-permute-done((bf16[128,512]{1,0:T(8,128)(2,1)S(1)}, bf16[128,512]{1,0:T(8,128)(2,1)S(1)}, u32[]{:S(2)}, u32[]{:S(2)}) %collective-permute-start.22) | collective-permute-done | bytes 131104 | tf_op jit(solution)/shard_map/ppermute | solution.py:34
  70.3 1.7 %more.1.acc = f32[128,6400]{1,0:T(8,128)S(1)} custom-call(bf16[128,512]{1,0:T(8,128)(2,1)S(1)} %collective-permute-done.22.piece.r3, f32[1,2048]{1,0:T(1,128)S(1)} %bitcast.16, bf16[2048,6400]{1,0:T(8,128)(2,1)S(1)} %bitcast.14, f32[128,6400]{1,0:T(8,128)S(1)} %open.1.old), custom_call_target="tpu_custom_call", output_to_operand_aliasing={{}: (3, {})} | custom-call | flops 2000000000 | bytes 6000000 | tf_op jit(solution)/shard_map/more/pallas_call | solution.py:333
  72.0 3.3 %close.1 = bf16[64,6400]{1,0:T(8,128)(2,1)} custom-call(bf16[128,512]{1,0:T(8,128)(2,1)S(1)} %finish.1.piece.r0, bf16[128,512]{1,0:T(8,128)(2,1)S(1)} %collective-permute-done.20.r1, bf16[128,512]{1,0:T(8,128)(2,1)S(1)} %collective-permute-done.21.r2, bf16[128,512]{1,0:T(8,128)(2,1)S(1)} %collective-permute-done.22.piece.r3, f32[1,2048]{1,0:T(1,128)S(1)} %bitcast.17, ...), custom_call_target="tpu_custom_call" | custom-call | flops 3000000000 | bytes 9000000 | tf_op jit(solution)/shard_map/close/pallas_call | solution.py:343
  (61 shorter events, 7.1 us)
Async XLA Ops:
  0.0 22.6 %copy-start.9 = (s32[128]{0:T(128)S(1)}, s32[128]{0:T(128)}, u32[]{:S(2)}) copy-start(s32[128]{0:T(128)} %perm_h.1) | copy-start | bytes 1540
  4.3 18.3 %copy-start.5 = (bf16[2048,128]{1,0:T(8,128)(2,1)S(1)}, bf16[2048,128]{1,0:T(8,128)(2,1)}, u32[]{:S(2)}) copy-start(bf16[2048,128]{1,0:T(8,128)(2,1)} %w_out.1) | copy-start | bytes 1572868
  4.3 7.2 %collective-permute-start = (bf16[8,2048]{1,0:T(8,128)(2,1)}, bf16[8,2048]{1,0:T(8,128)(2,1)S(1)}, u32[]{:S(2)}, u32[]{:S(2)}) collective-permute-start(bf16[8,2048]{1,0:T(8,128)(2,1)} %attend.1.refs_0_), channel_id=1, source_target_pairs={{0,12},{1,13},{2,14},{3,15},{4,8},{5,9},{6,10},{7,11},{8,4},{9,5},... | collective-permute-start | bytes 98312 | tf_op jit(solution)/shard_map/ppermute | solution.py:34
  9.4 5.0 %collective-permute-start.1 = (bf16[8,2048]{1,0:T(8,128)(2,1)}, bf16[8,2048]{1,0:T(8,128)(2,1)S(1)}, u32[]{:S(2)}, u32[]{:S(2)}) collective-permute-start(bf16[8,2048]{1,0:T(8,128)(2,1)} %attend.1.refs_0_), channel_id=1, source_target_pairs={{0,8},{1,9},{2,10},{3,11},{4,12},{5,13},{6,14},{7,15},{8,0},{9,1},... | collective-permute-start | bytes 98312 | tf_op jit(solution)/shard_map/ppermute | solution.py:34
  9.4 5.0 %collective-permute-start.2 = (bf16[8,2048]{1,0:T(8,128)(2,1)}, bf16[8,2048]{1,0:T(8,128)(2,1)S(1)}, u32[]{:S(2)}, u32[]{:S(2)}) collective-permute-start(bf16[8,2048]{1,0:T(8,128)(2,1)} %attend.1.refs_0_), channel_id=1, source_target_pairs={{0,4},{1,5},{2,6},{3,7},{4,0},{5,1},{6,2},{7,3},{8,12},{9,13},{10,... | collective-permute-start | bytes 98312 | tf_op jit(solution)/shard_map/ppermute | solution.py:34
  14.5 7.3 %collective-permute-start.3 = (bf16[32,2048]{1,0:T(8,128)(2,1)S(1)}, bf16[32,2048]{1,0:T(8,128)(2,1)S(1)}, u32[]{:S(2)}, u32[]{:S(2)}) collective-permute-start(bf16[32,2048]{1,0:T(8,128)(2,1)S(1)} %join.4.v0), channel_id=1, source_target_pairs={{0,3},{1,2},{2,1},{3,0},{4,7},{5,6},{6,5},{7,4},{8,11},{9,10},{10,... | collective-permute-start | bytes 393224 | tf_op jit(solution)/shard_map/ppermute | solution.py:34
  17.0 5.6 %collective-permute-start.4 = (bf16[32,2048]{1,0:T(8,128)(2,1)S(1)}, bf16[32,2048]{1,0:T(8,128)(2,1)S(1)}, u32[]{:S(2)}, u32[]{:S(2)}) collective-permute-start(bf16[32,2048]{1,0:T(8,128)(2,1)S(1)} %join.4.v0), channel_id=1, source_target_pairs={{0,2},{1,3},{2,0},{3,1},{4,6},{5,7},{6,4},{7,5},{8,10},{9,11},{10,... | collective-permute-start | bytes 393224 | tf_op jit(solution)/shard_map/ppermute | solution.py:34
  17.5 5.1 %collective-permute-start.5 = (bf16[32,2048]{1,0:T(8,128)(2,1)S(1)}, bf16[32,2048]{1,0:T(8,128)(2,1)S(1)}, u32[]{:S(2)}, u32[]{:S(2)}) collective-permute-start(bf16[32,2048]{1,0:T(8,128)(2,1)S(1)} %join.4.v0), channel_id=1, source_target_pairs={{0,1},{1,0},{2,3},{3,2},{4,5},{5,4},{6,7},{7,6},{8,9},{9,8},{10,11... | collective-permute-start | bytes 393224 | tf_op jit(solution)/shard_map/ppermute | solution.py:34
  23.2 5.8 %collective-permute-start.6 = (bf16[128,128]{1,0:T(8,128)(2,1)S(1)}, bf16[128,128]{1,0:T(8,128)(2,1)S(1)}, u32[]{:S(2)}, u32[]{:S(2)}) collective-permute-start(bf16[128,128]{1,0:T(8,128)(2,1)S(1)} %project.1.refs_3_), channel_id=1, source_target_pairs={{0,12},{1,13},{2,14},{3,15},{4,8},{5,9},{6,10},{7,11},{8,4},{9,5},... | collective-permute-start | bytes 98312 | tf_op jit(solution)/shard_map/ppermute | solution.py:34
  24.7 4.8 %collective-permute-start.7 = (bf16[128,128]{1,0:T(8,128)(2,1)S(1)}, bf16[128,128]{1,0:T(8,128)(2,1)S(1)}, u32[]{:S(2)}, u32[]{:S(2)}) collective-permute-start(bf16[128,128]{1,0:T(8,128)(2,1)S(1)} %project.1.refs_3_), channel_id=1, source_target_pairs={{0,8},{1,9},{2,10},{3,11},{4,12},{5,13},{6,14},{7,15},{8,0},{9,1},... | collective-permute-start | bytes 98312 | tf_op jit(solution)/shard_map/ppermute | solution.py:34
  25.4 4.5 %collective-permute-start.8 = (bf16[128,128]{1,0:T(8,128)(2,1)S(1)}, bf16[128,128]{1,0:T(8,128)(2,1)S(1)}, u32[]{:S(2)}, u32[]{:S(2)}) collective-permute-start(bf16[128,128]{1,0:T(8,128)(2,1)S(1)} %project.1.refs_3_), channel_id=1, source_target_pairs={{0,4},{1,5},{2,6},{3,7},{4,0},{5,1},{6,2},{7,3},{8,12},{9,13},{10,... | collective-permute-start | bytes 98312 | tf_op jit(solution)/shard_map/ppermute | solution.py:34
  29.8 37.0 %slice-start = ((s8[26214400]{0:T(1024)(128)(4,1)}), s8[4194304]{0:T(1024)(128)(4,1)S(1)}, s32[]{:S(2)}) async-start(s8[26214400]{0:T(1024)(128)(4,1)} %bitcast.13), calls=%async_computation | async-start | bytes 8388608
  29.8 6.0 %collective-permute-start.9 = (bf16[512,128]{1,0:T(8,128)(2,1)S(1)}, bf16[512,128]{1,0:T(8,128)(2,1)S(1)}, u32[]{:S(2)}, u32[]{:S(2)}) collective-permute-start(bf16[512,128]{1,0:T(8,128)(2,1)S(1)} %join.5), channel_id=1, source_target_pairs={{0,3},{1,2},{2,1},{3,0},{4,7},{5,6},{6,5},{7,4},{8,11},{9,10},{10,... | collective-permute-start | bytes 393224 | tf_op jit(solution)/shard_map/ppermute | solution.py:34
  31.4 5.8 %collective-permute-start.10 = (bf16[512,128]{1,0:T(8,128)(2,1)S(1)}, bf16[512,128]{1,0:T(8,128)(2,1)S(1)}, u32[]{:S(2)}, u32[]{:S(2)}) collective-permute-start(bf16[512,128]{1,0:T(8,128)(2,1)S(1)} %join.5), channel_id=1, source_target_pairs={{0,2},{1,3},{2,0},{3,1},{4,6},{5,7},{6,4},{7,5},{8,10},{9,11},{10,... | collective-permute-start | bytes 393224 | tf_op jit(solution)/shard_map/ppermute | solution.py:34
  32.9 5.0 %collective-permute-start.11 = (bf16[512,128]{1,0:T(8,128)(2,1)S(1)}, bf16[512,128]{1,0:T(8,128)(2,1)S(1)}, u32[]{:S(2)}, u32[]{:S(2)}) collective-permute-start(bf16[512,128]{1,0:T(8,128)(2,1)S(1)} %join.5), channel_id=1, source_target_pairs={{0,1},{1,0},{2,3},{3,2},{4,5},{5,4},{6,7},{7,6},{8,9},{9,8},{10,11... | collective-permute-start | bytes 393224 | tf_op jit(solution)/shard_map/ppermute | solution.py:34
  37.9 28.9 %slice-start.1 = ((s8[26214400]{0:T(1024)(128)(4,1)}), s8[4194304]{0:T(1024)(128)(4,1)S(1)}, s32[]{:S(2)}) async-start(s8[26214400]{0:T(1024)(128)(4,1)} %bitcast.13), calls=%async_computation.1 | async-start | bytes 8388608
  37.9 28.9 %slice-start.2 = ((s8[26214400]{0:T(1024)(128)(4,1)}), s8[4194304]{0:T(1024)(128)(4,1)S(1)}, s32[]{:S(2)}) async-start(s8[26214400]{0:T(1024)(128)(4,1)} %bitcast.13), calls=%async_computation.2 | async-start | bytes 8388608
  37.9 28.9 %slice-start.3 = ((s8[26214400]{0:T(1024)(128)(4,1)}), s8[4194304]{0:T(1024)(128)(4,1)S(1)}, s32[]{:S(2)}) async-start(s8[26214400]{0:T(1024)(128)(4,1)} %bitcast.13), calls=%async_computation.3 | async-start | bytes 8388608
  37.9 28.9 %slice-start.4 = ((s8[26214400]{0:T(1024)(128)(4,1)}), s8[4194304]{0:T(1024)(128)(4,1)S(1)}, s32[]{:S(2)}) async-start(s8[26214400]{0:T(1024)(128)(4,1)} %bitcast.13), calls=%async_computation.4 | async-start | bytes 8388608
  37.9 28.9 %slice-start.5 = ((s8[26214400]{0:T(1024)(128)(4,1)}), s8[4194304]{0:T(1024)(128)(4,1)S(1)}, s32[]{:S(2)}) async-start(s8[26214400]{0:T(1024)(128)(4,1)} %bitcast.13), calls=%async_computation.5 | async-start | bytes 8388608
  37.9 28.9 %slice-start.6 = ((s8[26214400]{0:T(1024)(128)(4,1)}), s8[1048576]{0:T(1024)(128)(4,1)S(1)}, s32[]{:S(2)}) async-start(s8[26214400]{0:T(1024)(128)(4,1)} %bitcast.13), calls=%async_computation.6 | async-start | bytes 2097152
  40.5 5.0 %collective-permute-start.15 = (bf16[128,512]{1,0:T(8,128)(2,1)S(1)}, bf16[128,512]{1,0:T(8,128)(2,1)S(1)}, u32[]{:S(2)}, u32[]{:S(2)}) collective-permute-start(bf16[128,512]{1,0:T(8,128)(2,1)S(1)} %get-tuple-element.18), channel_id=1, source_target_pairs={{0,1},{1,0},{2,3},{3,2},{4,5},{5,4},{6,7},{7,6},{8,9},{9,8},{10,11... | collective-permute-start | bytes 393224 | tf_op jit(solution)/shard_map/ppermute | solution.py:34
  41.4 6.0 %collective-permute-start.12 = (bf16[128,512]{1,0:T(8,128)(2,1)S(1)}, bf16[128,512]{1,0:T(8,128)(2,1)S(1)}, u32[]{:S(2)}, u32[]{:S(2)}) collective-permute-start(bf16[128,512]{1,0:T(8,128)(2,1)S(1)} %get-tuple-element.15), channel_id=1, source_target_pairs={{0,3},{1,2},{2,1},{3,0},{4,7},{5,6},{6,5},{7,4},{8,11},{9,10},{10,... | collective-permute-start | bytes 393224 | tf_op jit(solution)/shard_map/ppermute | solution.py:34
  42.8 5.9 %collective-permute-start.13 = (bf16[128,512]{1,0:T(8,128)(2,1)S(1)}, bf16[128,512]{1,0:T(8,128)(2,1)S(1)}, u32[]{:S(2)}, u32[]{:S(2)}) collective-permute-start(bf16[128,512]{1,0:T(8,128)(2,1)S(1)} %get-tuple-element.16), channel_id=1, source_target_pairs={{0,2},{1,3},{2,0},{3,1},{4,6},{5,7},{6,4},{7,5},{8,10},{9,11},{10,... | collective-permute-start | bytes 393224 | tf_op jit(solution)/shard_map/ppermute | solution.py:34
  44.1 1.3 %collective-permute-start.14 = (bf16[64,512]{1,0:T(8,128)(2,1)S(1)}, bf16[64,512]{1,0:T(8,128)(2,1)S(1)}, u32[]{:S(2)}, u32[]{:S(2)}) collective-permute-start(bf16[64,512]{1,0:T(8,128)(2,1)S(1)} %get-tuple-element.17), channel_id=1, source_target_pairs={{0,16},{16,0},{1,17},{17,1},{2,18},{18,2},{3,19},{19,3},{4,20},{20... | collective-permute-start | bytes 196616 | tf_op jit(solution)/shard_map/ppermute | solution.py:29
  48.8 6.9 %collective-permute-start.16 = (bf16[64,512]{1,0:T(8,128)(2,1)S(1)}, bf16[64,512]{1,0:T(8,128)(2,1)S(1)}, u32[]{:S(2)}, u32[]{:S(2)}) collective-permute-start(bf16[64,512]{1,0:T(8,128)(2,1)S(1)} %get-tuple-element.21), channel_id=1, source_target_pairs={{0,24},{1,25},{2,26},{3,27},{4,28},{5,29},{6,30},{7,31},{8,16},{9,... | collective-permute-start | bytes 196616 | tf_op jit(solution)/shard_map/ppermute | solution.py:23
  48.8 6.8 %collective-permute-start.17 = (bf16[64,512]{1,0:T(8,128)(2,1)S(1)}, bf16[64,512]{1,0:T(8,128)(2,1)S(1)}, u32[]{:S(2)}, u32[]{:S(2)}) collective-permute-start(bf16[64,512]{1,0:T(8,128)(2,1)S(1)} %get-tuple-element.21), channel_id=1, source_target_pairs={{0,16},{16,0},{1,17},{17,1},{2,18},{18,2},{3,19},{19,3},{4,20},{20... | collective-permute-start | bytes 196616 | tf_op jit(solution)/shard_map/ppermute | solution.py:29
  50.6 6.9 %collective-permute-start.18 = (bf16[64,512]{1,0:T(8,128)(2,1)S(1)}, bf16[64,512]{1,0:T(8,128)(2,1)S(1)}, u32[]{:S(2)}, u32[]{:S(2)}) collective-permute-start(bf16[64,512]{1,0:T(8,128)(2,1)S(1)} %get-tuple-element.22.a), channel_id=1, source_target_pairs={{0,8},{1,9},{2,10},{3,11},{4,12},{5,13},{6,14},{7,15},{8,0},{9,1},... | collective-permute-start | bytes 196616 | tf_op jit(solution)/shard_map/ppermute | solution.py:34
  57.6 5.6 %collective-permute-start.19 = (bf16[128,512]{1,0:T(8,128)(2,1)S(1)}, bf16[128,512]{1,0:T(8,128)(2,1)S(1)}, u32[]{:S(2)}, u32[]{:S(2)}) collective-permute-start(bf16[128,512]{1,0:T(8,128)(2,1)S(1)} %pair.1.own), channel_id=1, source_target_pairs={{0,4},{1,5},{2,6},{3,7},{4,0},{5,1},{6,2},{7,3},{8,12},{9,13},{10,... | collective-permute-start | bytes 393224 | tf_op jit(solution)/shard_map/ppermute | solution.py:34
  63.2 7.1 %collective-permute-start.22 = (bf16[128,512]{1,0:T(8,128)(2,1)S(1)}, bf16[128,512]{1,0:T(8,128)(2,1)S(1)}, u32[]{:S(2)}, u32[]{:S(2)}) collective-permute-start(bf16[128,512]{1,0:T(8,128)(2,1)S(1)} %finish.1.piece.r0), channel_id=1, source_target_pairs={{0,3},{1,2},{2,1},{3,0},{4,7},{5,6},{6,5},{7,4},{8,11},{9,10},{10,... | collective-permute-start | bytes 393224 | tf_op jit(solution)/shard_map/ppermute | solution.py:34
  64.8 7.2 %collective-permute-start.20 = (bf16[128,512]{1,0:T(8,128)(2,1)S(1)}, bf16[128,512]{1,0:T(8,128)(2,1)S(1)}, u32[]{:S(2)}, u32[]{:S(2)}) collective-permute-start(bf16[128,512]{1,0:T(8,128)(2,1)S(1)} %finish.1.piece.r0), channel_id=1, source_target_pairs={{0,1},{1,0},{2,3},{3,2},{4,5},{5,4},{6,7},{7,6},{8,9},{9,8},{10,11... | collective-permute-start | bytes 393224 | tf_op jit(solution)/shard_map/ppermute | solution.py:34
  66.0 6.0 %collective-permute-start.21 = (bf16[128,512]{1,0:T(8,128)(2,1)S(1)}, bf16[128,512]{1,0:T(8,128)(2,1)S(1)}, u32[]{:S(2)}, u32[]{:S(2)}) collective-permute-start(bf16[128,512]{1,0:T(8,128)(2,1)S(1)} %finish.1.piece.r0), channel_id=1, source_target_pairs={{0,2},{1,3},{2,0},{3,1},{4,6},{5,7},{6,4},{7,5},{8,10},{9,11},{10,... | collective-permute-start | bytes 393224 | tf_op jit(solution)/shard_map/ppermute | solution.py:34
  (8 other events, 99.1 us)
